TPU v7x, 32 devices: a whole 2x2x4 slice. The times are simulated.
32 devices in a mesh: dp: 4 (over z), tensor: 8 (over y, x, core).
Axes of the slice: x: 2, y: 2, z: 4, core: 2. Of those that a mesh axis runs over, the one named last changes fastest.
Arguments:
- block_input: bfloat16 [8192, 2048], P(('dp', 'tensor')), may hold values from -6 to 6
- segments: int32 [4, 2048], P('dp'), may hold values from 0 to 15, never falling along the last dimension, each value on 1 to 1024 neighbouring positions
- routes: int32 [8192, 8], P('dp'), may hold values from 0 to 15, all different within a row
- w_query: bfloat16 [2048, 2048], P(None, 'tensor'), as said below
- w_key: bfloat16 [2048, 2048], P(None, 'tensor'), as said below
- w_value: bfloat16 [2048, 2048], P(None, 'tensor'), may hold values from -0.125 to 0.125
- w_output: bfloat16 [2048, 2048], P('tensor'), may hold values from -0.5 to 0.5
- attn_gain: float32 [2048], replicated, may hold values from 0.5 to 1.5
- query_gain: float32 [2048], P('tensor'), may hold values from 0.5 to 1.5
- key_gain: float32 [2048], P('tensor'), may hold values from 0.5 to 1.5
- moe_gain: float32 [2048], replicated, may hold values from 0.5 to 1.5
- router: bfloat16 [2048, 16], replicated, may hold values from -0.06591797 to 0.06591797
- w_gate: bfloat16 [16, 2048, 1024], P(None, None, 'tensor'), may hold values from -0.125 to 0.125
- w_up: bfloat16 [16, 2048, 1024], P(None, None, 'tensor'), may hold values from -0.125 to 0.125
- w_down: bfloat16 [16, 1024, 2048], P(None, 'tensor'), may hold values from -1.5 to 1.5
- cotangent: bfloat16 [8192, 2048], P(('dp', 'tensor')), may hold values from -6 to 6
Outputs:
- block_output: bfloat16 [8192, 2048], P(('dp', 'tensor'))
- grad_input: float32 [8192, 2048], P(('dp', 'tensor'))
- grad_query: float32 [2048, 2048], P('dp', 'tensor')
- grad_key: float32 [2048, 2048], P('dp', 'tensor')
- grad_value: float32 [2048, 2048], P('dp', 'tensor')
- grad_output_proj: float32 [2048, 2048], P('tensor', 'dp')
- grad_attn_gain: float32 [2048], replicated
- grad_query_gain: float32 [2048], replicated
- grad_key_gain: float32 [2048], replicated
- grad_moe_gain: float32 [2048], replicated
- grad_router: float32 [2048, 16], replicated
- grad_gate: float32 [16, 2048, 1024], P(None, 'dp', 'tensor')
- grad_up: float32 [16, 2048, 1024], P(None, 'dp', 'tensor')
- grad_down: float32 [16, 1024, 2048], P(None, 'tensor', 'dp')
Inputs may be any that keep to these rules, and one draw needn't show every extreme that they name: `w_query`: entries are of order one over the root of 2048. `w_key`: entries are of order one over the root of 2048.
All inputs are finite; a program needn't handle non-finite values.
Results may differ from a plain program's by a relative error of at most 0.02.
Values may be sent and summed in bfloat16 or wider, within the bound.
A program may use at most 1.1875 GiB of HBM per device.

v0:
```python
import math

import jax
import jax.numpy as jnp
from jax import lax
from jax.sharding import PartitionSpec as P

HEAD_DIM = 128


EPS = 1e-05


def rms_scale(values):
    return lax.rsqrt(jnp.mean(values * values, axis=-1, keepdims=True) + EPS)


def doc_positions(segments):
    row_length = segments.shape[1]
    token_index = jnp.arange(row_length, dtype=jnp.int32)[None, :]
    previous = jnp.concatenate([segments[:, :1] - 1, segments[:, :-1]], axis=1)
    doc_start = jnp.where(segments != previous, token_index, jnp.zeros_like(token_index))
    return token_index - lax.cummax(doc_start, axis=1)


def route_slots(routes, capacity, experts):
    pair_count = routes.shape[0] * routes.shape[1]
    chosen = routes.reshape(pair_count)
    onehot = (chosen[:, None] == jnp.arange(experts, dtype=jnp.int32)[None, :]).astype(jnp.int32)
    earlier = jnp.cumsum(onehot, axis=0) - onehot
    position = jnp.sum(earlier * onehot, axis=1)
    kept_pairs = position < capacity
    slot_total = experts * capacity
    slot_index = jnp.where(kept_pairs, chosen * capacity + position, slot_total)
    pair_index = jnp.arange(pair_count, dtype=jnp.int32)
    pair_of_slot = jnp.zeros((slot_total,), jnp.int32).at[slot_index].set(pair_index, mode="drop")
    filled = (
        jnp.zeros((slot_total,), jnp.int32)
        .at[slot_index]
        .set(jnp.ones((pair_count,), jnp.int32), mode="drop")
    )
    return (slot_index, kept_pairs, pair_of_slot, filled)


def rope_tables(positions, head_dim):
    half_dim = head_dim // 2
    frequency = jnp.exp(
        jnp.arange(half_dim, dtype=jnp.float32) * (-2.0 * math.log(10000.0) / head_dim)
    )
    angles = positions.astype(jnp.float32)[:, None] * frequency[None, :]
    return (jnp.cos(angles), jnp.sin(angles))


def rotate(values, cosine, sine_table):
    half_dim = values.shape[-1] // 2
    leading, trailing = (values[..., :half_dim], values[..., half_dim:])
    cos_heads = cosine[:, None, :]
    sin_heads = sine_table[:, None, :]
    return jnp.concatenate(
        [leading * cos_heads - trailing * sin_heads, trailing * cos_heads + leading * sin_heads],
        axis=-1,
    )


def rotate_back(grad_values, cosine, sine_table):
    half_dim = grad_values.shape[-1] // 2
    leading, trailing = (grad_values[..., :half_dim], grad_values[..., half_dim:])
    cos_heads = cosine[:, None, :]
    sin_heads = sine_table[:, None, :]
    return jnp.concatenate(
        [leading * cos_heads + trailing * sin_heads, trailing * cos_heads - leading * sin_heads],
        axis=-1,
    )


def contract_rows(left_side, right_side):
    return lax.dot_general(
        left_side, right_side, (((0,), (0,)), ((), ())), preferred_element_type=jnp.float32
    )


def contract_cols(left_side, right_side):
    return lax.dot_general(
        left_side, right_side, (((1,), (1,)), ((), ())), preferred_element_type=jnp.float32
    )


def combine_slots(slot_table, slot_pairs, kept_float):
    total = jnp.zeros((slot_pairs.shape[0], slot_table.shape[1]), jnp.float32)
    for rank in range(slot_pairs.shape[1]):
        total = total + slot_table[slot_pairs[:, rank]] * kept_float[:, rank : rank + 1]
    return total


def per_device(
    block_input,
    segments,
    routes,
    w_query,
    w_key,
    w_value,
    w_output,
    attn_gain,
    query_gain,
    key_gain,
    moe_gain,
    router,
    w_gate,
    w_up,
    w_down,
    cotangent,
):
    own_rows = block_input.shape[0]
    model_width = block_input.shape[1]
    local_cols = w_query.shape[1]
    local_heads = local_cols // HEAD_DIM
    seq_count, seq_length = segments.shape
    token_count = seq_count * seq_length
    experts = router.shape[1]
    top_count = routes.shape[1]
    capacity = 5 * token_count * top_count // (4 * experts)
    rank_start = lax.axis_index("tensor") * own_rows
    col_start = lax.axis_index("tensor") * local_cols
    score_scale = 1.0 / math.sqrt(HEAD_DIM)
    block_rows = min(512, seq_length)
    block_count = token_count // block_rows
    full_input = lax.all_gather(block_input, "tensor", axis=0, tiled=True)
    input_wide = full_input.astype(jnp.float32)
    scale_one = rms_scale(input_wide)
    normed = (input_wide * scale_one * attn_gain).astype(jnp.bfloat16)
    query_raw = jnp.dot(normed, w_query, preferred_element_type=jnp.float32)
    key_raw = jnp.dot(normed, w_key, preferred_element_type=jnp.float32)
    value_low = jnp.dot(normed, w_value, preferred_element_type=jnp.float32).astype(jnp.bfloat16)
    query_sq, key_sq = lax.psum(
        (jnp.sum(query_raw * query_raw, axis=1), jnp.sum(key_raw * key_raw, axis=1)), "tensor"
    )
    query_rs = lax.rsqrt(query_sq / model_width + EPS)[:, None]
    key_rs = lax.rsqrt(key_sq / model_width + EPS)[:, None]
    query_unit = query_raw * query_rs
    key_unit = key_raw * key_rs
    positions = doc_positions(segments).reshape(token_count)
    cosine, sine_table = rope_tables(positions, HEAD_DIM)
    queries = rotate(
        (query_unit * query_gain).reshape(token_count, local_heads, HEAD_DIM), cosine, sine_table
    ).astype(jnp.bfloat16)
    keys_rot = rotate(
        (key_unit * key_gain).reshape(token_count, local_heads, HEAD_DIM), cosine, sine_table
    ).astype(jnp.bfloat16)
    value_heads = value_low.reshape(token_count, local_heads, HEAD_DIM)
    segment_ids = segments.reshape(token_count)

    def block_view(block_id):
        row_start = block_id * block_rows
        seq_start = row_start // seq_length * seq_length
        query_pos = row_start - seq_start + jnp.arange(block_rows, dtype=jnp.int32)
        key_pos = jnp.arange(seq_length, dtype=jnp.int32)
        query_seg = lax.dynamic_slice_in_dim(segment_ids, row_start, block_rows, 0)
        allowed = (query_seg[:, None] == segment_ids[None, :]) & (
            key_pos[None, :] <= query_pos[:, None]
        )
        query_block = lax.dynamic_slice_in_dim(queries, row_start, block_rows, 0)
        scores = (
            jnp.einsum("qhd,khd->hqk", query_block, keys_rot, preferred_element_type=jnp.float32)
            * score_scale
        )
        scores = jnp.where(allowed[None, :, :], scores, -1e30)
        return (row_start, seq_start, query_block, keys_rot, value_heads, scores)

    def attend(block_id):
        row_start, seq_start, query_block, key_block, value_block, scores = block_view(block_id)
        top_score = jnp.max(scores, axis=-1, keepdims=True)
        exponent = jnp.exp(scores - top_score)
        row_total = jnp.sum(exponent, axis=-1, keepdims=True)
        weights = (exponent / row_total).astype(jnp.bfloat16)
        attended = jnp.einsum(
            "hqk,khd->qhd", weights, value_block, preferred_element_type=jnp.float32
        )
        return (attended, top_score[..., 0] + jnp.log(row_total[..., 0]))

    attended_all, log_sums = lax.map(attend, jnp.arange(block_count, dtype=jnp.int32))
    attn_low = attended_all.reshape(token_count, local_cols).astype(jnp.bfloat16)
    attn_total = lax.psum(jnp.dot(attn_low, w_output, preferred_element_type=jnp.float32), "tensor")
    residual_wide = input_wide + attn_total
    moe_in = (residual_wide * rms_scale(residual_wide) * moe_gain).astype(jnp.bfloat16)
    residual = lax.dynamic_slice_in_dim(residual_wide, rank_start, own_rows, 0)
    scale_two = rms_scale(residual)
    logits = jnp.dot(moe_in, router, preferred_element_type=jnp.float32)
    router_probs = jax.nn.softmax(logits, axis=-1)
    gate_values = jnp.take_along_axis(router_probs, routes, axis=1)
    slot_index, kept_pairs, pair_of_slot, filled = route_slots(routes, capacity, experts)
    live_slots = filled.astype(jnp.float32).reshape(experts, capacity)
    gate_slot = (
        gate_values.reshape(token_count * top_count)[pair_of_slot].reshape(experts, capacity)
        * live_slots
    )
    token_of_slot = (pair_of_slot // top_count).reshape(experts, capacity)
    live_low = live_slots.astype(jnp.bfloat16)
    slot_safe = jnp.minimum(slot_index, experts * capacity - 1)
    slot_pairs = slot_safe.reshape(token_count, top_count)
    kept_float = kept_pairs.astype(jnp.float32).reshape(token_count, top_count)
    cotangent_wide = lax.all_gather(cotangent, "tensor", axis=0, tiled=True)

    def expert_forward(carry_none, pieces):
        rows_of, live_of, gate_of, gate_w, up_w, down_w = pieces
        slot_rows = moe_in[rows_of] * live_of[:, None]
        gate_pre = jnp.dot(slot_rows, gate_w, preferred_element_type=jnp.float32)
        up_pre = jnp.dot(slot_rows, up_w, preferred_element_type=jnp.float32)
        activated = (jax.nn.silu(gate_pre) * up_pre).astype(jnp.bfloat16)
        expert_out = jnp.dot(activated, down_w, preferred_element_type=jnp.float32)
        gate_dot = jnp.sum(cotangent_wide[rows_of].astype(jnp.float32) * expert_out, axis=1)
        return (carry_none, (gate_of[:, None] * expert_out, gate_pre, up_pre, activated, gate_dot))

    unused_carry, kept_state = lax.scan(
        expert_forward, None, (token_of_slot, live_low, gate_slot, w_gate, w_up, w_down)
    )
    gated_out, gate_keep, up_keep, act_keep, dot_parts = kept_state
    moe_part = combine_slots(
        gated_out.reshape(experts * capacity, model_width), slot_pairs, kept_float
    )
    moe_own_out = lax.psum_scatter(
        moe_part.astype(jnp.bfloat16), "tensor", scatter_dimension=0, tiled=True
    ).astype(jnp.float32)
    block_output = (residual + moe_own_out).astype(jnp.bfloat16)
    slot_grads = lax.psum(dot_parts.astype(jnp.bfloat16), "tensor").astype(jnp.float32)
    pair_grads = (
        slot_grads.reshape(experts * capacity)[slot_safe] * kept_pairs.astype(jnp.float32)
    ).reshape(token_count, top_count)
    expert_ids = jnp.arange(experts, dtype=jnp.int32)
    prob_grads = jnp.sum(
        pair_grads[:, :, None]
        * (routes[:, :, None] == expert_ids[None, None, :]).astype(jnp.float32),
        axis=1,
    )
    logit_grads = (
        router_probs * (prob_grads - jnp.sum(router_probs * prob_grads, axis=1, keepdims=True))
    ).astype(jnp.bfloat16)
    own_logit = lax.dynamic_slice_in_dim(logit_grads, rank_start, own_rows, 0)
    own_moe_in = lax.dynamic_slice_in_dim(moe_in, rank_start, own_rows, 0)
    router_grad = contract_rows(own_moe_in, own_logit)
    router_back = contract_cols(own_logit, router)

    def expert_backward(carry_none, pieces):
        rows_of, live_of, gate_of, gate_w, up_w, down_w, gate_pre, up_pre, activated = pieces
        slot_rows = moe_in[rows_of] * live_of[:, None]
        out_grad = (gate_of[:, None] * cotangent_wide[rows_of].astype(jnp.float32)).astype(
            jnp.bfloat16
        )
        act_grad = contract_cols(out_grad, down_w)
        down_grad = contract_rows(activated, out_grad)
        sigmoid_val = jax.nn.sigmoid(gate_pre)
        silu_val = gate_pre * sigmoid_val
        gate_grad = (
            act_grad * up_pre * sigmoid_val * (1.0 + gate_pre * (1.0 - sigmoid_val))
        ).astype(jnp.bfloat16)
        up_grad = (act_grad * silu_val).astype(jnp.bfloat16)
        gate_w_grad = contract_rows(slot_rows, gate_grad)
        up_w_grad = contract_rows(slot_rows, up_grad)
        row_grads = contract_cols(gate_grad, gate_w) + contract_cols(up_grad, up_w)
        return (carry_none, (row_grads, gate_w_grad, up_w_grad, down_grad))

    unused_back, expert_grads = lax.scan(
        expert_backward,
        None,
        (token_of_slot, live_low, gate_slot, w_gate, w_up, w_down, gate_keep, up_keep, act_keep),
    )
    slot_row_grads, gate_w_grads, up_w_grads, down_w_grads = expert_grads
    back_part = combine_slots(
        slot_row_grads.reshape(experts * capacity, model_width), slot_pairs, kept_float
    )
    moe_grad = lax.psum_scatter(back_part, "tensor", scatter_dimension=0, tiled=True) + router_back
    unit_two = residual * scale_two
    moe_gain_grad = jnp.sum(moe_grad * unit_two, axis=0)
    scaled_two = moe_grad * moe_gain
    residual_grad = cotangent.astype(jnp.float32) + scale_two * (
        scaled_two - unit_two * jnp.mean(scaled_two * unit_two, axis=1, keepdims=True)
    )
    residual_wide_grad = lax.all_gather(
        residual_grad.astype(jnp.bfloat16), "tensor", axis=0, tiled=True
    )
    output_grad = contract_rows(attn_low, residual_wide_grad)
    heads_grad = (
        contract_cols(residual_wide_grad, w_output)
        .astype(jnp.bfloat16)
        .reshape(token_count, local_heads, HEAD_DIM)
    )

    def attend_back(accum_pair, block_id):
        key_acc, value_acc = accum_pair
        row_start, seq_start, query_block, key_block, value_block, scores = block_view(block_id)
        probs_block = jnp.exp(scores - log_sums[block_id][:, :, None])
        out_block = lax.dynamic_slice_in_dim(heads_grad, row_start, block_rows, 0)
        prob_grad = jnp.einsum(
            "qhd,khd->hqk", out_block, value_block, preferred_element_type=jnp.float32
        )
        score_grad = (
            probs_block * (prob_grad - jnp.sum(probs_block * prob_grad, axis=-1, keepdims=True))
        ).astype(jnp.bfloat16)
        query_grad = (
            jnp.einsum("hqk,khd->qhd", score_grad, key_block, preferred_element_type=jnp.float32)
            * score_scale
        )
        key_part = (
            jnp.einsum("hqk,qhd->khd", score_grad, query_block, preferred_element_type=jnp.float32)
            * score_scale
        )
        value_part = jnp.einsum(
            "hqk,qhd->khd",
            probs_block.astype(jnp.bfloat16),
            out_block,
            preferred_element_type=jnp.float32,
        )
        key_acc = key_acc + key_part
        value_acc = value_acc + value_part
        return ((key_acc, value_acc), query_grad)

    zero_heads = jnp.zeros((token_count, local_heads, HEAD_DIM), jnp.float32)
    key_value_grads, query_blocks = lax.scan(
        attend_back, (zero_heads, zero_heads), jnp.arange(block_count, dtype=jnp.int32)
    )
    key_rot_grad, value_grad = key_value_grads
    query_rot_grad = query_blocks.reshape(token_count, local_heads, HEAD_DIM)
    query_norm_grad = rotate_back(query_rot_grad, cosine, sine_table).reshape(
        token_count, local_cols
    )
    key_norm_grad = rotate_back(key_rot_grad, cosine, sine_table).reshape(token_count, local_cols)
    query_gain_grad = jnp.sum(query_norm_grad * query_unit, axis=0)
    key_gain_grad = jnp.sum(key_norm_grad * key_unit, axis=0)
    query_scaled = query_norm_grad * query_gain
    key_scaled = key_norm_grad * key_gain
    query_dot, key_dot = lax.psum(
        (jnp.sum(query_scaled * query_unit, axis=1), jnp.sum(key_scaled * key_unit, axis=1)),
        "tensor",
    )
    query_grad_low = (
        query_rs * (query_scaled - query_unit * (query_dot / model_width)[:, None])
    ).astype(jnp.bfloat16)
    key_grad_low = (key_rs * (key_scaled - key_unit * (key_dot / model_width)[:, None])).astype(
        jnp.bfloat16
    )
    value_grad_low = value_grad.reshape(token_count, local_cols).astype(jnp.bfloat16)
    query_w_grad = contract_rows(normed, query_grad_low)
    key_w_grad = contract_rows(normed, key_grad_low)
    value_w_grad = contract_rows(normed, value_grad_low)
    total_back = contract_cols(query_grad_low, w_query)
    total_back = total_back + contract_cols(key_grad_low, w_key)
    normed_grad = lax.psum_scatter(
        (total_back + contract_cols(value_grad_low, w_value)).astype(jnp.bfloat16),
        "tensor",
        scatter_dimension=0,
        tiled=True,
    ).astype(jnp.float32)
    input_own = block_input.astype(jnp.float32)
    scale_own = lax.dynamic_slice_in_dim(scale_one, rank_start, own_rows, 0)
    unit_one = input_own * scale_own
    attn_gain_grad = jnp.sum(normed_grad * unit_one, axis=0)
    scaled_one = normed_grad * attn_gain
    grad_input = residual_grad + scale_own * (
        scaled_one - unit_one * jnp.mean(scaled_one * unit_one, axis=1, keepdims=True)
    )
    reduced = (
        lax.psum_scatter(
            query_w_grad.astype(jnp.bfloat16), "dp", scatter_dimension=0, tiled=True
        ).astype(jnp.float32),
        lax.psum_scatter(
            key_w_grad.astype(jnp.bfloat16), "dp", scatter_dimension=0, tiled=True
        ).astype(jnp.float32),
        lax.psum_scatter(
            value_w_grad.astype(jnp.bfloat16), "dp", scatter_dimension=0, tiled=True
        ).astype(jnp.float32),
        lax.psum_scatter(
            output_grad.astype(jnp.bfloat16), "dp", scatter_dimension=1, tiled=True
        ).astype(jnp.float32),
        lax.psum_scatter(
            gate_w_grads.astype(jnp.bfloat16), "dp", scatter_dimension=1, tiled=True
        ).astype(jnp.float32),
        lax.psum_scatter(
            up_w_grads.astype(jnp.bfloat16), "dp", scatter_dimension=1, tiled=True
        ).astype(jnp.float32),
        lax.psum_scatter(
            down_w_grads.astype(jnp.bfloat16), "dp", scatter_dimension=2, tiled=True
        ).astype(jnp.float32),
    )
    query_gain_full = lax.dynamic_update_slice_in_dim(
        jnp.zeros((model_width,), jnp.float32), query_gain_grad, col_start, 0
    )
    key_gain_full = lax.dynamic_update_slice_in_dim(
        jnp.zeros((model_width,), jnp.float32), key_gain_grad, col_start, 0
    )
    small_sums = lax.psum(
        (attn_gain_grad, moe_gain_grad, router_grad, query_gain_full, key_gain_full),
        ("dp", "tensor"),
    )
    return (
        block_output,
        grad_input,
        reduced[0],
        reduced[1],
        reduced[2],
        reduced[3],
        small_sums[0],
        small_sums[3],
        small_sums[4],
        small_sums[1],
        small_sums[2],
        reduced[4],
        reduced[5],
        reduced[6],
    )


def solution(mesh):
    placed = (
        P(("dp", "tensor"), None),
        P("dp", None),
        P("dp", None),
        P(None, "tensor"),
        P(None, "tensor"),
        P(None, "tensor"),
        P("tensor", None),
        P(),
        P("tensor"),
        P("tensor"),
        P(),
        P(),
        P(None, None, "tensor"),
        P(None, None, "tensor"),
        P(None, "tensor", None),
        P(("dp", "tensor"), None),
    )
    return jax.shard_map(
        per_device,
        mesh=mesh,
        in_specs=placed,
        out_specs=(
            P(("dp", "tensor"), None),
            P(("dp", "tensor"), None),
            P("dp", "tensor"),
            P("dp", "tensor"),
            P("dp", "tensor"),
            P("tensor", "dp"),
            P(),
            P(),
            P(),
            P(),
            P(),
            P(None, "dp", "tensor"),
            P(None, "dp", "tensor"),
            P(None, "tensor", "dp"),
        ),
        check_vma=False,
    )
```

profile of v0, /device:TPU:0, one launch (start us, length us, event | category | flops | bytes accessed | tf_op | source)
XLA Modules:
  0.0 4113.1 jit_solution(16178546317519512101)
XLA Ops:
  16.8 50.3 %all-gather.4.cloned.1.call-done = bf16[2048,2048]{1,0:T(8,128)(2,1)} async-done(((bf16[256,2048]{1,0:T(8,128)(2,1)}), bf16[2048,2048]{1,0:T(8,128)(2,1)}) %all-gather.4.cloned.1.call-update) | async-done | bytes 8388624 | tf_op jit(solution)/shard_map/all_gather | solution.py:127
  153.9 48.6 %while.65 = (s32[]{:T(128)}, bf16[4,512,2,128]{3,1,2,0:T(8,128)(2,1)}, f32[4,2,512]{2,1,0:T(2,128)}, s32[4]{0:T(128)S(1)}, s32[2048]{0:T(1024)S(1)}, /*index=5*/...) while((s32[]{:T(128)}, ...), condition=%wide.region_10.11_spmd, body=%wide.region_7.10_spmd.sunk | while | flops 1102052864 | bytes 40683976 | solution.py:180
  227.0 60.4 %scatter_custom_fusion.1 = s32[20480]{0:T(1024)S(1)} fusion(s32[16384]{0:T(1024)S(1)} %bitcast.329, s32[16384]{0:T(1024)S(1)} %broadcast.493, s32[]{:T(128)} %constant.281.clone.1), kind=kCustom, calls=%fused_computation.273 | custom fusion | bytes 81924 | tf_op jit(solution)/shard_map/scatter | solution.py:40
  287.4 60.5 %scatter_custom_fusion = s32[20480]{0:T(1024)S(1)} fusion(s32[16384]{0:T(1024)S(1)} %bitcast.330, s32[16384]{0:T(1024)S(1)} %iota.76, s32[]{:T(128)} %constant.281.clone.1), kind=kCustom, calls=%fused_computation.275 | custom fusion | bytes 81924 | tf_op jit(solution)/shard_map/scatter | solution.py:36
  361.4 72.6 %all-reduce.6.cloned.1.call-done = f32[2048,2048]{1,0:T(8,128)} async-done(((f32[2048,2048]{1,0:T(8,128)}), f32[2048,2048]{1,0:T(8,128)}) %all-reduce.6.cloned.1.call-update) | async-done | bytes 16777232 | tf_op jit(solution)/shard_map/psum | solution.py:182
  453.3 130.6 %gather_fusion.22 = f32[16384]{0:T(1024)S(1)} fusion(f32[2048,16]{0,1:T(8,128)S(1)} %fusion.130, s32[16384]{0:T(1024)S(1)} %reshape.732), kind=kCustom, calls=%fused_computation.22 | custom fusion | bytes 262144 | tf_op jit(solution)/shard_map/jit(take_along_axis)/gather | solution.py:189
  585.7 113.0 %gather_fusion.4 = f32[20480]{0:T(1024)S(1)} fusion(f32[16384]{0:T(1024)S(1)} %select_n.185, s32[20480]{0:T(1024)S(1)} %copy-done.38), kind=kCustom, calls=%fused_computation.4 | custom fusion | bytes 245760 | tf_op jit(solution)/shard_map/gather | solution.py:193
  698.8 51.3 %broadcast.464.clone = f32[16,1280,2048]{2,1,0:T(8,128)} broadcast(f32[]{:T(128)} %constant.282.clone.1), dimensions={} | broadcast | bytes 167772160 | tf_op jit(solution)/shard_map/broadcast.41
  750.1 850.5 %while.66 = (s32[]{:T(128)}, f32[16,1280,2048]{2,1,0:T(8,128)}, f32[16,1280,128]{2,1,0:T(8,128)}, f32[16,1280,128]{2,1,0:T(8,128)}, bf16[16,1280,128]{2,1,0:T(8,...) while((s32[]{:T(128)}, f32[16,1280,2048]{2,1,0:T(8,128)}, ...), condition=%wide.region_22.23_spmd, body=%wide.region_20.22_spmd.sunk | while | flops 2029982208 | bytes 95692488 | solution.py:213
  1600.6 51.3 %broadcast.464 = f32[16,1280,2048]{2,1,0:T(8,128)} broadcast(f32[]{:T(128)} %constant.282.clone.1), dimensions={} | broadcast | bytes 167772160 | tf_op jit(solution)/shard_map/broadcast.41
  1651.9 881.2 %while.67 = (s32[]{:T(128)}, f32[16,1280,2048]{2,1,0:T(8,128)}, bf16[16,2048,128]{2,1,0:T(8,128)(2,1)}, bf16[16,2048,128]{2,1,0:T(8,128)(2,1)}, bf16[16,128,2048...) while((s32[]{:T(128)}, f32[16,1280,2048]{2,1,0:T(8,128)}, ...), condition=%wide.region_26.27_spmd, body=%wide.region_25.26_spmd.sunk | while | flops 4052260608 | bytes 123734248 | solution.py:261
  2533.1 51.4 %gather_fusion.20 = f32[2048,2048]{1,0:T(8,128)} fusion(f32[20480,2048]{1,0:T(8,128)} %bitcast.38, s32[2048]{0:T(1024)S(1)} %copy-done.58), kind=kCustom, calls=%fused_computation.20 | custom fusion | bytes 33562624 | tf_op jit(solution)/shard_map/gather | solution.py:91
  2584.5 51.9 %gather_fusion.19 = f32[2048,2048]{1,0:T(8,128)} fusion(f32[20480,2048]{1,0:T(8,128)} %bitcast.38, s32[2048]{0:T(1024)S(1)} %copy-done.56), kind=kCustom, calls=%fused_computation.19 | custom fusion | bytes 33562624 | tf_op jit(solution)/shard_map/gather | solution.py:91
  2636.4 51.5 %gather_fusion.18 = f32[2048,2048]{1,0:T(8,128)} fusion(f32[20480,2048]{1,0:T(8,128)} %bitcast.38, s32[2048]{0:T(1024)S(1)} %copy-done.62), kind=kCustom, calls=%fused_computation.18 | custom fusion | bytes 33562624 | tf_op jit(solution)/shard_map/gather | solution.py:91
  2687.9 51.7 %gather_fusion.17 = f32[2048,2048]{1,0:T(8,128)} fusion(f32[20480,2048]{1,0:T(8,128)} %bitcast.38, s32[2048]{0:T(1024)S(1)} %copy-done.60), kind=kCustom, calls=%fused_computation.17 | custom fusion | bytes 33562624 | tf_op jit(solution)/shard_map/gather | solution.py:91
  2739.5 51.8 %gather_fusion.16 = f32[2048,2048]{1,0:T(8,128)} fusion(f32[20480,2048]{1,0:T(8,128)} %bitcast.38, s32[2048]{0:T(1024)S(1)} %copy-done.66), kind=kCustom, calls=%fused_computation.16 | custom fusion | bytes 33562624 | tf_op jit(solution)/shard_map/gather | solution.py:91
  2791.3 52.2 %gather_fusion.15 = f32[2048,2048]{1,0:T(8,128)} fusion(f32[20480,2048]{1,0:T(8,128)} %bitcast.38, s32[2048]{0:T(1024)S(1)} %copy-done.64), kind=kCustom, calls=%fused_computation.15 | custom fusion | bytes 33562624 | tf_op jit(solution)/shard_map/gather | solution.py:91
  2843.5 56.8 %gather_fusion.14 = f32[2048,2048]{1,0:T(8,128)} fusion(f32[20480,2048]{1,0:T(8,128)} %bitcast.38, s32[2048]{0:T(1024)S(1)} %copy-done.54), kind=kCustom, calls=%fused_computation.14 | custom fusion | bytes 33562624 | tf_op jit(solution)/shard_map/gather | solution.py:91
  2900.4 80.6 %gather_fusion.13 = f32[2048,2048]{1,0:T(8,128)} fusion(f32[20480,2048]{1,0:T(8,128)} %bitcast.38, s32[2048]{0:T(1024)S(1)} %copy-done.52), kind=kCustom, calls=%fused_computation.13 | custom fusion | bytes 33562624 | tf_op jit(solution)/shard_map/gather | solution.py:91
  2981.0 47.7 %multiply_add_fusion = f32[2048,2048]{1,0:T(8,128)} fusion(f32[2048,2048]{1,0:T(8,128)} %gather_fusion.20, f32[2048,2048]{1,0:T(8,128)} %gather_fusion.19, f32[2048,2048]{1,0:T(8,128)} %gather_fusion.18, f32[2048,2048]{1,0:T(8,128)} %gather_fusion.17, f32[2048,2048]{1,0:T(8,128)} %gather_fusion.16, f32[2048,2048]{1,0:T(8,128)} %gather_fusion.15, ...), kind=kLoop, calls=%fused_computation.152 | loop fusion | flops 62914560 | bytes 151060480 | tf_op jit(solution)/shard_map/add | solution.py:91
  3053.8 90.5 %gather_fusion.21 = f32[16384]{0:T(1024)S(1)} fusion(f32[20480]{0:T(1024)S(1)} %reshape.551, s32[16384]{0:T(1024)S(1)} %broadcast_clamp_fusion), kind=kCustom, calls=%fused_computation.21 | custom fusion | bytes 196608 | tf_op jit(solution)/shard_map/gather | solution.py:226
  3163.2 52.4 %all-gather.8.cloned.1.call-done = bf16[2048,2048]{1,0:T(8,128)(2,1)} async-done(((bf16[256,2048]{1,0:T(8,128)(2,1)}), bf16[2048,2048]{1,0:T(8,128)(2,1)}) %all-gather.8.cloned.1.call-update) | async-done | bytes 8388624 | tf_op jit(solution)/shard_map/all_gather | solution.py:277
  3222.6 97.5 %while.68 = (s32[]{:T(128)}, f32[2048,2,128]{0,2,1:T(8,128)}, f32[2048,2,128]{0,2,1:T(8,128)}, f32[4,512,2,128]{3,1,0,2:T(8,128)}, s32[4]{0:T(128)S(1)}, /*index...) while((s32[]{:T(128)}, f32[2048,2,128]{0,2,1:T(8,128)}, ...), condition=%wide.region_34.35_spmd.clone, body=%wide.region_32.34_spmd.clone.sunk | while | flops 2721709568 | bytes 84457992 | solution.py:317
  3439.0 50.5 %gather_fusion.12 = f32[2048,2048]{1,0:T(8,128)} fusion(f32[20480,2048]{1,0:T(8,128)} %bitcast.37, s32[2048]{0:T(1024)S(1)} %copy-done.59), kind=kCustom, calls=%fused_computation.12 | custom fusion | bytes 33562624 | tf_op jit(solution)/shard_map/gather | solution.py:91
  3489.6 50.8 %gather_fusion.11 = f32[2048,2048]{1,0:T(8,128)} fusion(f32[20480,2048]{1,0:T(8,128)} %bitcast.37, s32[2048]{0:T(1024)S(1)} %copy-done.57), kind=kCustom, calls=%fused_computation.11 | custom fusion | bytes 33562624 | tf_op jit(solution)/shard_map/gather | solution.py:91
  3540.4 50.6 %gather_fusion.10 = f32[2048,2048]{1,0:T(8,128)} fusion(f32[20480,2048]{1,0:T(8,128)} %bitcast.37, s32[2048]{0:T(1024)S(1)} %copy-done.63), kind=kCustom, calls=%fused_computation.10 | custom fusion | bytes 33562624 | tf_op jit(solution)/shard_map/gather | solution.py:91
  3591.0 50.5 %gather_fusion.9 = f32[2048,2048]{1,0:T(8,128)} fusion(f32[20480,2048]{1,0:T(8,128)} %bitcast.37, s32[2048]{0:T(1024)S(1)} %copy-done.61), kind=kCustom, calls=%fused_computation.9 | custom fusion | bytes 33562624 | tf_op jit(solution)/shard_map/gather | solution.py:91
  3641.6 50.6 %gather_fusion.8 = f32[2048,2048]{1,0:T(8,128)} fusion(f32[20480,2048]{1,0:T(8,128)} %bitcast.37, s32[2048]{0:T(1024)S(1)} %copy-done.67), kind=kCustom, calls=%fused_computation.8 | custom fusion | bytes 33562624 | tf_op jit(solution)/shard_map/gather | solution.py:91
  3692.2 50.6 %gather_fusion.7 = f32[2048,2048]{1,0:T(8,128)} fusion(f32[20480,2048]{1,0:T(8,128)} %bitcast.37, s32[2048]{0:T(1024)S(1)} %copy-done.65), kind=kCustom, calls=%fused_computation.7 | custom fusion | bytes 33562624 | tf_op jit(solution)/shard_map/gather | solution.py:91
  3742.8 52.7 %gather_fusion.6 = f32[2048,2048]{1,0:T(8,128)} fusion(f32[20480,2048]{1,0:T(8,128)} %bitcast.37, s32[2048]{0:T(1024)S(1)} %copy-done.55), kind=kCustom, calls=%fused_computation.6 | custom fusion | bytes 33562624 | tf_op jit(solution)/shard_map/gather | solution.py:91
  3795.6 64.6 %gather_fusion.5 = f32[2048,2048]{1,0:T(8,128)} fusion(f32[20480,2048]{1,0:T(8,128)} %bitcast.37, s32[2048]{0:T(1024)S(1)} %copy-done.53), kind=kCustom, calls=%fused_computation.5 | custom fusion | bytes 33562624 | tf_op jit(solution)/shard_map/gather | solution.py:91
  4022.0 82.8 %all-reduce.8.cloned.1.call-done = f32[2048,16]{0,1:T(8,128)} async-done(((f32[2048,16]{0,1:T(8,128)}), f32[2048,16]{0,1:T(8,128)}) %all-reduce.8.cloned.1.call-update) | async-done | bytes 131088 | tf_op jit(solution)/shard_map/psum | solution.py:389
  (977 shorter events, 2348.9 us)
Async XLA Ops:
  7.2 89.3 %copy-start = (bf16[2048,256]{1,0:T(8,128)(2,1)S(1)}, bf16[2048,256]{1,0:T(8,128)(2,1)}, u32[]{:S(2)}) copy-start(bf16[2048,256]{1,0:T(8,128)(2,1)} %param.27) | copy-start | bytes 3145732
  7.2 59.9 %all-gather.4.cloned.1.call-start = ((), (), s32[]{:S(2)}) async-start(), calls=%async_computation.10 | async-start | bytes 9437184 | tf_op jit(solution)/shard_map/all_gather | solution.py:127
  7.9 426.0 %all-reduce.6.cloned.1.call-start = ((), (), s32[]{:S(2)}) async-start(), calls=%async_computation.11 | async-start | bytes 33554432 | tf_op jit(solution)/shard_map/psum | solution.py:182
  16.8 130.0 %copy-start.18 = (f32[2048,64]{1,0:T(8,128)}, f32[2048,64]{1,0:T(8,128)S(1)}, u32[]{:S(2)}) copy-start(f32[2048,64]{1,0:T(8,128)S(1)} %get-tuple-element.773) | copy-start | bytes 1572868
  215.9 482.9 %all-gather.6.cloned.1.call-start = ((), (), s32[]{:S(2)}) async-start(), calls=%async_computation.12 | async-start | bytes 9437184 | tf_op jit(solution)/shard_map/all_gather | solution.py:201
  216.7 2936.0 %reduce-scatter.13.cloned.1.call-start = ((), (), s32[]{:S(2)}) async-start(), calls=%async_computation.14 | async-start | bytes 18874368 | tf_op jit(solution)/shard_map/reduce_scatter | solution.py:270
  221.5 135.1 %copy-start.14 = (s32[2048,8]{1,0:T(8,128)}, s32[2048,8]{1,0:T(8,128)S(1)}, u32[]{:S(2)}) copy-start(s32[2048,8]{1,0:T(8,128)S(1)} %reduce_sum.197) | copy-start | bytes 196612
  361.4 81.7 %copy-start.46 = (f32[2048]{0:T(1024)S(1)}, f32[2048]{0:T(1024)}, u32[]{:S(2)}) copy-start(f32[2048]{0:T(1024)} %param.34) | copy-start | bytes 24580
  453.3 130.6 %copy-start.1 = (f32[2048,16]{0,1:T(8,128)}, f32[2048,16]{0,1:T(8,128)S(1)}, u32[]{:S(2)}) copy-start(f32[2048,16]{0,1:T(8,128)S(1)} %fusion.130) | copy-start | bytes 393220
  453.3 131.5 %copy-start.31 = (s32[2048,8]{0,1:T(8,128)S(1)}, s32[2048,8]{0,1:T(8,128)}, u32[]{:S(2)}) copy-start(s32[2048,8]{0,1:T(8,128)} %param.26) | copy-start | bytes 196612
  453.3 132.3 %copy-start.38 = (s32[20480]{0:T(1024)S(1)}, s32[20480]{0:T(1024)}, u32[]{:S(2)}) copy-start(s32[20480]{0:T(1024)} %get-tuple-element.772) | copy-start | bytes 245764
  585.7 113.1 %copy-start.36 = (s32[20480]{0:T(1024)S(1)}, s32[20480]{0:T(1024)}, u32[]{:S(2)}) copy-start(s32[20480]{0:T(1024)} %copy-done.35) | copy-start | bytes 245764
  1651.9 881.2 %copy-start.58 = (s32[2048]{0:T(1024)S(1)}, s32[2048]{0:T(1024)}, u32[]{:S(2)}) copy-start(s32[2048]{0:T(1024)} %get-tuple-element.784) | copy-start | bytes 24580
  2900.3 80.6 %copy-start.69 = (f32[2048]{0:T(1024)S(1)}, f32[2048]{0:T(1024)}, u32[]{:S(2)}) copy-start(f32[2048]{0:T(1024)} %get-tuple-element.608) | copy-start | bytes 24580
  2900.3 80.6 %copy-start.71 = (f32[2048]{0:T(1024)S(1)}, f32[2048]{0:T(1024)}, u32[]{:S(2)}) copy-start(f32[2048]{0:T(1024)} %get-tuple-element.609) | copy-start | bytes 24580
  2900.3 80.6 %copy-start.73 = (f32[2048]{0:T(1024)S(1)}, f32[2048]{0:T(1024)}, u32[]{:S(2)}) copy-start(f32[2048]{0:T(1024)} %get-tuple-element.610) | copy-start | bytes 24580
  2900.3 80.6 %copy-start.75 = (f32[2048]{0:T(1024)S(1)}, f32[2048]{0:T(1024)}, u32[]{:S(2)}) copy-start(f32[2048]{0:T(1024)} %get-tuple-element.611) | copy-start | bytes 24580
  3028.8 186.8 %all-gather.8.cloned.1.call-start = ((), (), s32[]{:S(2)}) async-start(), calls=%async_computation.15 | async-start | bytes 9437184 | tf_op jit(solution)/shard_map/all_gather | solution.py:277
  3053.8 92.2 %copy-start.15 = (s32[2048,8]{1,0:T(8,128)S(1)}, s32[2048,8]{1,0:T(8,128)}, u32[]{:S(2)}) copy-start(s32[2048,8]{1,0:T(8,128)} %copy-done.14) | copy-start | bytes 196612
  3053.8 96.0 %copy-start.32 = (s32[2048,8]{0,1:T(8,128)S(1)}, s32[2048,8]{0,1:T(8,128)}, u32[]{:S(2)}) copy-start(s32[2048,8]{0,1:T(8,128)} %param.26) | copy-start | bytes 196612
  3053.8 96.1 %copy-start.25 = (f32[2048,16]{0,1:T(8,128)S(1)}, f32[2048,16]{0,1:T(8,128)}, u32[]{:S(2)}) copy-start(f32[2048,16]{0,1:T(8,128)} %copy-done.24) | copy-start | bytes 393220
  3053.8 98.9 %copy-start.40 = (bf16[2048,16]{0,1:T(8,128)(2,1)S(1)}, bf16[2048,16]{0,1:T(8,128)(2,1)}, u32[]{:S(2)}) copy-start(bf16[2048,16]{0,1:T(8,128)(2,1)} %param.35) | copy-start | bytes 196612
  3161.0 747.3 %reduce-scatter.27.cloned.1.call-start = ((), (), s32[]{:S(2)}) async-start(), calls=%async_computation.23 | async-start | bytes 10485760 | tf_op jit(solution)/shard_map/reduce_scatter | solution.py:376
  3161.6 750.8 %reduce-scatter.25.cloned.1.call-start = ((), (), s32[]{:S(2)}) async-start(), calls=%async_computation.22 | async-start | bytes 10485760 | tf_op jit(solution)/shard_map/reduce_scatter | solution.py:373
  3162.3 755.0 %reduce-scatter.29.cloned.1.call-start = ((), (), s32[]{:S(2)}) async-start(), calls=%async_computation.24 | async-start | bytes 10485760 | tf_op jit(solution)/shard_map/reduce_scatter | solution.py:379
  3163.1 759.2 %reduce-scatter.23.cloned.1.call-start = ((), (), s32[]{:S(2)}) async-start(), calls=%async_computation.20 | async-start | bytes 1310720 | tf_op jit(solution)/shard_map/reduce_scatter | solution.py:370
  3331.9 592.3 %reduce-scatter.21.cloned.1.call-start = ((), (), s32[]{:S(2)}) async-start(), calls=%async_computation.19 | async-start | bytes 1310720 | tf_op jit(solution)/shard_map/reduce_scatter | solution.py:367
  3356.9 569.0 %reduce-scatter.19.cloned.1.call-start = ((), (), s32[]{:S(2)}) async-start(), calls=%async_computation.18 | async-start | bytes 1310720 | tf_op jit(solution)/shard_map/reduce_scatter | solution.py:364
  3398.2 529.5 %reduce-scatter.17.cloned.1.call-start = ((), (), s32[]{:S(2)}) async-start(), calls=%async_computation.17 | async-start | bytes 1310720 | tf_op jit(solution)/shard_map/reduce_scatter | solution.py:361
  3412.9 516.7 %reduce-scatter.15.cloned.1.call-start = ((), (), s32[]{:S(2)}) async-start(), calls=%async_computation.16 | async-start | bytes 9437184 | tf_op jit(solution)/shard_map/reduce_scatter | solution.py:346
  3438.4 537.6 %reduce-scatter.11.cloned.1.call-start = ((), (), s32[]{:S(2)}) async-start(), calls=%async_computation.13 | async-start | bytes 9437184 | tf_op jit(solution)/shard_map/reduce_scatter | solution.py:220
  3905.0 199.8 %all-reduce.8.cloned.1.call-start = ((), (), s32[]{:S(2)}) async-start(), calls=%async_computation.21 | async-start | bytes 262144 | tf_op jit(solution)/shard_map/psum | solution.py:389
  (139 other events, 2875.8 us)
Sparse Core Ops, SparseCore 0:
  9.9 57.1 all-gather.3
  216.1 217.8 all-reduce.5
  436.0 54.3 all-gather.5
  3028.9 116.1 reduce-scatter.12
  3161.1 54.4 all-gather.7
  3217.9 144.4 reduce-scatter.26
  3364.9 145.1 reduce-scatter.24
  3512.6 145.1 reduce-scatter.28
  3660.2 27.8 reduce-scatter.22
  3690.3 25.7 reduce-scatter.20
  3718.5 25.8 reduce-scatter.18
  3747.0 25.7 reduce-scatter.16
  3776.7 69.9 reduce-scatter.14
  3905.1 70.8 reduce-scatter.10
  3982.3 122.4 all-reduce.7
where the time goes:
time: 4150 us; the launch traced here: 4110 us
  local copies, waits for them, and re-layouts  2540 us (61%)
  matrix products  799 us (19%)
  other arithmetic  326 us (8%)
  waiting for transfers between devices  305 us (7%)
  blocking collectives  113 us (3%)
    gather x16, local copies, waits for them, and re-layouts, combine_slots(): slot_table[slot_pairs[:, rank]] * kept_float[:, rank:rank + 1]  869 us
    dot_general x53, matrix products, contract_cols(): lax.dot_general(left_side, right_side, (((1,), (1,)), ((), ())), preferre...  265 us
    gather x16, local copies, waits for them, and re-layouts, expert_forward(): slot_rows = moe_in[rows_of] * live_of[:, None]  245 us
    gather x16, local copies, waits for them, and re-layouts, expert_backward(): cotangent_wide[rows_of].astype(jnp.float32)  245 us
    gather x16, local copies, waits for them, and re-layouts, expert_backward(): slot_rows = moe_in[rows_of] * live_of[:, None]  245 us
    gather x16, local copies, waits for them, and re-layouts, expert_forward(): cotangent_wide[rows_of].astype(jnp.float32) * expert_out  245 us
    dot_general x53, matrix products, contract_rows(): lax.dot_general(left_side, right_side, (((0,), (0,)), ((), ())), preferre...  171 us
    gather x5, local copies, waits for them, and re-layouts, per_device(): gate_values = jnp.take_along_axis(router_probs, routes, axis=1)  132 us
  transfers between devices with their start and end apart: 15, of which 5 were waited for; matrix products, arithmetic and copies ran while one was open for 29% of the time, Pallas kernels for 0%

commit v1 on v0

v1 whole, which is shorter than its diff:
```python
import functools
import math

import jax
import jax.numpy as jnp
from jax import lax
from jax.experimental import pallas as pl
from jax.experimental.pallas import tpu as pltpu
from jax.sharding import PartitionSpec as P

HEAD_DIM = 128
EPS = 1e-05
NEG = -1e30
MIB = 1 << 20
BF = jnp.bfloat16
F32 = jnp.float32


def rms_scale(values):
    return lax.rsqrt(jnp.mean(values * values, axis=-1, keepdims=True) + EPS)


def dot_nn(a, b):
    return lax.dot_general(a, b, (((1,), (0,)), ((), ())), preferred_element_type=F32)


def dot_nt(a, b):
    return lax.dot_general(a, b, (((1,), (1,)), ((), ())), preferred_element_type=F32)


def dot_tn(a, b):
    return lax.dot_general(a, b, (((0,), (0,)), ((), ())), preferred_element_type=F32)


def attn_fwd_body(lo_ref, q_ref, k_ref, v_ref, sq_ref, sk_ref, o_ref, lse_ref, *, block, heads):
    qb = pl.program_id(0)
    scale = 1.0 / math.sqrt(HEAD_DIM)
    seg_q = sq_ref[...]
    row = qb * block + lax.broadcasted_iota(jnp.int32, (block, block), 0)
    col0 = lax.broadcasted_iota(jnp.int32, (block, block), 1)
    qs = [q_ref[:, h * HEAD_DIM : (h + 1) * HEAD_DIM] for h in range(heads)]

    def step(kb, carry):
        rows = pl.ds(pl.multiple_of(kb * block, block), block)
        allowed = (seg_q == sk_ref[kb]) & (kb * block + col0 <= row)
        out = []
        for h in range(heads):
            m, l, acc = carry[h]
            cols = slice(h * HEAD_DIM, (h + 1) * HEAD_DIM)
            s = jnp.where(allowed, dot_nt(qs[h], k_ref[rows, cols]) * scale, NEG)
            m_new = jnp.maximum(m, jnp.max(s, axis=1, keepdims=True))
            p = jnp.exp(s - m_new)
            alpha = jnp.exp(m - m_new)
            l = alpha * l + jnp.sum(p, axis=1, keepdims=True)
            acc = alpha * acc + dot_nn(p.astype(BF), v_ref[rows, cols])
            out.append((m_new, l, acc))
        return tuple(out)

    init = tuple(
        (
            jnp.full((block, 1), NEG, F32),
            jnp.zeros((block, 1), F32),
            jnp.zeros((block, HEAD_DIM), F32),
        )
        for _ in range(heads)
    )
    final = lax.fori_loop(lo_ref[qb], qb + 1, step, init)
    for h in range(heads):
        m, l, acc = final[h]
        o_ref[:, h * HEAD_DIM : (h + 1) * HEAD_DIM] = acc / l
        lse_ref[:, h : h + 1] = m + jnp.log(l)


def attn_fwd(lo, q, k, v, seg_col, seg_rows, block):
    tokens, cols = q.shape
    heads = cols // HEAD_DIM
    nb = tokens // block
    full = lambda shape: pl.BlockSpec(shape, lambda i, lo: (0,) * len(shape))
    return pl.pallas_call(
        functools.partial(attn_fwd_body, block=block, heads=heads),
        out_shape=(
            jax.ShapeDtypeStruct((tokens, cols), F32),
            jax.ShapeDtypeStruct((tokens, heads), F32),
        ),
        grid_spec=pltpu.PrefetchScalarGridSpec(
            num_scalar_prefetch=1,
            grid=(nb,),
            in_specs=[
                pl.BlockSpec((block, cols), lambda i, lo: (i, 0)),
                full((tokens, cols)),
                full((tokens, cols)),
                pl.BlockSpec((block, 1), lambda i, lo: (i, 0)),
                full((nb, 1, block)),
            ],
            out_specs=[
                pl.BlockSpec((block, cols), lambda i, lo: (i, 0)),
                pl.BlockSpec((block, heads), lambda i, lo: (i, 0)),
            ],
        ),
        compiler_params=pltpu.CompilerParams(vmem_limit_bytes=32 * MIB),
        cost_estimate=pl.CostEstimate(
            flops=8 * 10**9, bytes_accessed=8 * MIB, transcendentals=8 * 10**6
        ),
        name="attn_fwd",
    )(lo, q, k, v, seg_col, seg_rows)


def attn_bwd_body(
    lo_ref, q_ref, k_ref, v_ref, do_ref, o_ref, lse_ref, sq_ref, sk_ref, dq_ref, dk_ref, dv_ref, *, block, heads
):
    qb = pl.program_id(0)
    scale = 1.0 / math.sqrt(HEAD_DIM)

    @pl.when(qb == 0)
    def _():
        dk_ref[...] = jnp.zeros_like(dk_ref)
        dv_ref[...] = jnp.zeros_like(dv_ref)

    seg_q = sq_ref[...]
    row = qb * block + lax.broadcasted_iota(jnp.int32, (block, block), 0)
    col0 = lax.broadcasted_iota(jnp.int32, (block, block), 1)
    hc = [slice(h * HEAD_DIM, (h + 1) * HEAD_DIM) for h in range(heads)]
    qs = [q_ref[:, c] for c in hc]
    dos = [do_ref[:, c] for c in hc]
    lse = [lse_ref[:, h : h + 1] for h in range(heads)]
    dsum = [
        jnp.sum(dos[h].astype(F32) * o_ref[:, hc[h]], axis=1, keepdims=True) for h in range(heads)
    ]

    def step(kb, carry):
        rows = pl.ds(pl.multiple_of(kb * block, block), block)
        allowed = (seg_q == sk_ref[kb]) & (kb * block + col0 <= row)
        out = []
        for h in range(heads):
            k_blk = k_ref[rows, hc[h]]
            s = jnp.where(allowed, dot_nt(qs[h], k_blk) * scale, NEG)
            p = jnp.exp(s - lse[h])
            dp = dot_nt(dos[h], v_ref[rows, hc[h]])
            ds = (p * (dp - dsum[h])).astype(BF)
            dv_ref[rows, hc[h]] += dot_tn(p.astype(BF), dos[h])
            dk_ref[rows, hc[h]] += dot_tn(ds, qs[h]) * scale
            out.append(carry[h] + dot_nn(ds, k_blk))
        return tuple(out)

    init = tuple(jnp.zeros((block, HEAD_DIM), F32) for _ in range(heads))
    final = lax.fori_loop(lo_ref[qb], qb + 1, step, init)
    for h in range(heads):
        dq_ref[:, hc[h]] = final[h] * scale


def attn_bwd(lo, q, k, v, do, o, lse, seg_col, seg_rows, block):
    tokens, cols = q.shape
    heads = cols // HEAD_DIM
    nb = tokens // block
    full = lambda shape: pl.BlockSpec(shape, lambda i, lo: (0,) * len(shape))
    rowed = lambda c: pl.BlockSpec((block, c), lambda i, lo: (i, 0))
    return pl.pallas_call(
        functools.partial(attn_bwd_body, block=block, heads=heads),
        out_shape=tuple(jax.ShapeDtypeStruct((tokens, cols), F32) for _ in range(3)),
        grid_spec=pltpu.PrefetchScalarGridSpec(
            num_scalar_prefetch=1,
            grid=(nb,),
            in_specs=[
                rowed(cols),
                full((tokens, cols)),
                full((tokens, cols)),
                rowed(cols),
                rowed(cols),
                rowed(heads),
                rowed(1),
                full((nb, 1, block)),
            ],
            out_specs=[rowed(cols), full((tokens, cols)), full((tokens, cols))],
        ),
        compiler_params=pltpu.CompilerParams(vmem_limit_bytes=40 * MIB),
        cost_estimate=pl.CostEstimate(
            flops=20 * 10**9, bytes_accessed=16 * MIB, transcendentals=8 * 10**6
        ),
        name="attn_bwd",
    )(lo, q, k, v, do, o, lse, seg_col, seg_rows)


def expert_body(
    x_hbm, xt_hbm, g_hbm, gates_ref, wg_ref, wu_ref, wd_ref, _dgu_in, _ga_in,
    dgu_ref, ga_ref, dots_ref, grads_ref,
    x_v, xt_v, g_v, wcat, sem_x, sem_t, sem_g, *, first, rows_blk, parts
):
    p = pl.program_id(0)
    tokens, width = x_v.shape
    nblk = tokens // rows_blk
    hid = wg_ref.shape[2]
    experts = gates_ref.shape[1]
    ds = width // parts

    def x_copy(i):
        r = pl.ds(i * rows_blk, rows_blk)
        return pltpu.make_async_copy(x_hbm.at[r], x_v.at[r], sem_x.at[i])

    def g_copy(i):
        r = pl.ds(i * rows_blk, rows_blk)
        return pltpu.make_async_copy(g_hbm.at[r], g_v.at[r], sem_g.at[i])

    t_copy = pltpu.make_async_copy(xt_hbm, xt_v, sem_t)

    @pl.when(p == 0)
    def _():
        for i in range(nblk):
            x_copy(i).start()
            g_copy(i).start()
        t_copy.start()
        dots_ref[...] = jnp.zeros_like(dots_ref)

    wcat[:, 0:hid] = wg_ref[0]
    wcat[:, hid : 2 * hid] = wg_ref[1]
    wcat[:, 2 * hid : 3 * hid] = wu_ref[0]
    wcat[:, 3 * hid : 4 * hid] = wu_ref[1]
    lane = lax.broadcasted_iota(jnp.int32, (rows_blk, experts), 1)
    e0 = 2 * (first + p)

    def block(i, _):
        r = pl.ds(pl.multiple_of(i * rows_blk, rows_blk), rows_blk)

        @pl.when(p == 0)
        def _():
            pltpu.make_async_copy(x_hbm.at[r], x_v.at[r], sem_x.at[i]).wait()
            pltpu.make_async_copy(g_hbm.at[r], g_v.at[r], sem_g.at[i]).wait()

        gu = dot_nn(x_v[r, :], wcat[...])
        q = dot_nt(g_v[r, :], wd_ref[...])
        gate_rows = gates_ref[r, :]
        dots = dots_ref[r, :]
        for j in range(2):
            pre = gu[:, j * hid : (j + 1) * hid]
            up = gu[:, (2 + j) * hid : (3 + j) * hid]
            back = q[:, j * hid : (j + 1) * hid]
            here = lane == e0 + j
            gate = jnp.sum(jnp.where(here, gate_rows, 0.0), axis=1, keepdims=True)
            sig = jax.nn.sigmoid(pre)
            silu = pre * sig
            act = silu * up
            dot = jnp.sum(act * back, axis=1, keepdims=True)
            dots = dots + jnp.where(here, dot, 0.0)
            scaled = gate * back
            d_up = scaled * silu
            d_gate = scaled * up * (sig + silu * (1.0 - sig))
            dgu_ref[0, r, j * hid : (j + 1) * hid] = d_gate.astype(BF)
            dgu_ref[0, r, (2 + j) * hid : (3 + j) * hid] = d_up.astype(BF)
            ga_ref[0, r, j * hid : (j + 1) * hid] = (gate * act).astype(BF)
        dots_ref[r, :] = dots
        return 0

    lax.fori_loop(0, nblk, block, 0)

    @pl.when(p == 0)
    def _():
        t_copy.wait()

    for s in range(parts):
        gd = dot_tn(ga_ref[0], g_v[:, s * ds : (s + 1) * ds]).astype(BF)
        gw = dot_nn(xt_v[s * ds : (s + 1) * ds, :], dgu_ref[0]).astype(BF)
        for j in range(2):
            grads_ref[s, 3 * j] = gw[:, j * hid : (j + 1) * hid]
            grads_ref[s, 3 * j + 1] = gw[:, (2 + j) * hid : (3 + j) * hid]
            for c in range(ds // hid):
                grads_ref[s, 3 * j + 2, c * hid : (c + 1) * hid, :] = gd[
                    j * hid : (j + 1) * hid, c * hid : (c + 1) * hid
                ]


def expert_chunk(x, xt, g, gates, wg, wu, wd, dgu, ga, *, first, pairs, parts):
    tokens, width = x.shape
    experts, _, hid = wg.shape
    rows_blk = 512
    nblk = tokens // rows_blk
    ds = width // parts
    any_spec = pl.BlockSpec(memory_space=pl.ANY)
    return pl.pallas_call(
        functools.partial(expert_body, first=first, rows_blk=rows_blk, parts=parts),
        out_shape=(
            jax.ShapeDtypeStruct(dgu.shape, BF),
            jax.ShapeDtypeStruct(ga.shape, BF),
            jax.ShapeDtypeStruct((tokens, experts), F32),
            jax.ShapeDtypeStruct((parts, pairs * 6, ds, hid), BF),
        ),
        grid=(pairs,),
        in_specs=[
            any_spec,
            any_spec,
            any_spec,
            pl.BlockSpec((tokens, experts), lambda p: (0, 0)),
            pl.BlockSpec((2, width, hid), lambda p: (first + p, 0, 0)),
            pl.BlockSpec((2, width, hid), lambda p: (first + p, 0, 0)),
            pl.BlockSpec((2 * hid, width), lambda p: (first + p, 0)),
            any_spec,
            any_spec,
        ],
        out_specs=[
            pl.BlockSpec((1, tokens, 4 * hid), lambda p: (first + p, 0, 0)),
            pl.BlockSpec((1, tokens, 2 * hid), lambda p: (first + p, 0, 0)),
            pl.BlockSpec((tokens, experts), lambda p: (0, 0)),
            pl.BlockSpec((parts, 6, ds, hid), lambda p: (0, p, 0, 0)),
        ],
        scratch_shapes=[
            pltpu.VMEM((tokens, width), BF),
            pltpu.VMEM((width, tokens), BF),
            pltpu.VMEM((tokens, width), BF),
            pltpu.VMEM((width, 4 * hid), BF),
            pltpu.SemaphoreType.DMA((nblk,)),
            pltpu.SemaphoreType.DMA,
            pltpu.SemaphoreType.DMA((nblk,)),
        ],
        input_output_aliases={7: 0, 8: 1},
        compiler_params=pltpu.CompilerParams(vmem_limit_bytes=60 * MIB),
        cost_estimate=pl.CostEstimate(
            flops=pairs * 12 * tokens * width * hid * 2,
            bytes_accessed=40 * MIB,
            transcendentals=pairs * tokens * 2 * hid,
        ),
        name="expert_chunk",
    )(x, xt, g, gates, wg, wu, wd, dgu, ga)


def expert_back_body(dgu_ref, wg_ref, wu_ref, out_ref, wcat, acc):
    p = pl.program_id(1)
    hid = wg_ref.shape[2]
    wcat[:, 0:hid] = wg_ref[0]
    wcat[:, hid : 2 * hid] = wg_ref[1]
    wcat[:, 2 * hid : 3 * hid] = wu_ref[0]
    wcat[:, 3 * hid : 4 * hid] = wu_ref[1]
    rows = 256
    cols = 1024
    for i in range(acc.shape[0] // rows):
        for j in range(acc.shape[1] // cols):
            r = slice(i * rows, (i + 1) * rows)
            c = slice(j * cols, (j + 1) * cols)
            part = dot_nt(dgu_ref[0, r, :], wcat[c, :])

            @pl.when(p == 0)
            def _():
                acc[r, c] = part

            @pl.when(p > 0)
            def _():
                acc[r, c] += part

    @pl.when(p == pl.num_programs(1) - 1)
    def _():
        out_ref[...] = acc[...].astype(BF)


def expert_back(dgu, wg, wu):
    pairs, tokens, _ = dgu.shape
    _, width, hid = wg.shape
    rows = 1024
    return pl.pallas_call(
        expert_back_body,
        out_shape=jax.ShapeDtypeStruct((tokens, width), BF),
        grid=(tokens // rows, pairs),
        in_specs=[
            pl.BlockSpec((1, rows, 4 * hid), lambda i, p: (p, i, 0)),
            pl.BlockSpec((2, width, hid), lambda i, p: (p, 0, 0)),
            pl.BlockSpec((2, width, hid), lambda i, p: (p, 0, 0)),
        ],
        out_specs=pl.BlockSpec((rows, width), lambda i, p: (i, 0)),
        scratch_shapes=[pltpu.VMEM((width, 4 * hid), BF), pltpu.VMEM((rows, width), F32)],
        compiler_params=pltpu.CompilerParams(vmem_limit_bytes=48 * MIB),
        cost_estimate=pl.CostEstimate(
            flops=2 * pairs * tokens * width * 4 * hid,
            bytes_accessed=64 * MIB,
            transcendentals=0,
        ),
        name="expert_back",
    )(dgu, wg, wu)


def swap(value, axis, size, bit):
    return lax.ppermute(value, axis, [(i, i ^ bit) for i in range(size)])


def sum_all(value, axis, size):
    bit = 1
    while bit < size:
        value = value + swap(value, axis, size, bit)
        bit *= 2
    return value


def bits_of(size):
    return [1 << b for b in range(size.bit_length() - 1)]


def scatter_sum(value, size):
    me = lax.axis_index("tensor")
    rows, cols = value.shape
    own = rows // size
    nbits = size.bit_length() - 1
    x = value.reshape((2,) * nbits + (own, cols))

    def halve(y, live, bit):
        axis = live.index(bit)
        mine = (me // bit) % 2
        send = lax.dynamic_index_in_dim(y, 1 - mine, axis, keepdims=False)
        keep = lax.dynamic_index_in_dim(y, mine, axis, keepdims=False)
        got = swap(send, "tensor", size, bit)
        return (keep.astype(F32) + got.astype(F32)).astype(BF), [b for b in live if b != bit]

    live = bits_of(size)[::-1]
    x, live = halve(x, live, 1)
    rest = bits_of(size)[1:]
    halves = []
    for order, part in ((rest, slice(0, cols // 2)), (rest[::-1], slice(cols // 2, cols))):
        y, ly = x[..., part], list(live)
        for bit in order:
            y, ly = halve(y, ly, bit)
        halves.append(y)
    return jnp.concatenate(halves, axis=-1)


def gather_rows(value, size):
    me = lax.axis_index("tensor")
    own, cols = value.shape
    rest = bits_of(size)[1:]
    halves = []

    def join(y, bit):
        got = swap(y, "tensor", size, bit)
        low = (me // bit) % 2 == 0
        return jnp.stack([jnp.where(low, y, got), jnp.where(low, got, y)], axis=0)

    for order, part in ((rest, slice(0, cols // 2)), (rest[::-1], slice(cols // 2, cols))):
        y = value[:, part]
        for bit in order:
            y = join(y, bit)
        lead = list(order[::-1])
        perm = [lead.index(b) for b in rest[::-1]]
        n = len(lead)
        y = y.transpose(tuple(perm) + (n, n + 1))
        halves.append(y)
    y = jnp.concatenate(halves, axis=-1)
    y = join(y, 1)
    n = len(rest)
    y = y.transpose(tuple(range(1, n + 1)) + (0, n + 1, n + 2))
    return y.reshape(own * size, cols)


def half_swap(values):
    pieces = []
    half = HEAD_DIM // 2
    for h in range(values.shape[1] // HEAD_DIM):
        base = h * HEAD_DIM
        pieces += [values[:, base + half : base + HEAD_DIM], values[:, base : base + half]]
    return jnp.concatenate(pieces, axis=1)


def per_device(
    block_input, segments, routes, w_query, w_key, w_value, w_output, attn_gain, query_gain, key_gain,
    moe_gain, router, w_gate, w_up, w_down, cotangent, *, n_dp, n_tensor
):
    own_rows, model_width = block_input.shape
    local_cols = w_query.shape[1]
    local_heads = local_cols // HEAD_DIM
    token_count = segments.shape[0] * segments.shape[1]
    experts = router.shape[1]
    top_count = routes.shape[1]
    hid = w_gate.shape[2]
    capacity = 5 * token_count * top_count // (4 * experts)
    me = lax.axis_index("tensor")
    rank_start = me * own_rows
    col_start = me * local_cols
    block = 256

    full_input = lax.all_gather(block_input, "tensor", axis=0, tiled=True)

    seg = segments.reshape(token_count)
    values16 = jnp.arange(16, dtype=jnp.int32)
    below = jnp.sum((seg[None, :] < values16[:, None]).astype(jnp.int32), axis=1)
    doc_start = jnp.sum(
        jnp.where(seg[:, None] == values16[None, :], below[None, :], 0), axis=1
    )
    positions = jnp.arange(token_count, dtype=jnp.int32) - doc_start
    half = HEAD_DIM // 2
    frequency = jnp.exp(
        jnp.arange(half, dtype=F32) * (-2.0 * math.log(10000.0) / HEAD_DIM)
    )
    angles = positions.astype(F32)[:, None] * frequency[None, :]
    cosine, sine = jnp.cos(angles), jnp.sin(angles)
    cos_all = jnp.concatenate([cosine] * (2 * local_heads), axis=1)
    sin_all = jnp.concatenate([-sine, sine] * local_heads, axis=1)
    cos_all, sin_all = lax.optimization_barrier((cos_all, sin_all))
    lo_block = doc_start[::block] // block
    seg_col = seg[:, None]
    seg_rows = seg.reshape(token_count // block, 1, block)

    expert_ids = jnp.arange(experts, dtype=jnp.int32)
    routed = jnp.sum(
        (routes[:, :, None] == expert_ids[None, None, :]).astype(F32), axis=1
    )
    tri = (
        jnp.arange(block, dtype=jnp.int32)[:, None] > jnp.arange(block, dtype=jnp.int32)[None, :]
    ).astype(BF)
    nb = token_count // block
    routed_b = routed.reshape(nb, block, experts)
    within = jnp.einsum("ij,bje->bie", tri, routed_b.astype(BF), preferred_element_type=F32)
    sums = jnp.sum(routed_b, axis=1)
    before = jnp.sum(
        jnp.where(
            (jnp.arange(nb)[:, None] > jnp.arange(nb)[None, :])[:, :, None], sums[None, :, :], 0.0
        ),
        axis=1,
    )
    place = within + before[:, None, :]
    mask = (routed_b * (place < capacity).astype(F32)).reshape(token_count, experts)

    full_input, w_output_in = lax.optimization_barrier((full_input, w_output))
    full_wo = lax.all_gather(w_output_in, "tensor", axis=0, tiled=True)
    full_wo, cot_in = lax.optimization_barrier((full_wo, cotangent))
    full_cot = lax.all_gather(cot_in, "tensor", axis=0, tiled=True)

    input_wide = full_input.astype(F32)
    scale_one = rms_scale(input_wide)
    normed = (input_wide * scale_one * attn_gain).astype(BF)
    w_qkv = jnp.concatenate([w_query, w_key, w_value], axis=1)
    qkv = dot_nn(normed, w_qkv)
    query_raw = qkv[:, :local_cols]
    key_raw = qkv[:, local_cols : 2 * local_cols]
    value_low = qkv[:, 2 * local_cols :].astype(BF)
    squares = jnp.stack(
        [jnp.sum(query_raw * query_raw, axis=1), jnp.sum(key_raw * key_raw, axis=1)]
    )
    squares = sum_all(squares, "tensor", n_tensor)
    scales = lax.rsqrt(squares / model_width + EPS)
    query_rs = scales[0][:, None]
    key_rs = scales[1][:, None]
    query_unit = query_raw * query_rs
    key_unit = key_raw * key_rs
    q_n = query_unit * query_gain
    k_n = key_unit * key_gain
    queries = (q_n * cos_all + half_swap(q_n) * sin_all).astype(BF)
    keys_rot = (k_n * cos_all + half_swap(k_n) * sin_all).astype(BF)
    attended, lse = attn_fwd(lo_block, queries, keys_rot, value_low, seg_col, seg_rows, block)
    attn_low = attended.astype(BF)

    own_attn = lax.all_to_all(
        attn_low.reshape(n_tensor, own_rows, local_cols), "tensor", 0, 0
    )
    own_attn = own_attn.transpose(1, 0, 2).reshape(own_rows, model_width)
    input_own = block_input.astype(F32)
    residual = input_own + dot_nn(own_attn, full_wo)
    scale_two = rms_scale(residual)
    own_moe_in = (residual * scale_two * moe_gain).astype(BF)
    moe_in = lax.all_gather(own_moe_in, "tensor", axis=0, tiled=True)

    router_probs = jax.nn.softmax(dot_nn(moe_in, router), axis=-1)
    gates = router_probs * mask
    moe_in_t = moe_in.T
    pairs_total = experts // 2
    chunk_pairs = 2
    wd_flat = w_down.reshape(experts * hid, model_width)
    dgu = jnp.zeros((pairs_total, token_count, 4 * hid), BF)
    ga = jnp.zeros((pairs_total, token_count, 2 * hid), BF)
    dots = None
    reduced = []
    for c in range(pairs_total // chunk_pairs):
        dgu, ga, dot_c, grads = expert_chunk(
            moe_in, moe_in_t, full_cot, gates, w_gate, w_up, wd_flat, dgu, ga,
            first=c * chunk_pairs, pairs=chunk_pairs, parts=n_dp,
        )
        dots = dot_c if dots is None else dots + dot_c
        reduced.append(lax.psum_scatter(grads, "dp", scatter_dimension=0, tiled=False))
    back_part = expert_back(dgu, w_gate, w_up)
    moe_back = scatter_sum(back_part, n_tensor).astype(F32)

    out_part = sum(
        dot_nn(ga[p], wd_flat[p * 2 * hid : (p + 1) * 2 * hid]) for p in range(pairs_total)
    )
    moe_out = scatter_sum(out_part.astype(BF), n_tensor).astype(F32)
    block_output = (residual + moe_out).astype(BF)

    own_dots = jnp.sum(
        lax.all_to_all(dots.reshape(n_tensor, own_rows, experts), "tensor", 0, 0), axis=0
    )
    own_mask = lax.dynamic_slice_in_dim(mask, rank_start, own_rows, 0)
    own_probs = lax.dynamic_slice_in_dim(router_probs, rank_start, own_rows, 0)
    prob_grads = own_dots * own_mask
    own_logit = (
        own_probs * (prob_grads - jnp.sum(own_probs * prob_grads, axis=1, keepdims=True))
    ).astype(BF)
    router_grad = dot_tn(own_logit, own_moe_in)
    moe_grad = moe_back + dot_nt(own_logit, router)

    unit_two = residual * scale_two
    moe_gain_grad = jnp.sum(moe_grad * unit_two, axis=0)
    scaled_two = moe_grad * moe_gain
    residual_grad = cotangent.astype(F32) + scale_two * (
        scaled_two - unit_two * jnp.mean(scaled_two * unit_two, axis=1, keepdims=True)
    )
    residual_low = gather_rows(residual_grad.astype(BF), n_tensor)
    output_grad = dot_tn(attn_low, residual_low)
    heads_grad = dot_nt(residual_low, w_output).astype(BF)

    dq_rot, dk_rot, dv = attn_bwd(
        lo_block, queries, keys_rot, value_low, heads_grad, attended, lse, seg_col, seg_rows, block
    )
    query_norm_grad = dq_rot * cos_all - half_swap(dq_rot) * sin_all
    key_norm_grad = dk_rot * cos_all - half_swap(dk_rot) * sin_all
    query_gain_grad = jnp.sum(query_norm_grad * query_unit, axis=0)
    key_gain_grad = jnp.sum(key_norm_grad * key_unit, axis=0)
    query_scaled = query_norm_grad * query_gain
    key_scaled = key_norm_grad * key_gain
    inner = jnp.stack(
        [jnp.sum(query_scaled * query_unit, axis=1), jnp.sum(key_scaled * key_unit, axis=1)]
    )
    inner = sum_all(inner, "tensor", n_tensor) / model_width
    query_grad_low = (query_rs * (query_scaled - query_unit * inner[0][:, None])).astype(BF)
    key_grad_low = (key_rs * (key_scaled - key_unit * inner[1][:, None])).astype(BF)
    qkv_grad = jnp.concatenate([query_grad_low, key_grad_low, dv.astype(BF)], axis=1)
    qkv_w_grad = dot_tn(normed, qkv_grad).astype(BF)
    normed_part = dot_nt(qkv_grad, w_qkv).astype(BF)
    normed_grad = scatter_sum(normed_part, n_tensor).astype(F32)
    scale_own = rms_scale(input_own)
    unit_one = input_own * scale_own
    attn_gain_grad = jnp.sum(normed_grad * unit_one, axis=0)
    scaled_one = normed_grad * attn_gain
    grad_input = residual_grad + scale_own * (
        scaled_one - unit_one * jnp.mean(scaled_one * unit_one, axis=1, keepdims=True)
    )

    wo_red = lax.psum_scatter(
        output_grad.astype(BF), "dp", scatter_dimension=1, tiled=True
    ).astype(F32)
    qkv_red = lax.psum_scatter(qkv_w_grad, "dp", scatter_dimension=0, tiled=True).astype(F32)
    early = jnp.concatenate([router_grad, moe_gain_grad[None, :]], axis=0)
    early = sum_all(sum_all(early, "tensor", n_tensor), "dp", n_dp)
    gains = jnp.stack(
        [
            attn_gain_grad,
            lax.dynamic_update_slice_in_dim(
                jnp.zeros((model_width,), F32), query_gain_grad, col_start, 0
            ),
            lax.dynamic_update_slice_in_dim(
                jnp.zeros((model_width,), F32), key_gain_grad, col_start, 0
            ),
        ]
    )
    gains = sum_all(sum_all(gains, "tensor", n_tensor), "dp", n_dp)

    ds = model_width // n_dp
    gate_out, up_out, down_out = [], [], []
    for r in reduced:
        r = r.reshape(2 * chunk_pairs, 3, ds, hid)
        gate_out.append(r[:, 0])
        up_out.append(r[:, 1])
        down = r[:, 2].reshape(2 * chunk_pairs, ds // hid, hid, hid)
        down_out.append(down.transpose(0, 2, 1, 3).reshape(2 * chunk_pairs, hid, ds))
    grad_gate = jnp.concatenate(gate_out, axis=0).astype(F32)
    grad_up = jnp.concatenate(up_out, axis=0).astype(F32)
    grad_down = jnp.concatenate(down_out, axis=0).astype(F32)
    return (
        block_output,
        grad_input,
        qkv_red[:, :local_cols],
        qkv_red[:, local_cols : 2 * local_cols],
        qkv_red[:, 2 * local_cols :],
        wo_red,
        gains[0],
        gains[1],
        gains[2],
        early[experts],
        early[:experts].T,
        grad_gate,
        grad_up,
        grad_down,
    )


def solution(mesh):
    rows = P(("dp", "tensor"), None)
    cols = P(None, "tensor")
    wide = P(None, None, "tensor")
    placed = (
        rows, P("dp", None), P("dp", None), cols, cols, cols, P("tensor", None), P(), P("tensor"), P("tensor"),
        P(), P(), wide, wide, P(None, "tensor", None), rows,
    )
    outs = (
        rows, rows, P("dp", "tensor"), P("dp", "tensor"), P("dp", "tensor"), P("tensor", "dp"), P(), P(), P(), P(),
        P(), P(None, "dp", "tensor"), P(None, "dp", "tensor"), P(None, "tensor", "dp"),
    )
    return jax.shard_map(
        functools.partial(
            per_device, n_dp=mesh.shape["dp"], n_tensor=mesh.shape["tensor"]
        ),
        mesh=mesh,
        in_specs=placed,
        out_specs=outs,
        check_vma=False,
    )
```

time: 4150 us -> 1010 us (0.24)
  local copies, waits for them, and re-layouts: 2540 us -> 172 us
  matrix products: 799 us -> 161 us
  Pallas kernels: 0 us -> 272 us
  other arithmetic: 326 us -> 100 us
  blocking collectives: 113 us -> 0 us
  waiting for transfers between devices: 305 us -> 238 us
    gather x88 -> x0, local copies, waits for them, and re-layouts: 2190 us -> none  [the longest x16 869 us: combine_slots(): slot_table[slot_pairs[:, rank]] * kept_float[:, rank:rank + 1]]
    dot_general x187 -> x18, matrix products: 799 us -> 161 us  [the longest x11 126 us: dot_nn(): lax.dot_general(a, b, (((1,), (0,)), ((), ())), preferred_element_type=F32)]
    pallas_call x0 -> x7, Pallas kernels: none -> 272 us  [the longest x4 149 us: expert_chunk(): pl.pallas_call(functools.partial(expert_body, first=first, rows_blk=rows_...]
    psum x2 -> x0, waiting for transfers between devices: 155 us -> none  [the longest x1 82.8 us: per_device(): lax.psum((attn_gain_grad, moe_gain_grad, router_grad, query_gain_full, ke...]
    scatter x2 -> x0, local copies, waits for them, and re-layouts: 121 us -> none  [the longest x1 60.5 us: route_slots(): jnp.zeros((slot_total,), jnp.int32).at[slot_index]]
    psum x4 -> x0, blocking collectives: 113 us -> none  [the longest x1 40.3 us: per_device(): lax.psum((attn_gain_grad, moe_gain_grad, router_grad, query_gain_full, ke...]
    another operation x10 -> x7, local copies, waits for them, and re-layouts: 104 us -> 2.01 us  [the longest x4 1.64 us: per_device(): down = r[:, 2].reshape(2 * chunk_pairs, ds // hid, hid, hid)]
    ppermute x0 -> x36, waiting for transfers between devices: none -> 76.3 us  [swap(): return lax.ppermute(value, axis, [(i, i ^ bit) for i in range(size)])]
  transfers between devices with their start and end apart: 15 -> 48, of which waited for: 5 -> 18; matrix products, arithmetic and copies ran while one was open for 29% -> 40% of each run, Pallas kernels for 0% -> 24%
where the time goes in v1:
time: 1010 us; the launch traced here: 1000 us
  Pallas kernels  272 us (27%)
  waiting for transfers between devices  238 us (24%)
  local copies, waits for them, and re-layouts  172 us (17%)
  matrix products  161 us (16%)
  other arithmetic  100 us (10%)
  starting transfers between devices  40 us (4%)
  between operations  16.5 us (2%)
    pallas_call x4, Pallas kernels, expert_chunk(): pl.pallas_call(functools.partial(expert_body, first=first, rows_blk=rows_...  149 us
    dot_general x11, matrix products, dot_nn(): lax.dot_general(a, b, (((1,), (0,)), ((), ())), preferred_element_type=F32)  126 us
    pallas_call x1, Pallas kernels, expert_back(): pl.pallas_call(expert_back_body, out_shape=jax.ShapeDtypeStruct((tokens,...  80.5 us
    ppermute x36, waiting for transfers between devices, swap(): return lax.ppermute(value, axis, [(i, i ^ bit) for i in range(size)])  76.3 us
    all_gather x1, waiting for transfers between devices, per_device(): full_input = lax.all_gather(block_input, 'tensor', axis=0, tiled=True)  59.1 us
    all_gather x1, waiting for transfers between devices, per_device(): moe_in = lax.all_gather(own_moe_in, 'tensor', axis=0, tiled=True)  52.2 us
    unnamed x226, local copies, waits for them, and re-layouts  42.5 us
    all_gather x1, waiting for transfers between devices, per_device(): full_cot = lax.all_gather(cot_in, 'tensor', axis=0, tiled=True)  35.4 us
  transfers between devices with their start and end apart: 48, of which 18 were waited for; matrix products, arithmetic and copies ran while one was open for 40% of the time, Pallas kernels for 24%

profile of v1, /device:TPU:0, one launch (start us, length us, event | category | flops | bytes accessed | tf_op | source)
XLA Modules:
  0.0 1000.5 jit_solution(15574689366418038440)
XLA Ops:
  8.0 59.1 %all-gather.5.cloned.1.call-done = bf16[2048,2048]{1,0:T(8,128)(2,1)} async-done(((bf16[256,2048]{1,0:T(8,128)(2,1)}), bf16[2048,2048]{1,0:T(8,128)(2,1)}) %all-gather.5.cloned.1.call-update) | async-done | bytes 8388624 | tf_op jit(solution)/shard_map/all_gather | solution.py:472
  75.7 7.2 fusion.11
  106.9 20.1 %attn_fwd.1 = (f32[2048,256]{1,0:T(8,128)S(1)}, f32[2048,2]{1,0:T(8,128)S(1)}) custom-call(s32[8]{0:T(128)S(1)} %and_select_fusion.lo_ref, bf16[2048,256]{1,0:T(8,128)(2,1)S(1)} %get-tuple-element.181.q_ref, bf16[2048,256]{1,0:T(8,128)(2,1)S(1)} %get-tuple-element.180.k_ref, bf16[2048,256]{1,0:T(8,128)(2,1)S(1)} %slice.414.v_ref, ...), custom_call_target="tpu_custom_call" | custom-call | flops 8000000000 | bytes 8388608 | tf_op jit(solution)/shard_map/attn_fwd/pallas_call | solution.py:79
  135.7 13.8 %all-to-all-done = bf16[8,256,256]{1,2,0:T(8,128)(2,1)} async-done(((bf16[8,256,256]{1,2,0:T(8,128)(2,1)}), bf16[8,256,256]{1,2,0:T(8,128)(2,1)}, u32[]{:S(2)}, u32[]{:S(2)}) %all-to-all-start) | async-done | bytes 1048608 | tf_op jit(solution)/shard_map/all_to_all | solution.py:543
  149.5 7.3 multiply_reduce_fusion.6
  162.6 52.2 %all-gather.9.cloned.1.call-done = bf16[2048,2048]{0,1:T(8,128)(2,1)} async-done(((bf16[256,2048]{0,1:T(8,128)(2,1)}), bf16[2048,2048]{0,1:T(8,128)(2,1)}) %all-gather.9.cloned.1.call-update) | async-done | bytes 8388624 | tf_op jit(solution)/shard_map/all_gather | solution.py:551
  219.8 12.4 %copy.212.x_hbm = bf16[2048,2048]{1,0:T(8,128)(2,1)} copy(bf16[2048,2048]{0,1:T(8,128)(2,1)} %all-gather.9.cloned.1.call-done) | data formatting | bytes 16777216 | tf_op jit(solution)/shard_map/all_gather | solution.py:551
  235.6 35.4 %all-gather.11.cloned.1.call-done.g_hbm = bf16[2048,2048]{1,0:T(8,128)(2,1)} async-done(((bf16[256,2048]{1,0:T(8,128)(2,1)}), bf16[2048,2048]{1,0:T(8,128)(2,1)}) %all-gather.11.cloned.1.call-update) | async-done | bytes 8388624 | tf_op jit(solution)/shard_map/all_gather | solution.py:517
  280.9 36.6 %expert_chunk.4 = (bf16[8,2048,512]{2,1,0:T(8,128)(2,1)}, bf16[8,2048,256]{2,1,0:T(8,128)(2,1)}, f32[2048,16]{1,0:T(8,128)}, bf16[4,12,512,128]{3,2,1,0:T(8,128)(2,1)}) custom-call(bf16[2048,2048]{1,0:T(8,128)(2,1)} %copy.212.x_hbm, bf16[2048,2048]{1,0:T(8,128)(2,1)} %bitcast.259, ...), custom_call_target="tpu_custom_call", output_to_operand_aliasing={{0}: (7, {}), {1}: (8, {})} | custom-call | flops 25769803776 | bytes 41943040 | tf_op jit(solution)/shard_map/expert_chunk/pallas_call | solution.py:277
  317.8 37.5 %expert_chunk.5 = (bf16[8,2048,512]{2,1,0:T(8,128)(2,1)}, bf16[8,2048,256]{2,1,0:T(8,128)(2,1)}, f32[2048,16]{1,0:T(8,128)}, bf16[4,12,512,128]{3,2,1,0:T(8,128)(2,1)}) custom-call(bf16[2048,2048]{1,0:T(8,128)(2,1)} %copy.212.x_hbm, bf16[2048,2048]{1,0:T(8,128)(2,1)} %bitcast.260, ...), custom_call_target="tpu_custom_call", output_to_operand_aliasing={{0}: (7, {}), {1}: (8, {})} | custom-call | flops 25769803776 | bytes 41943040 | tf_op jit(solution)/shard_map/expert_chunk/pallas_call | solution.py:277
  355.3 37.5 %expert_chunk.6 = (bf16[8,2048,512]{2,1,0:T(8,128)(2,1)}, bf16[8,2048,256]{2,1,0:T(8,128)(2,1)}, f32[2048,16]{1,0:T(8,128)}, bf16[4,12,512,128]{3,2,1,0:T(8,128)(2,1)}) custom-call(bf16[2048,2048]{1,0:T(8,128)(2,1)} %copy.212.x_hbm, bf16[2048,2048]{1,0:T(8,128)(2,1)} %bitcast.261, ...), custom_call_target="tpu_custom_call", output_to_operand_aliasing={{0}: (7, {}), {1}: (8, {})} | custom-call | flops 25769803776 | bytes 41943040 | tf_op jit(solution)/shard_map/expert_chunk/pallas_call | solution.py:277
  392.8 37.9 %expert_chunk.7 = (bf16[8,2048,512]{2,1,0:T(8,128)(2,1)}, bf16[8,2048,256]{2,1,0:T(8,128)(2,1)}, f32[2048,16]{1,0:T(8,128)}, bf16[4,12,512,128]{3,2,1,0:T(8,128)(2,1)}) custom-call(bf16[2048,2048]{1,0:T(8,128)(2,1)} %copy.212.x_hbm, bf16[2048,2048]{1,0:T(8,128)(2,1)} %bitcast.262, ...), custom_call_target="tpu_custom_call", output_to_operand_aliasing={{0}: (7, {}), {1}: (8, {})} | custom-call | flops 25769803776 | bytes 41943040 | tf_op jit(solution)/shard_map/expert_chunk/pallas_call | solution.py:277
  430.7 80.5 %expert_back.1 = bf16[2048,2048]{1,0:T(8,128)(2,1)} custom-call(bf16[8,2048,512]{2,1,0:T(8,128)(2,1)} %get-tuple-element.55.dgu_ref, bf16[16,2048,128]{2,1,0:T(8,128)(2,1)} %wg_ref.9, bf16[16,2048,128]{2,1,0:T(8,128)(2,1)} %wu_ref.9), custom_call_target="tpu_custom_call" | custom-call | flops 34359738368 | bytes 67108864 | tf_op jit(solution)/shard_map/expert_back/pallas_call | solution.py:355
  511.2 8.5 constant_dynamic-slice_fusion.3
  527.9 6.7 fusion.80
  548.8 9.8 fusion.42
  558.6 9.4 fusion.44
  568.1 9.6 fusion.46
  585.4 9.3 fusion.48
  598.2 9.6 fusion.50
  613.4 9.3 collective-permute-done.9
  625.1 9.4 fusion.52
  644.8 9.4 fusion.54
  659.0 40.7 %add_convert_fusion = bf16[2048,2048]{1,0:T(8,128)(2,1)} fusion(f32[2048,2048]{1,0:T(8,128)} %fusion.42, f32[2048,2048]{1,0:T(8,128)} %fusion.44, f32[2048,2048]{1,0:T(8,128)} %fusion.46, f32[2048,2048]{1,0:T(8,128)} %fusion.48, f32[2048,2048]{1,0:T(8,128)} %fusion.50, f32[2048,2048]{1,0:T(8,128)} %fusion.54, f32[2048,2048]{1,0:T(8,128)} %fusion.52, ...), kind=kOutput, calls=%fused_computation.5 | convolution fusion | flops 2181038080 | bytes 127926272 | tf_op jit(solution)/shard_map/dot_general | solution.py:24
  699.7 8.5 constant_dynamic-slice_fusion.5
  750.0 11.6 %copy.222 = bf16[2,2,2,256,2048]{4,3,2,1,0:T(8,128)(2,1)} copy(bf16[2,2,2,256,2048]{3,4,0,1,2:T(8,128)(2,1)} %maximum_bitcast_fusion) | data formatting | bytes 16777216 | tf_op jit(solution)/shard_map/transpose | solution.py:442
  767.7 22.4 %attn_bwd.1 = (f32[2048,256]{1,0:T(8,128)S(1)}, f32[2048,256]{1,0:T(8,128)S(1)}, f32[2048,256]{1,0:T(8,128)S(1)}) custom-call(s32[8]{0:T(128)S(1)} %and_select_fusion.lo_ref, bf16[2048,256]{1,0:T(8,128)(2,1)S(1)} %copy-done.6, bf16[2048,256]{1,0:T(8,128)(2,1)S(1)} %copy-done.4, bf16[2048,256]{1,0:T(8,128)(2,1)S(1)} %copy-done.8, ...), custom_call_target="tpu_custom_call" | custom-call | flops 20000000000 | bytes 16777216 | tf_op jit(solution)/shard_map/attn_bwd/pallas_call | solution.py:157
  808.4 22.7 %collective-permute-done.20 = f32[2,2048]{1,0:T(2,128)S(1)} collective-permute-done((f32[2,2048]{1,0:T(2,128)S(1)}, f32[2,2048]{1,0:T(2,128)S(1)}, u32[]{:S(2)}, u32[]{:S(2)}) %collective-permute-start.20) | collective-permute-done | bytes 16416 | tf_op jit(solution)/shard_map/ppermute | solution.py:377
  833.1 7.2 convolution_convert_fusion
  881.3 16.1 %collective-permute-done.35 = f32[17,2048]{1,0:T(8,128)S(1)} collective-permute-done((f32[17,2048]{1,0:T(8,128)S(1)}, f32[17,2048]{1,0:T(8,128)S(1)}, u32[]{:S(2)}, u32[]{:S(2)}) %collective-permute-start.35) | collective-permute-done | bytes 139296 | tf_op jit(solution)/shard_map/ppermute | solution.py:377
  903.9 11.3 %convolution_convert_fusion.1 = bf16[2048,768]{1,0:T(8,128)(2,1)} fusion(bf16[2048,2048]{1,0:T(8,128)(2,1)} %all-gather.5.cloned.1.call-done, f32[2048]{0:T(1024)S(1)} %copy-done.94, f32[2048]{0:T(1024)S(1)} %copy-done.105, bf16[2048,256]{1,0:T(8,128)(2,1)S(1)} %copy-done.74, bf16[2048,256]{1,0:T(8,128)(2,1)S(1)} %copy-done.78, ...), kind=kOutput, calls=%fused_computation.17 | convolution fusion | flops 6470238208 | bytes 14696448 | tf_op jit(solution)/shard_map/dot_general | solution.py:32
  930.1 9.9 collective-permute-done.24
  (471 shorter events, 304.9 us)
Async XLA Ops:
  7.2 59.8 %all-gather.5.cloned.1.call-start = ((), (), s32[]{:S(2)}) async-start(), calls=%async_computation.8 | async-start | bytes 9437184 | tf_op jit(solution)/shard_map/all_gather | solution.py:472
  8.0 127.7 %all-gather.7.cloned.1.call-start = ((), (), s32[]{:S(2)}) async-start(), calls=%async_computation.9 | async-start | bytes 9437184 | tf_op jit(solution)/shard_map/all_gather | solution.py:515
  129.8 19.7 %all-to-all-start = ((bf16[8,256,256]{1,2,0:T(8,128)(2,1)}), bf16[8,256,256]{1,2,0:T(8,128)(2,1)}, u32[]{:S(2)}, u32[]{:S(2)}) async-start(bf16[8,256,256]{1,2,0:T(8,128)(2,1)} %copy.202), calls=%async_computation | async-start | bytes 2097152 | tf_op jit(solution)/shard_map/all_to_all | solution.py:543
  134.1 80.8 %all-gather.9.cloned.1.call-start = ((), (), s32[]{:S(2)}) async-start(), calls=%async_computation.10 | async-start | bytes 9437184 | tf_op jit(solution)/shard_map/all_gather | solution.py:551
  159.6 111.4 %all-gather.11.cloned.1.call-start = ((), (), s32[]{:S(2)}) async-start(), calls=%async_computation.11 | async-start | bytes 9437184 | tf_op jit(solution)/shard_map/all_gather | solution.py:517
  160.2 764.8 %reduce-scatter.11.cloned.1.call-start = ((), (), s32[]{:S(2)}) async-start(), calls=%async_computation.14 | async-start | bytes 7864320 | tf_op jit(solution)/shard_map/reduce_scatter | solution.py:569
  317.5 609.9 %reduce-scatter.13.cloned.1.call-start = ((), (), s32[]{:S(2)}) async-start(), calls=%async_computation.15 | async-start | bytes 7864320 | tf_op jit(solution)/shard_map/reduce_scatter | solution.py:569
  525.9 51.7 %collective-permute-start.8 = (bf16[2,2,256,2048]{2,3,1,0:T(8,128)(2,1)}, bf16[2,2,256,2048]{2,3,1,0:T(8,128)(2,1)}, u32[]{:S(2)}, u32[]{:S(2)}) collective-permute-start(bf16[2,2,256,2048]{2,3,1,0:T(8,128)(2,1)} %bitcast.287), channel_id=1, source_target_pairs={{0,1},{1,0},{2,3},{3,2},{4,5},{5,4},{6,7},{7,6},{8,9},{9,8},{10,11... | collective-permute-start | bytes 12582920 | tf_op jit(solution)/shard_map/ppermute | solution.py:377
  545.4 89.1 %all-to-all-start.1 = ((f32[8,256,16]{1,2,0:T(8,128)}), f32[8,256,16]{1,2,0:T(8,128)S(1)}, u32[]{:S(2)}, u32[]{:S(2)}) async-start(f32[8,256,16]{1,2,0:T(8,128)} %copy.218), calls=%async_computation.1 | async-start | bytes 262144 | tf_op jit(solution)/shard_map/all_to_all | solution.py:580
  548.7 403.6 %reduce-scatter.17.cloned.1.call-start = ((), (), s32[]{:S(2)}) async-start(), calls=%async_computation.17 | async-start | bytes 7864320 | tf_op jit(solution)/shard_map/reduce_scatter | solution.py:569
  583.5 25.7 %collective-permute-start.11 = (bf16[2,256,1024]{1,2,0:T(8,128)(2,1)}, bf16[2,256,1024]{1,2,0:T(8,128)(2,1)}, u32[]{:S(2)}, u32[]{:S(2)}) collective-permute-start(bf16[2,256,1024]{1,2,0:T(8,128)(2,1)} %dynamic-slice_bitcast_fusion.2), channel_id=1, source_target_pairs={{0,4},{1,5},{2,6},{3,7},{4,0},{5,1},{6,2},{7,3},{8,12},{9,13},{10,... | collective-permute-start | bytes 3145736 | tf_op jit(solution)/shard_map/ppermute | solution.py:377
  594.8 363.5 %reduce-scatter.15.cloned.1.call-start = ((), (), s32[]{:S(2)}) async-start(), calls=%async_computation.16 | async-start | bytes 7864320 | tf_op jit(solution)/shard_map/reduce_scatter | solution.py:569
  596.6 26.1 %collective-permute-start.9 = (bf16[2,256,1024]{1,2,0:T(8,128)(2,1)S(1)}, bf16[2,256,1024]{1,2,0:T(8,128)(2,1)S(1)}, u32[]{:S(2)}, u32[]{:S(2)}) collective-permute-start(bf16[2,256,1024]{1,2,0:T(8,128)(2,1)S(1)} %dynamic-slice_bitcast_fusion.3), channel_id=1, source_target_pairs={{0,2},{1,3},{2,0},{3,1},{4,6},{5,7},{6,4},{7,5},{8,10},{9,11},{10,... | collective-permute-start | bytes 3145736 | tf_op jit(solution)/shard_map/ppermute | solution.py:377
  611.7 24.2 %collective-permute-start.12 = (bf16[256,1024]{0,1:T(8,128)(2,1)}, bf16[256,1024]{0,1:T(8,128)(2,1)}, u32[]{:S(2)}, u32[]{:S(2)}) collective-permute-start(bf16[256,1024]{0,1:T(8,128)(2,1)} %dynamic-slice_bitcast_fusion.8), channel_id=1, source_target_pairs={{0,2},{1,3},{2,0},{3,1},{4,6},{5,7},{6,4},{7,5},{8,10},{9,11},{10,... | collective-permute-start | bytes 1572872 | tf_op jit(solution)/shard_map/ppermute | solution.py:377
  656.9 57.6 %collective-permute-start.16 = (bf16[2,256,1024]{1,2,0:T(8,128)(2,1)}, bf16[2,256,1024]{1,2,0:T(8,128)(2,1)}, u32[]{:S(2)}, u32[]{:S(2)}) collective-permute-start(bf16[2,256,1024]{1,2,0:T(8,128)(2,1)} %pad_maximum_fusion.7), channel_id=1, source_target_pairs={{0,2},{1,3},{2,0},{3,1},{4,6},{5,7},{6,4},{7,5},{8,10},{9,11},{10,... | collective-permute-start | bytes 3145736 | tf_op jit(solution)/shard_map/ppermute | solution.py:377
  658.5 57.8 %collective-permute-start.14 = (bf16[2,256,1024]{1,2,0:T(8,128)(2,1)}, bf16[2,256,1024]{1,2,0:T(8,128)(2,1)}, u32[]{:S(2)}, u32[]{:S(2)}) collective-permute-start(bf16[2,256,1024]{1,2,0:T(8,128)(2,1)} %pad_maximum_fusion.6), channel_id=1, source_target_pairs={{0,4},{1,5},{2,6},{3,7},{4,0},{5,1},{6,2},{7,3},{8,12},{9,13},{10,... | collective-permute-start | bytes 3145736 | tf_op jit(solution)/shard_map/ppermute | solution.py:377
  714.4 16.5 %collective-permute-start.3 = (bf16[2,2,256,2048]{2,3,1,0:T(8,128)(2,1)}, bf16[2,2,256,2048]{2,3,1,0:T(8,128)(2,1)}, u32[]{:S(2)}, u32[]{:S(2)}) collective-permute-start(bf16[2,2,256,2048]{2,3,1,0:T(8,128)(2,1)} %bitcast.289), channel_id=1, source_target_pairs={{0,1},{1,0},{2,3},{3,2},{4,5},{5,4},{6,7},{7,6},{8,9},{9,8},{10,11... | collective-permute-start | bytes 12582920 | tf_op jit(solution)/shard_map/ppermute | solution.py:377
  721.2 16.6 %collective-permute-start.17 = (bf16[2,2,256,2048]{2,3,0,1:T(8,128)(2,1)}, bf16[2,2,256,2048]{2,3,0,1:T(8,128)(2,1)}, u32[]{:S(2)}, u32[]{:S(2)}) collective-permute-start(bf16[2,2,256,2048]{2,3,0,1:T(8,128)(2,1)} %pad_maximum_fusion), channel_id=1, source_target_pairs={{0,1},{1,0},{2,3},{3,2},{4,5},{5,4},{6,7},{7,6},{8,9},{9,8},{10,11... | collective-permute-start | bytes 12582920 | tf_op jit(solution)/shard_map/ppermute | solution.py:377
  728.3 246.9 %reduce-scatter.9.cloned.1.call-start = ((), (), s32[]{:S(2)}) async-start(), calls=%async_computation.13 | async-start | bytes 1310720 | tf_op jit(solution)/shard_map/reduce_scatter | solution.py:628
  805.4 46.3 %collective-permute-start.6 = (bf16[2,256,1024]{1,2,0:T(8,128)(2,1)}, bf16[2,256,1024]{1,2,0:T(8,128)(2,1)}, u32[]{:S(2)}, u32[]{:S(2)}) collective-permute-start(bf16[2,256,1024]{1,2,0:T(8,128)(2,1)} %dynamic-slice_bitcast_fusion.4), channel_id=1, source_target_pairs={{0,4},{1,5},{2,6},{3,7},{4,0},{5,1},{6,2},{7,3},{8,12},{9,13},{10,... | collective-permute-start | bytes 3145736 | tf_op jit(solution)/shard_map/ppermute | solution.py:377
  806.9 53.6 %collective-permute-start.4 = (bf16[2,256,1024]{1,2,0:T(8,128)(2,1)}, bf16[2,256,1024]{1,2,0:T(8,128)(2,1)}, u32[]{:S(2)}, u32[]{:S(2)}) collective-permute-start(bf16[2,256,1024]{1,2,0:T(8,128)(2,1)} %dynamic-slice_bitcast_fusion.5), channel_id=1, source_target_pairs={{0,2},{1,3},{2,0},{3,1},{4,6},{5,7},{6,4},{7,5},{8,10},{9,11},{10,... | collective-permute-start | bytes 3145736 | tf_op jit(solution)/shard_map/ppermute | solution.py:377
  807.5 23.6 %collective-permute-start.20 = (f32[2,2048]{1,0:T(2,128)S(1)}, f32[2,2048]{1,0:T(2,128)S(1)}, u32[]{:S(2)}, u32[]{:S(2)}) collective-permute-start(f32[2,2048]{1,0:T(2,128)S(1)} %fusion.120), channel_id=1, source_target_pairs={{0,4},{1,5},{2,6},{3,7},{4,0},{5,1},{6,2},{7,3},{8,12},{9,13},{10,... | collective-permute-start | bytes 49160 | tf_op jit(solution)/shard_map/ppermute | solution.py:377
  808.2 42.8 %collective-permute-start.31 = (f32[17,2048]{1,0:T(8,128)S(1)}, f32[17,2048]{1,0:T(8,128)S(1)}, u32[]{:S(2)}, u32[]{:S(2)}) collective-permute-start(f32[17,2048]{1,0:T(8,128)S(1)} %pad_maximum_fusion.9), channel_id=1, source_target_pairs={{0,1},{1,0},{2,3},{3,2},{4,5},{5,4},{6,7},{7,6},{8,9},{9,8},{10,11... | collective-permute-start | bytes 417800 | tf_op jit(solution)/shard_map/ppermute | solution.py:377
  851.0 64.2 %collective-permute-start.21 = (bf16[2,2,256,2048]{2,3,1,0:T(8,128)(2,1)}, bf16[2,2,256,2048]{2,3,1,0:T(8,128)(2,1)}, u32[]{:S(2)}, u32[]{:S(2)}) collective-permute-start(bf16[2,2,256,2048]{2,3,1,0:T(8,128)(2,1)} %bitcast.288), channel_id=1, source_target_pairs={{0,1},{1,0},{2,3},{3,2},{4,5},{5,4},{6,7},{7,6},{8,9},{9,8},{10,11... | collective-permute-start | bytes 12582920 | tf_op jit(solution)/shard_map/ppermute | solution.py:377
  854.1 19.8 %collective-permute-start.7 = (bf16[256,1024]{0,1:T(8,128)(2,1)}, bf16[256,1024]{0,1:T(8,128)(2,1)}, u32[]{:S(2)}, u32[]{:S(2)}) collective-permute-start(bf16[256,1024]{0,1:T(8,128)(2,1)} %dynamic-slice_bitcast_fusion.10), channel_id=1, source_target_pairs={{0,2},{1,3},{2,0},{3,1},{4,6},{5,7},{6,4},{7,5},{8,10},{9,11},{10,... | collective-permute-start | bytes 1572872 | tf_op jit(solution)/shard_map/ppermute | solution.py:377
  862.9 16.4 %collective-permute-start.5 = (bf16[256,1024]{0,1:T(8,128)(2,1)}, bf16[256,1024]{0,1:T(8,128)(2,1)}, u32[]{:S(2)}, u32[]{:S(2)}) collective-permute-start(bf16[256,1024]{0,1:T(8,128)(2,1)} %dynamic-slice_bitcast_fusion.11), channel_id=1, source_target_pairs={{0,4},{1,5},{2,6},{3,7},{4,0},{5,1},{6,2},{7,3},{8,12},{9,13},{10,... | collective-permute-start | bytes 1572872 | tf_op jit(solution)/shard_map/ppermute | solution.py:377
  873.8 117.1 %reduce-scatter.7.cloned.1.call-start = ((), (), s32[]{:S(2)}) async-start(), calls=%async_computation.12 | async-start | bytes 3932160 | tf_op jit(solution)/shard_map/reduce_scatter | solution.py:631
  876.8 20.6 %collective-permute-start.35 = (f32[17,2048]{1,0:T(8,128)S(1)}, f32[17,2048]{1,0:T(8,128)S(1)}, u32[]{:S(2)}, u32[]{:S(2)}) collective-permute-start(f32[17,2048]{1,0:T(8,128)S(1)} %add.348), channel_id=1, source_target_pairs={{0,16},{8,24},{16,0},{24,8},{1,17},{9,25},{17,1},{25,9},{2,18},{10... | collective-permute-start | bytes 417800 | tf_op jit(solution)/shard_map/ppermute | solution.py:377
  921.1 18.9 %collective-permute-start.24 = (bf16[2,256,1024]{1,2,0:T(8,128)(2,1)}, bf16[2,256,1024]{1,2,0:T(8,128)(2,1)}, u32[]{:S(2)}, u32[]{:S(2)}) collective-permute-start(bf16[2,256,1024]{1,2,0:T(8,128)(2,1)} %dynamic-slice_bitcast_fusion), channel_id=1, source_target_pairs={{0,4},{1,5},{2,6},{3,7},{4,0},{5,1},{6,2},{7,3},{8,12},{9,13},{10,... | collective-permute-start | bytes 3145736 | tf_op jit(solution)/shard_map/ppermute | solution.py:377
  924.5 22.0 %collective-permute-start.22 = (bf16[2,256,1024]{1,2,0:T(8,128)(2,1)}, bf16[2,256,1024]{1,2,0:T(8,128)(2,1)}, u32[]{:S(2)}, u32[]{:S(2)}) collective-permute-start(bf16[2,256,1024]{1,2,0:T(8,128)(2,1)} %dynamic-slice_bitcast_fusion.1), channel_id=1, source_target_pairs={{0,2},{1,3},{2,0},{3,1},{4,6},{5,7},{6,4},{7,5},{8,10},{9,11},{10,... | collective-permute-start | bytes 3145736 | tf_op jit(solution)/shard_map/ppermute | solution.py:377
  942.4 19.8 %collective-permute-start.25 = (bf16[256,1024]{0,1:T(8,128)(2,1)}, bf16[256,1024]{0,1:T(8,128)(2,1)}, u32[]{:S(2)}, u32[]{:S(2)}) collective-permute-start(bf16[256,1024]{0,1:T(8,128)(2,1)} %dynamic-slice_bitcast_fusion.6), channel_id=1, source_target_pairs={{0,2},{1,3},{2,0},{3,1},{4,6},{5,7},{6,4},{7,5},{8,10},{9,11},{10,... | collective-permute-start | bytes 1572872 | tf_op jit(solution)/shard_map/ppermute | solution.py:377
  949.2 14.2 %collective-permute-start.23 = (bf16[256,1024]{0,1:T(8,128)(2,1)}, bf16[256,1024]{0,1:T(8,128)(2,1)}, u32[]{:S(2)}, u32[]{:S(2)}) collective-permute-start(bf16[256,1024]{0,1:T(8,128)(2,1)} %dynamic-slice_bitcast_fusion.7), channel_id=1, source_target_pairs={{0,4},{1,5},{2,6},{3,7},{4,0},{5,1},{6,2},{7,3},{8,12},{9,13},{10,... | collective-permute-start | bytes 1572872 | tf_op jit(solution)/shard_map/ppermute | solution.py:377
  (124 other events, 1197.2 us)
Sparse Core Ops, SparseCore 0:
  9.9 57.0 all-gather.4
  69.0 54.5 all-gather.6
  159.7 55.1 all-gather.8
  216.6 54.3 all-gather.10
  317.6 110.7 reduce-scatter.10
  430.6 111.2 reduce-scatter.12
  594.9 111.0 reduce-scatter.16
  728.4 111.7 reduce-scatter.14
  873.9 29.6 reduce-scatter.8
  915.3 59.1 reduce-scatter.6

commit v2 on v1

v2 whole, which is shorter than its diff:
```python
import functools
import math

import jax
import jax.numpy as jnp
from jax import lax
from jax.experimental import pallas as pl
from jax.experimental.pallas import tpu as pltpu
from jax.sharding import PartitionSpec as P

HEAD_DIM = 128
EPS = 1e-05
NEG = -1e30
MIB = 1 << 20
BF = jnp.bfloat16
F32 = jnp.float32


def rms_scale(values):
    return lax.rsqrt(jnp.mean(values * values, axis=-1, keepdims=True) + EPS)


def dot_nn(a, b):
    return lax.dot_general(a, b, (((1,), (0,)), ((), ())), preferred_element_type=F32)


def dot_nt(a, b):
    return lax.dot_general(a, b, (((1,), (1,)), ((), ())), preferred_element_type=F32)


def dot_tn(a, b):
    return lax.dot_general(a, b, (((0,), (0,)), ((), ())), preferred_element_type=F32)


def partner(me, bit):
    return me + bit * (1 - 2 * ((me // bit) % 2))


def remote(src, dst, send_sem, recv_sem, target):
    return pltpu.make_async_remote_copy(
        src_ref=src,
        dst_ref=dst,
        send_sem=send_sem,
        recv_sem=recv_sem,
        device_id={"tensor": target},
        device_id_type=pl.DeviceIdType.MESH,
    )


def greet(targets):
    barrier = pltpu.get_barrier_semaphore()
    for t in targets:
        pl.semaphore_signal(
            barrier, inc=1, device_id={"tensor": t}, device_id_type=pl.DeviceIdType.MESH
        )
    pl.semaphore_wait(barrier, len(targets))


def attn_fwd_body(
    q_ref, k_ref, v_ref, sq_ref, sk_ref, o_ref, low_ref, lse_ref, own_ref, buf, send_sem, recv_sem, here_sem,
    *, block, heads, reach, size
):
    qb = pl.program_id(0)
    me = lax.axis_index("tensor")
    scale = 1.0 / math.sqrt(HEAD_DIM)
    cols_all = heads * HEAD_DIM

    @pl.when(qb == 0)
    def _():
        greet([lax.rem(me + t, size) for t in range(1, size)])

    seg_q = sq_ref[...]
    row = qb * block + lax.broadcasted_iota(jnp.int32, (block, block), 0)
    col0 = lax.broadcasted_iota(jnp.int32, (block, block), 1)
    qs = [q_ref[:, h * HEAD_DIM : (h + 1) * HEAD_DIM] for h in range(heads)]

    def step(kb, carry):
        rows = pl.ds(pl.multiple_of(kb * block, block), block)
        allowed = (seg_q == sk_ref[kb]) & (kb * block + col0 <= row)
        out = []
        for h in range(heads):
            m, l, acc = carry[h]
            cols = slice(h * HEAD_DIM, (h + 1) * HEAD_DIM)
            s = jnp.where(allowed, dot_nt(qs[h], k_ref[rows, cols]) * scale, NEG)
            m_new = jnp.maximum(m, jnp.max(s, axis=1, keepdims=True))
            p = jnp.exp(s - m_new)
            alpha = jnp.exp(m - m_new)
            l = alpha * l + jnp.sum(p, axis=1, keepdims=True)
            acc = alpha * acc + dot_nn(p.astype(BF), v_ref[rows, cols])
            out.append((m_new, l, acc))
        return tuple(out)

    init = tuple(
        (
            jnp.full((block, 1), NEG, F32),
            jnp.zeros((block, 1), F32),
            jnp.zeros((block, HEAD_DIM), F32),
        )
        for _ in range(heads)
    )
    final = lax.fori_loop(jnp.maximum(qb - reach, 0), qb + 1, step, init)
    for h in range(heads):
        m, l, acc = final[h]
        cols = slice(h * HEAD_DIM, (h + 1) * HEAD_DIM)
        out = acc / l
        o_ref[:, cols] = out
        low_ref[:, cols] = out.astype(BF)
        buf[qb, :, cols] = out.astype(BF)
        lse_ref[:, h : h + 1] = m + jnp.log(l)

    own = own_ref.shape[0]
    per = block // own

    def rows_of(dev):
        return buf.at[dev // per, pl.ds(pl.multiple_of((dev % per) * own, own), own)]

    def land(src):
        return own_ref.at[:, pl.ds(pl.multiple_of(src * cols_all, HEAD_DIM), cols_all)]

    def send(t):
        return remote(rows_of(t), land(me), send_sem.at[t], recv_sem.at[me], t)

    for j in range(per):
        dest = qb * per + j

        @pl.when(dest != me)
        def _():
            send(dest).start()

        @pl.when(dest == me)
        def _():
            pltpu.make_async_copy(rows_of(me), land(me), here_sem).start()

    @pl.when(qb == pl.num_programs(0) - 1)
    def _():
        pltpu.make_async_copy(rows_of(me), land(me), here_sem).wait()
        for t in range(1, size):
            other = lax.rem(me + t, size)
            send(other).wait_send()
            remote(
                rows_of(other), land(other), send_sem.at[other], recv_sem.at[other], other
            ).wait_recv()


def attn_fwd(q, k, v, seg_col, seg_rows, block, reach, size, cid):
    tokens, cols = q.shape
    heads = cols // HEAD_DIM
    nb = tokens // block
    full = lambda shape: pl.BlockSpec(shape, lambda i: (0,) * len(shape))
    rowed = lambda c: pl.BlockSpec((block, c), lambda i: (i, 0))
    return pl.pallas_call(
        functools.partial(attn_fwd_body, block=block, heads=heads, reach=reach, size=size),
        out_shape=(
            jax.ShapeDtypeStruct((tokens, cols), F32),
            jax.ShapeDtypeStruct((tokens, cols), BF),
            jax.ShapeDtypeStruct((tokens, heads), F32),
            jax.ShapeDtypeStruct((tokens // size, cols * size), BF),
        ),
        grid=(nb,),
        in_specs=[
            rowed(cols),
            full((tokens, cols)),
            full((tokens, cols)),
            rowed(1),
            full((nb, 1, block)),
        ],
        out_specs=[rowed(cols), rowed(cols), rowed(heads), pl.BlockSpec(memory_space=pl.ANY)],
        scratch_shapes=[
            pltpu.VMEM((nb, block, cols), BF),
            pltpu.SemaphoreType.DMA((size,)),
            pltpu.SemaphoreType.DMA((size,)),
            pltpu.SemaphoreType.DMA,
        ],
        compiler_params=pltpu.CompilerParams(
            vmem_limit_bytes=32 * MIB, collective_id=cid, has_side_effects=True
        ),
        cost_estimate=pl.CostEstimate(
            flops=10**8, bytes_accessed=4 * MIB, transcendentals=10**5
        ),
        name="attn_fwd",
    )(q, k, v, seg_col, seg_rows)


def attn_bwd_body(
    lo_ref, q_ref, k_ref, v_ref, do_ref, o_ref, lse_ref, sq_ref, sk_ref, dq_ref, dk_ref, dv_ref, *, block, heads
):
    qb = pl.program_id(0)
    scale = 1.0 / math.sqrt(HEAD_DIM)

    @pl.when(qb == 0)
    def _():
        dk_ref[...] = jnp.zeros_like(dk_ref)
        dv_ref[...] = jnp.zeros_like(dv_ref)

    seg_q = sq_ref[...]
    row = qb * block + lax.broadcasted_iota(jnp.int32, (block, block), 0)
    col0 = lax.broadcasted_iota(jnp.int32, (block, block), 1)
    hc = [slice(h * HEAD_DIM, (h + 1) * HEAD_DIM) for h in range(heads)]
    qs = [q_ref[:, c] for c in hc]
    dos = [do_ref[:, c] for c in hc]
    lse = [lse_ref[:, h : h + 1] for h in range(heads)]
    dsum = [
        jnp.sum(dos[h].astype(F32) * o_ref[:, hc[h]], axis=1, keepdims=True) for h in range(heads)
    ]

    def step(kb, carry):
        rows = pl.ds(pl.multiple_of(kb * block, block), block)
        allowed = (seg_q == sk_ref[kb]) & (kb * block + col0 <= row)
        out = []
        for h in range(heads):
            k_blk = k_ref[rows, hc[h]]
            s = jnp.where(allowed, dot_nt(qs[h], k_blk) * scale, NEG)
            p = jnp.exp(s - lse[h])
            dp = dot_nt(dos[h], v_ref[rows, hc[h]])
            ds = (p * (dp - dsum[h])).astype(BF)
            dv_ref[rows, hc[h]] += dot_tn(p.astype(BF), dos[h])
            dk_ref[rows, hc[h]] += dot_tn(ds, qs[h]) * scale
            out.append(carry[h] + dot_nn(ds, k_blk))
        return tuple(out)

    init = tuple(jnp.zeros((block, HEAD_DIM), F32) for _ in range(heads))
    final = lax.fori_loop(lo_ref[qb], qb + 1, step, init)
    for h in range(heads):
        dq_ref[:, hc[h]] = final[h] * scale


def attn_bwd(lo, q, k, v, do, o, lse, seg_col, seg_rows, block):
    tokens, cols = q.shape
    heads = cols // HEAD_DIM
    nb = tokens // block
    full = lambda shape: pl.BlockSpec(shape, lambda i, lo: (0,) * len(shape))
    rowed = lambda c: pl.BlockSpec((block, c), lambda i, lo: (i, 0))
    return pl.pallas_call(
        functools.partial(attn_bwd_body, block=block, heads=heads),
        out_shape=tuple(jax.ShapeDtypeStruct((tokens, cols), F32) for _ in range(3)),
        grid_spec=pltpu.PrefetchScalarGridSpec(
            num_scalar_prefetch=1,
            grid=(nb,),
            in_specs=[
                rowed(cols),
                full((tokens, cols)),
                full((tokens, cols)),
                rowed(cols),
                rowed(cols),
                rowed(heads),
                rowed(1),
                full((nb, 1, block)),
            ],
            out_specs=[rowed(cols), full((tokens, cols)), full((tokens, cols))],
        ),
        compiler_params=pltpu.CompilerParams(vmem_limit_bytes=40 * MIB),
        cost_estimate=pl.CostEstimate(
            flops=10**8, bytes_accessed=4 * MIB, transcendentals=10**5
        ),
        name="attn_bwd",
    )(lo, q, k, v, do, o, lse, seg_col, seg_rows)


def expert_body(*refs, first, rows_blk, parts):
    lead = first == 0
    if lead:
        x_hbm, g_hbm, gates_ref, wg_ref, wu_ref, wd_ref = refs[:6]
        dgu_ref, ga_ref, wcat, dots_ref, grads_ref, xt_hbm = refs[6:12]
        x_v, xt_v, g_v, sem_x, sem_t, sem_g = refs[12:]
    else:
        x_hbm, g_hbm, gates_ref, wg_ref, wu_ref, wd_ref, xt_hbm = refs[:7]
        dgu_ref, ga_ref, wcat, dots_ref, grads_ref = refs[10:15]
        x_v, xt_v, g_v, sem_x, sem_t, sem_g = refs[15:]
    p = pl.program_id(0)
    tokens, width = x_v.shape
    nblk = tokens // rows_blk
    hid = wg_ref.shape[2]
    experts = gates_ref.shape[1]
    ds = width // parts

    if lead:
        t_copy = pltpu.make_async_copy(xt_v, xt_hbm, sem_t)
    else:
        t_copy = pltpu.make_async_copy(xt_hbm, xt_v, sem_t)

    def copies(i):
        r = pl.ds(i * rows_blk, rows_blk)
        return (
            pltpu.make_async_copy(x_hbm.at[r], x_v.at[r], sem_x.at[i]),
            pltpu.make_async_copy(g_hbm.at[r], g_v.at[r], sem_g.at[i]),
        )

    @pl.when(p == 0)
    def _():
        for i in range(nblk):
            for c in copies(i):
                c.start()
        if not lead:
            t_copy.start()
        dots_ref[...] = jnp.zeros_like(dots_ref)

    wcat[:, 0:hid] = wg_ref[0]
    wcat[:, hid : 2 * hid] = wg_ref[1]
    wcat[:, 2 * hid : 3 * hid] = wu_ref[0]
    wcat[:, 3 * hid : 4 * hid] = wu_ref[1]
    lane = lax.broadcasted_iota(jnp.int32, (rows_blk, experts), 1)
    e0 = 2 * (first + p)

    def block(i, _):
        start = pl.multiple_of(i * rows_blk, rows_blk)
        r = pl.ds(start, rows_blk)

        @pl.when(p == 0)
        def _():
            for c in copies(i):
                c.wait()

        if lead:
            xt_v[:, r] = x_v[r, :].T
        gu = dot_nn(x_v[r, :], wcat[...])
        q = dot_nt(g_v[r, :], wd_ref[...])
        gate_rows = gates_ref[r, :]
        dots = dots_ref[r, :]
        for j in range(2):
            pre = gu[:, j * hid : (j + 1) * hid]
            up = gu[:, (2 + j) * hid : (3 + j) * hid]
            back = q[:, j * hid : (j + 1) * hid]
            here = lane == e0 + j
            gate = jnp.sum(jnp.where(here, gate_rows, 0.0), axis=1, keepdims=True)
            sig = jax.nn.sigmoid(pre)
            silu = pre * sig
            act = silu * up
            dot = jnp.sum(act * back, axis=1, keepdims=True)
            dots = dots + jnp.where(here, dot, 0.0)
            scaled = gate * back
            d_up = scaled * silu
            d_gate = scaled * up * (sig + silu * (1.0 - sig))
            dgu_ref[r, j * hid : (j + 1) * hid] = d_gate.astype(BF)
            dgu_ref[r, (2 + j) * hid : (3 + j) * hid] = d_up.astype(BF)
            ga_ref[r, j * hid : (j + 1) * hid] = (gate * act).astype(BF)
        dots_ref[r, :] = dots
        return 0

    lax.fori_loop(0, nblk, block, 0)

    @pl.when(p == 0)
    def _():
        if lead:
            t_copy.start()
        else:
            t_copy.wait()

    for s in range(parts):
        gd = dot_tn(ga_ref[...], g_v[:, s * ds : (s + 1) * ds]).astype(BF)
        gw = dot_nn(xt_v[s * ds : (s + 1) * ds, :], dgu_ref[...]).astype(BF)
        for j in range(2):
            grads_ref[s, 3 * j] = gw[:, j * hid : (j + 1) * hid]
            grads_ref[s, 3 * j + 1] = gw[:, (2 + j) * hid : (3 + j) * hid]
            for c in range(ds // hid):
                grads_ref[s, 3 * j + 2, c * hid : (c + 1) * hid, :] = gd[
                    j * hid : (j + 1) * hid, c * hid : (c + 1) * hid
                ]

    if lead:

        @pl.when(p == 0)
        def _():
            t_copy.wait()


def expert_chunk(x, g, gates, wg, wu, wd, carried, *, first, pairs, parts):
    tokens, width = x.shape
    experts, _, hid = wg.shape
    total = experts // 2
    rows_blk = 512
    nblk = tokens // rows_blk
    ds = width // parts
    lead = first == 0
    assert not lead or pairs == 1
    any_spec = pl.BlockSpec(memory_space=pl.ANY)
    colblk = lambda rows, c: pl.BlockSpec((rows, c), lambda p: (0, first + p))
    in_specs = [
        any_spec,
        any_spec,
        pl.BlockSpec((tokens, experts), lambda p: (0, 0)),
        pl.BlockSpec((2, width, hid), lambda p: (first + p, 0, 0)),
        pl.BlockSpec((2, width, hid), lambda p: (first + p, 0, 0)),
        pl.BlockSpec((2 * hid, width), lambda p: (first + p, 0)),
    ]
    out_shape = [
        jax.ShapeDtypeStruct((tokens, total * 4 * hid), BF),
        jax.ShapeDtypeStruct((tokens, total * 2 * hid), BF),
        jax.ShapeDtypeStruct((width, total * 4 * hid), BF),
        jax.ShapeDtypeStruct((tokens, experts), F32),
        jax.ShapeDtypeStruct((parts, pairs * 6, ds, hid), BF),
    ]
    out_specs = [
        colblk(tokens, 4 * hid),
        colblk(tokens, 2 * hid),
        colblk(width, 4 * hid),
        pl.BlockSpec((tokens, experts), lambda p: (0, 0)),
        pl.BlockSpec((parts, 6, ds, hid), lambda p: (0, p, 0, 0)),
    ]
    args = [x, g, gates, wg, wu, wd]
    alias = {}
    if lead:
        out_shape.append(jax.ShapeDtypeStruct((width, tokens), BF))
        out_specs.append(any_spec)
    else:
        xt, dgu, ga, wcat = carried
        args += [xt, dgu, ga, wcat]
        in_specs += [any_spec] * 4
        alias = {7: 0, 8: 1, 9: 2}
    return pl.pallas_call(
        functools.partial(expert_body, first=first, rows_blk=rows_blk, parts=parts),
        out_shape=tuple(out_shape),
        grid=(pairs,),
        in_specs=in_specs,
        out_specs=out_specs,
        scratch_shapes=[
            pltpu.VMEM((tokens, width), BF),
            pltpu.VMEM((width, tokens), BF),
            pltpu.VMEM((tokens, width), BF),
            pltpu.SemaphoreType.DMA((nblk,)),
            pltpu.SemaphoreType.DMA,
            pltpu.SemaphoreType.DMA((nblk,)),
        ],
        input_output_aliases=alias,
        compiler_params=pltpu.CompilerParams(vmem_limit_bytes=61 * MIB),
        cost_estimate=pl.CostEstimate(
            flops=10**9, bytes_accessed=4 * MIB, transcendentals=10**5
        ),
        name="expert_chunk",
    )(*args)


def matmul_scatter_body(
    l_hbm, r_hbm, out_ref, l_v, r_v, part, got1, got2, got3, sem_l, sem_r, send_sem, recv_sem,
    *, size, slices, nt
):
    me = lax.axis_index("tensor")
    tokens = l_v.shape[0]
    own = tokens // size
    sn = out_ref.shape[1] // slices
    mine = [(me // b) % 2 for b in (1, 2, 4)]
    group = 2

    def l_copy(i):
        r = pl.ds(i * own * group, own * group)
        return pltpu.make_async_copy(l_hbm.at[r], l_v.at[r], sem_l.at[i])

    def r_copy(s):
        c = pl.ds(s * sn, sn)
        if nt:
            return pltpu.make_async_copy(r_hbm.at[c], r_v.at[c], sem_r.at[s])
        return pltpu.make_async_copy(r_hbm.at[:, c], r_v.at[:, c], sem_r.at[s])

    r_copy(0).start()
    for i in range(size // group):
        l_copy(i).start()
    for s in range(1, slices):
        r_copy(s).start()
    greet([partner(me, b) for b in (1, 2, 4)])

    def hop(s, stage):
        a, b = (1, 2) if s % 2 == 0 else (2, 1)
        if stage == 0:
            src, dst, bit = part.at[s, 1 - mine[0]], got1.at[s], 1
        elif stage == 1:
            src, dst, bit = part.at[s, mine[0], pl.ds(2 * (1 - mine[a]), 2)], got2.at[s], 1 << a
        else:
            src, dst, bit = part.at[s, mine[0], 2 * mine[a] + 1 - mine[b]], got3.at[s], 1 << b
        return remote(src, dst, send_sem.at[stage, s], recv_sem.at[stage, s], partner(me, bit))

    def compute(s):
        r_copy(s).wait()

        def rows(i, _):
            if s == 0:
                l_copy(i).wait()
            r = pl.ds(pl.multiple_of(i * own * group, own * group), own * group)
            if nt:
                res = dot_nt(l_v[r, :], r_v[s * sn : (s + 1) * sn, :])
            else:
                res = dot_nn(l_v[r, :], r_v[:, s * sn : (s + 1) * sn])
            res = res.astype(BF)
            x, y = i % 2, i // 2
            pos = 2 * x + y if s % 2 == 0 else 2 * y + x
            for c in range(2):
                part[s, c, pos] = res[c * own : (c + 1) * own]
            return 0

        lax.fori_loop(0, size // group, rows, 0)
        hop(s, 0).start()

    def first(s):
        hop(s, 0).wait_recv()
        part[s, mine[0]] = (part[s, mine[0]].astype(F32) + got1[s].astype(F32)).astype(BF)
        hop(s, 1).start()

    def second(s):
        a = 1 if s % 2 == 0 else 2
        hop(s, 1).wait_recv()
        ix = pl.ds(2 * mine[a], 2)
        part[s, mine[0], ix] = (part[s, mine[0], ix].astype(F32) + got2[s].astype(F32)).astype(BF)
        hop(s, 2).start()

    def third(s):
        a, b = (1, 2) if s % 2 == 0 else (2, 1)
        hop(s, 2).wait_recv()
        out_ref[:, s * sn : (s + 1) * sn] = part[s, mine[0], 2 * mine[a] + mine[b]].astype(
            F32
        ) + got3[s].astype(F32)

    for t in range(slices + 5):
        if t < slices:
            compute(t)
        if 0 <= t - 1 < slices:
            first(t - 1)
        if 0 <= t - 3 < slices:
            second(t - 3)
        if 0 <= t - 5 < slices:
            third(t - 5)
    for s in range(slices):
        for stage in range(3):
            hop(s, stage).wait_send()


def matmul_scatter(left, right, size, cid, nt, name):
    tokens, depth = left.shape
    width = right.shape[0] if nt else right.shape[1]
    own = tokens // size
    if size != 8:
        part = (dot_nt if nt else dot_nn)(left, right).astype(BF)
        return lax.psum_scatter(part, "tensor", scatter_dimension=0, tiled=True).astype(F32)
    slices = 8
    sn = width // slices
    any_spec = pl.BlockSpec(memory_space=pl.ANY)
    return pl.pallas_call(
        functools.partial(matmul_scatter_body, size=size, slices=slices, nt=nt),
        out_shape=jax.ShapeDtypeStruct((own, width), F32),
        in_specs=[any_spec, any_spec],
        out_specs=pl.BlockSpec(memory_space=pltpu.VMEM),
        scratch_shapes=[
            pltpu.VMEM(left.shape, BF),
            pltpu.VMEM(right.shape, BF),
            pltpu.VMEM((slices, 2, size // 2, own, sn), BF),
            pltpu.VMEM((slices, size // 2, own, sn), BF),
            pltpu.VMEM((slices, size // 4, own, sn), BF),
            pltpu.VMEM((slices, own, sn), BF),
            pltpu.SemaphoreType.DMA((size // 2,)),
            pltpu.SemaphoreType.DMA((slices,)),
            pltpu.SemaphoreType.DMA((3, slices)),
            pltpu.SemaphoreType.DMA((3, slices)),
        ],
        compiler_params=pltpu.CompilerParams(
            vmem_limit_bytes=60 * MIB, collective_id=cid, has_side_effects=True
        ),
        cost_estimate=pl.CostEstimate(
            flops=10**9, bytes_accessed=4 * MIB, transcendentals=0
        ),
        name=name,
    )(left, right)


def gather_body(x_ref, out_ref, send_sem, recv_sem, here_sem):
    me = lax.axis_index("tensor")
    own = x_ref.shape[0]
    half = own // 2
    pc, px, py = (partner(me, b) for b in (1, 2, 4))
    diag = partner(px, 4)
    greet([pc, px, py])

    def piece(dev, a, n):
        return out_ref.at[pl.ds(pl.multiple_of(dev * own + a, half), n)]

    here = pltpu.make_async_copy(x_ref, piece(me, 0, own), here_sem)
    here.start()
    plan = [
        (me, 0, half, px),
        (me, half, half, py),
        (me, half, half, px),
        (me, 0, half, py),
        (me, 0, own, pc),
        (px, 0, half, py),
        (py, half, half, px),
        (px, 0, half, pc),
        (py, half, half, pc),
        (px, half, half, pc),
        (py, 0, half, pc),
        (diag, 0, half, pc),
        (diag, half, half, pc),
    ]

    def copy(k):
        dev, a, n, target = plan[k]
        src = x_ref.at[pl.ds(a, n)] if k < 5 else piece(dev, a, n)
        return remote(src, piece(dev, a, n), send_sem.at[k], recv_sem.at[k], target)

    def arrived(k):
        dev, a, n, target = plan[k]
        bit_dev = {0: px, 1: py, 2: px, 3: py, 4: pc, 5: diag, 6: diag}
        if k in bit_dev:
            src = bit_dev[k]
        else:
            src = partner(dev, 1)
        return remote(piece(src, a, n), piece(src, a, n), send_sem.at[k], recv_sem.at[k], target)

    for k in range(5):
        copy(k).start()
    arrived(0).wait_recv()
    copy(5).start()
    copy(7).start()
    arrived(1).wait_recv()
    copy(6).start()
    copy(8).start()
    arrived(2).wait_recv()
    copy(9).start()
    arrived(3).wait_recv()
    copy(10).start()
    arrived(5).wait_recv()
    copy(11).start()
    arrived(6).wait_recv()
    copy(12).start()
    for k in (4, 7, 8, 9, 10, 11, 12):
        arrived(k).wait_recv()
    for k in range(13):
        copy(k).wait_send()
    here.wait()


def gather_all(value, size, cid, name):
    own, cols = value.shape
    if size != 8:
        return lax.all_gather(value, "tensor", axis=0, tiled=True)
    any_spec = pl.BlockSpec(memory_space=pl.ANY)
    return pl.pallas_call(
        gather_body,
        out_shape=jax.ShapeDtypeStruct((own * size, cols), value.dtype),
        in_specs=[any_spec],
        out_specs=any_spec,
        scratch_shapes=[
            pltpu.SemaphoreType.DMA((13,)),
            pltpu.SemaphoreType.DMA((13,)),
            pltpu.SemaphoreType.DMA,
        ],
        compiler_params=pltpu.CompilerParams(collective_id=cid, has_side_effects=True),
        cost_estimate=pl.CostEstimate(flops=0, bytes_accessed=4 * MIB, transcendentals=0),
        name=name,
    )(value)


def swap(value, axis, size, bit):
    return lax.ppermute(value, axis, [(i, i ^ bit) for i in range(size)])


def sum_all(value, axis, size):
    bit = 1
    while bit < size:
        value = value + swap(value, axis, size, bit)
        bit *= 2
    return value


def bits_of(size):
    return [1 << b for b in range(size.bit_length() - 1)]


def half_swap(values):
    pieces = []
    half = HEAD_DIM // 2
    for h in range(values.shape[1] // HEAD_DIM):
        base = h * HEAD_DIM
        pieces += [values[:, base + half : base + HEAD_DIM], values[:, base : base + half]]
    return jnp.concatenate(pieces, axis=1)


def per_device(
    block_input, segments, routes, w_query, w_key, w_value, w_output, attn_gain, query_gain, key_gain,
    moe_gain, router, w_gate, w_up, w_down, cotangent, *, n_dp, n_tensor
):
    own_rows, model_width = block_input.shape
    local_cols = w_query.shape[1]
    local_heads = local_cols // HEAD_DIM
    token_count = segments.shape[0] * segments.shape[1]
    experts = router.shape[1]
    top_count = routes.shape[1]
    hid = w_gate.shape[2]
    capacity = 5 * token_count * top_count // (4 * experts)
    me = lax.axis_index("tensor")
    rank_start = me * own_rows
    col_start = me * local_cols
    block = 256

    full_input = lax.all_gather(block_input, "tensor", axis=0, tiled=True)

    seg = segments.reshape(token_count)
    values16 = jnp.arange(16, dtype=jnp.int32)
    below = jnp.sum((seg[None, :] < values16[:, None]).astype(jnp.int32), axis=1)
    doc_start = jnp.sum(
        jnp.where(seg[:, None] == values16[None, :], below[None, :], 0), axis=1
    )
    positions = jnp.arange(token_count, dtype=jnp.int32) - doc_start
    half = HEAD_DIM // 2
    frequency = jnp.exp(
        jnp.arange(half, dtype=F32) * (-2.0 * math.log(10000.0) / HEAD_DIM)
    )
    angles = positions.astype(F32)[:, None] * frequency[None, :]
    cosine, sine = jnp.cos(angles), jnp.sin(angles)
    cos_all = jnp.concatenate([cosine] * (2 * local_heads), axis=1)
    sin_all = jnp.concatenate([-sine, sine] * local_heads, axis=1)
    cos_all, sin_all = lax.optimization_barrier((cos_all, sin_all))
    lo_block = doc_start[::block] // block
    seg_col = seg[:, None]
    seg_rows = seg.reshape(token_count // block, 1, block)

    expert_ids = jnp.arange(experts, dtype=jnp.int32)
    routed = jnp.sum(
        (routes[:, :, None] == expert_ids[None, None, :]).astype(F32), axis=1
    )
    tri = (
        jnp.arange(block, dtype=jnp.int32)[:, None] > jnp.arange(block, dtype=jnp.int32)[None, :]
    ).astype(BF)
    nb = token_count // block
    routed_b = routed.reshape(nb, block, experts)
    within = jnp.einsum("ij,bje->bie", tri, routed_b.astype(BF), preferred_element_type=F32)
    sums = jnp.sum(routed_b, axis=1)
    before = jnp.sum(
        jnp.where(
            (jnp.arange(nb)[:, None] > jnp.arange(nb)[None, :])[:, :, None], sums[None, :, :], 0.0
        ),
        axis=1,
    )
    place = within + before[:, None, :]
    mask = (routed_b * (place < capacity).astype(F32)).reshape(token_count, experts)

    w_qkv = jnp.concatenate([w_query, w_key, w_value], axis=1)
    full_input, cos_all, sin_all, mask, w_qkv, lo_block, seg_col, seg_rows = lax.optimization_barrier(
        (full_input, cos_all, sin_all, mask, w_qkv, lo_block, seg_col, seg_rows)
    )
    full_input, w_output_in = lax.optimization_barrier((full_input, w_output))
    full_wo = lax.all_gather(w_output_in, "tensor", axis=0, tiled=True)

    input_wide = full_input.astype(F32)
    scale_one = rms_scale(input_wide)
    normed = (input_wide * scale_one * attn_gain).astype(BF)
    qkv = dot_nn(normed, w_qkv)
    query_raw = qkv[:, :local_cols]
    key_raw = qkv[:, local_cols : 2 * local_cols]
    value_low = qkv[:, 2 * local_cols :].astype(BF)
    squares = jnp.stack(
        [jnp.sum(query_raw * query_raw, axis=1), jnp.sum(key_raw * key_raw, axis=1)]
    )
    squares = sum_all(squares, "tensor", n_tensor)
    scales = lax.rsqrt(squares / model_width + EPS)
    query_rs = scales[0][:, None]
    key_rs = scales[1][:, None]
    query_unit = query_raw * query_rs
    key_unit = key_raw * key_rs
    q_n = query_unit * query_gain
    k_n = key_unit * key_gain
    queries = (q_n * cos_all + half_swap(q_n) * sin_all).astype(BF)
    keys_rot = (k_n * cos_all + half_swap(k_n) * sin_all).astype(BF)
    reach = min(1024 // block, token_count // block)
    attended, attn_low, lse, own_attn = attn_fwd(
        queries, keys_rot, value_low, seg_col, seg_rows, block, reach, n_tensor, 0
    )

    own_attn, cot_in = lax.optimization_barrier((own_attn, cotangent))
    full_cot = lax.all_gather(cot_in, "tensor", axis=0, tiled=True)

    input_own = block_input.astype(F32)
    residual = input_own + dot_nn(own_attn, full_wo)
    scale_two = rms_scale(residual)
    own_moe_in = (residual * scale_two * moe_gain).astype(BF)
    moe_in = gather_all(own_moe_in, n_tensor, 1, "gather_moe")

    router_probs = jax.nn.softmax(dot_nn(moe_in, router), axis=-1)
    gates = router_probs * mask
    wd_flat = w_down.reshape(experts * hid, model_width)
    pairs_total = experts // 2
    chunks = (1, 4, 3)
    dots = None
    reduced = []
    carried = None
    first = 0
    for count in chunks:
        res = expert_chunk(
            moe_in, full_cot, gates, w_gate, w_up, wd_flat, carried,
            first=first, pairs=count, parts=n_dp,
        )
        dgu, ga, wcat, dot_c, grads = res[:5]
        xt = res[5] if first == 0 else carried[0]
        if len(reduced) == 1:
            reduced[0], dgu = lax.optimization_barrier((reduced[0], dgu))
        carried = (xt, dgu, ga, wcat)
        dots = dot_c if dots is None else dots + dot_c
        if first + count < pairs_total:
            reduced.append(lax.psum_scatter(grads, "dp", scatter_dimension=0, tiled=False))
        first += count
    moe_back = matmul_scatter(dgu, wcat, n_tensor, 2, True, "moe_back")

    own_dots = jnp.sum(
        lax.all_to_all(dots.reshape(n_tensor, own_rows, experts), "tensor", 0, 0), axis=0
    )
    own_mask = lax.dynamic_slice_in_dim(mask, rank_start, own_rows, 0)
    own_probs = lax.dynamic_slice_in_dim(router_probs, rank_start, own_rows, 0)
    prob_grads = own_dots * own_mask
    own_logit = (
        own_probs * (prob_grads - jnp.sum(own_probs * prob_grads, axis=1, keepdims=True))
    ).astype(BF)
    router_grad = dot_tn(own_logit, own_moe_in)
    moe_grad = moe_back + dot_nt(own_logit, router)

    unit_two = residual * scale_two
    moe_gain_grad = jnp.sum(moe_grad * unit_two, axis=0)
    scaled_two = moe_grad * moe_gain
    residual_grad = cotangent.astype(F32) + scale_two * (
        scaled_two - unit_two * jnp.mean(scaled_two * unit_two, axis=1, keepdims=True)
    )
    residual_low = gather_all(residual_grad.astype(BF), n_tensor, 3, "gather_residual")
    output_grad = dot_tn(residual_low, attn_low).astype(BF)
    heads_grad = dot_nt(residual_low, w_output).astype(BF)

    dq_rot, dk_rot, dv = attn_bwd(
        lo_block, queries, keys_rot, value_low, heads_grad, attended, lse, seg_col, seg_rows, block
    )
    reduced[1], grads, dq_rot = lax.optimization_barrier((reduced[1], grads, dq_rot))
    reduced.append(lax.psum_scatter(grads, "dp", scatter_dimension=0, tiled=False))
    query_norm_grad = dq_rot * cos_all - half_swap(dq_rot) * sin_all
    key_norm_grad = dk_rot * cos_all - half_swap(dk_rot) * sin_all
    query_gain_grad = jnp.sum(query_norm_grad * query_unit, axis=0)
    key_gain_grad = jnp.sum(key_norm_grad * key_unit, axis=0)
    query_scaled = query_norm_grad * query_gain
    key_scaled = key_norm_grad * key_gain
    inner = jnp.stack(
        [jnp.sum(query_scaled * query_unit, axis=1), jnp.sum(key_scaled * key_unit, axis=1)]
    )
    inner = sum_all(inner, "tensor", n_tensor) / model_width
    query_grad_low = (query_rs * (query_scaled - query_unit * inner[0][:, None])).astype(BF)
    key_grad_low = (key_rs * (key_scaled - key_unit * inner[1][:, None])).astype(BF)
    qkv_grad = jnp.concatenate([query_grad_low, key_grad_low, dv.astype(BF)], axis=1)
    qkv_w_grad = dot_tn(normed, qkv_grad).astype(BF)
    normed_grad = matmul_scatter(qkv_grad, w_qkv, n_tensor, 4, True, "normed_back")
    moe_out = matmul_scatter(ga, wd_flat, n_tensor, 5, False, "moe_out")
    block_output = (residual + moe_out).astype(BF)
    scale_own = rms_scale(input_own)
    unit_one = input_own * scale_own
    attn_gain_grad = jnp.sum(normed_grad * unit_one, axis=0)
    scaled_one = normed_grad * attn_gain
    grad_input = residual_grad + scale_own * (
        scaled_one - unit_one * jnp.mean(scaled_one * unit_one, axis=1, keepdims=True)
    )

    proj_grad = jnp.concatenate([qkv_w_grad, output_grad], axis=1)
    reduced[2], proj_grad, block_output, grad_input = lax.optimization_barrier(
        (reduced[2], proj_grad, block_output, grad_input)
    )
    qkv_red = lax.psum_scatter(proj_grad, "dp", scatter_dimension=0, tiled=True).astype(F32)
    wo_red = qkv_red[:, 3 * local_cols :].T
    early = jnp.concatenate([router_grad, moe_gain_grad[None, :]], axis=0)
    early = sum_all(sum_all(early, "tensor", n_tensor), "dp", n_dp)
    gains = jnp.stack(
        [
            attn_gain_grad,
            lax.dynamic_update_slice_in_dim(
                jnp.zeros((model_width,), F32), query_gain_grad, col_start, 0
            ),
            lax.dynamic_update_slice_in_dim(
                jnp.zeros((model_width,), F32), key_gain_grad, col_start, 0
            ),
        ]
    )
    gains = sum_all(sum_all(gains, "tensor", n_tensor), "dp", n_dp)

    ds = model_width // n_dp
    gate_out, up_out, down_out = [], [], []
    for r, count in zip(reduced, chunks):
        r = r.reshape(2 * count, 3, ds, hid)
        gate_out.append(r[:, 0])
        up_out.append(r[:, 1])
        down = r[:, 2].reshape(2 * count, ds // hid, hid, hid)
        down_out.append(down.transpose(0, 2, 1, 3).reshape(2 * count, hid, ds))
    grad_gate = jnp.concatenate(gate_out, axis=0).astype(F32)
    grad_up = jnp.concatenate(up_out, axis=0).astype(F32)
    grad_down = jnp.concatenate(down_out, axis=0).astype(F32)
    return (
        block_output,
        grad_input,
        qkv_red[:, :local_cols],
        qkv_red[:, local_cols : 2 * local_cols],
        qkv_red[:, 2 * local_cols : 3 * local_cols],
        wo_red,
        gains[0],
        gains[1],
        gains[2],
        early[experts],
        early[:experts].T,
        grad_gate,
        grad_up,
        grad_down,
    )


def solution(mesh):
    rows = P(("dp", "tensor"), None)
    cols = P(None, "tensor")
    wide = P(None, None, "tensor")
    placed = (
        rows, P("dp", None), P("dp", None), cols, cols, cols, P("tensor", None), P(), P("tensor"), P("tensor"),
        P(), P(), wide, wide, P(None, "tensor", None), rows,
    )
    outs = (
        rows, rows, P("dp", "tensor"), P("dp", "tensor"), P("dp", "tensor"), P("tensor", "dp"), P(), P(), P(), P(),
        P(), P(None, "dp", "tensor"), P(None, "dp", "tensor"), P(None, "tensor", "dp"),
    )
    return jax.shard_map(
        functools.partial(
            per_device, n_dp=mesh.shape["dp"], n_tensor=mesh.shape["tensor"]
        ),
        mesh=mesh,
        in_specs=placed,
        out_specs=outs,
        check_vma=False,
    )
```

time: 1010 us -> 802 us (0.79)
  Pallas kernels: 272 us -> 476 us
  local copies, waits for them, and re-layouts: 172 us -> 47.6 us
  matrix products: 161 us -> 47.2 us
  waiting for transfers between devices: 238 us -> 125 us
  other arithmetic: 100 us -> 63.6 us
  starting transfers between devices: 40 us -> 20.7 us
    pallas_call x2 -> x6, Pallas kernels: 101 us -> 309 us  [the longest x3 168 us: matmul_scatter(): pl.pallas_call(functools.partial(matmul_scatter_body, size=size, slices=s...]
    dot_general x11 -> x3, matrix products: 126 us -> 19.3 us  [dot_nn(): lax.dot_general(a, b, (((1,), (0,)), ((), ())), preferred_element_type=F32)]
    all_gather x1 -> x0, waiting for transfers between devices: 52.2 us -> none  [per_device(): moe_in = lax.all_gather(own_moe_in, 'tensor', axis=0, tiled=True)]
    dynamic_slice x6 -> x0, local copies, waits for them, and re-layouts: 40 us -> none  [the longest x3 21.3 us: halve(): keep = lax.dynamic_index_in_dim(y, mine, axis, keepdims=False)]
    all_gather x1, waiting for transfers between devices: 35.4 us -> 0.01 us  [per_device(): full_cot = lax.all_gather(cot_in, 'tensor', axis=0, tiled=True)]
    convert_element_type x18 -> x2, other arithmetic: 32 us -> 1.94 us  [the longest x1 1.66 us: per_device(): residual_grad.astype(BF)]
    unnamed x226 -> x118, local copies, waits for them, and re-layouts: 42.5 us -> 20.6 us
    reduce_scatter x4 -> x3, waiting for transfers between devices: 0.03 us -> 19.1 us  [per_device(): lax.psum_scatter(grads, 'dp', scatter_dimension=0, tiled=False)]
  transfers between devices with their start and end apart: 48 -> 24, of which waited for: 18 -> 15; matrix products, arithmetic and copies ran while one was open for 40% -> 17% of each run, Pallas kernels for 24% -> 57%
where the time goes in v2:
time: 802 us; the launch traced here: 796 us
  Pallas kernels  476 us (59%)
  waiting for transfers between devices  125 us (16%)
  other arithmetic  63.6 us (8%)
  local copies, waits for them, and re-layouts  47.6 us (6%)
  matrix products  47.2 us (6%)
  starting transfers between devices  20.7 us (3%)
  between operations  15.4 us (2%)
    pallas_call x3, Pallas kernels, matmul_scatter(): pl.pallas_call(functools.partial(matmul_scatter_body, size=size, slices=s...  168 us
    pallas_call x3, Pallas kernels, expert_chunk(): pl.pallas_call(functools.partial(expert_body, first=first, rows_blk=rows_...  145 us
    pallas_call x2, Pallas kernels, gather_all(): pl.pallas_call(gather_body, out_shape=jax.ShapeDtypeStruct((own * size, c...  108 us
    ppermute x16, waiting for transfers between devices, swap(): return lax.ppermute(value, axis, [(i, i ^ bit) for i in range(size)])  58.5 us
    all_gather x1, waiting for transfers between devices, per_device(): full_input = lax.all_gather(block_input, 'tensor', axis=0, tiled=True)  45.5 us
    pallas_call x1, Pallas kernels, attn_fwd(): pl.pallas_call(functools.partial(attn_fwd_body, block=block, heads=heads,...  32.7 us
    pallas_call x1, Pallas kernels, attn_bwd(): pl.pallas_call(functools.partial(attn_bwd_body, block=block, heads=heads)...  22.4 us
    unnamed x118, local copies, waits for them, and re-layouts  20.6 us
  transfers between devices with their start and end apart: 24, of which 15 were waited for; matrix products, arithmetic and copies ran while one was open for 17% of the time, Pallas kernels for 57%

profile of v2, /device:TPU:0, one launch (start us, length us, event | category | flops | bytes accessed | tf_op | source)
XLA Modules:
  0.0 796.2 jit_solution(306022122748014008)
XLA Ops:
  9.7 3.7 fusion.28
  13.5 3.7 pad_maximum_fusion.3
  21.6 45.5 %all-gather.4.cloned.1.call-done = bf16[2048,2048]{1,0:T(8,128)(2,1)} async-done(((bf16[256,2048]{1,0:T(8,128)(2,1)}), bf16[2048,2048]{1,0:T(8,128)(2,1)}) %all-gather.4.cloned.1.call-update) | async-done | bytes 8388624 | tf_op jit(solution)/shard_map/all_gather | solution.py:690
  67.7 5.2 fusion
  73.4 7.3 fusion.7
  98.9 32.7 %attn_fwd.1 = (f32[2048,256]{1,0:T(8,128)S(1)}, bf16[2048,256]{1,0:T(8,128)(2,1)S(1)}, f32[2048,2]{1,0:T(8,128)S(1)}, bf16[256,2048]{1,0:T(8,128)(2,1)S(1)}) custom-call(bf16[2048,256]{1,0:T(8,128)(2,1)S(1)} %get-tuple-element.197.q_ref, bf16[2048,256]{1,0:T(8,128)(2,1)S(1)} %get-tuple-element.196.k_ref, bf16[2048,256]{1,0:T(8,128)(2,1)S(1)} %slice.231.v_ref, ...), custom_call_target="tpu_custom_call" | custom-call | flops 100000000 | bytes 4194304 | tf_op jit(solution)/shard_map/attn_fwd/pallas_call | solution.py:151
  136.1 6.4 multiply_reduce_fusion.6
  143.9 69.1 %gather_moe.1.refs_0_ = bf16[2048,2048]{1,0:T(8,128)(2,1)} custom-call(bf16[256,2048]{1,0:T(8,128)(2,1)} %multiply_convert_fusion.2.x_ref), custom_call_target="tpu_custom_call" | custom-call | bytes 4194304 | tf_op jit(solution)/shard_map/gather_moe/pallas_call | solution.py:632
  213.1 5.7 fusion.52
  221.9 3.1 fusion.39
  225.0 23.3 %expert_chunk.3 = (bf16[2048,4096]{1,0:T(8,128)(2,1)}, bf16[2048,2048]{1,0:T(8,128)(2,1)}, bf16[2048,4096]{1,0:T(8,128)(2,1)}, f32[2048,16]{1,0:T(8,128)}, bf16[...) custom-call(bf16[2048,2048]{1,0:T(8,128)(2,1)} %gather_moe.1.refs_0_, ...), custom_call_target="tpu_custom_call" | custom-call | flops 1000000000 | bytes 4194304 | tf_op jit(solution)/shard_map/expert_chunk/pallas_call | solution.py:409
  248.4 68.7 %expert_chunk.4 = (bf16[2048,4096]{1,0:T(8,128)(2,1)}, bf16[2048,2048]{1,0:T(8,128)(2,1)}, bf16[2048,4096]{1,0:T(8,128)(2,1)}, f32[2048,16]{1,0:T(8,128)}, bf16[4,24,512,128]{3,2,1,0:T(8,128)(2,1)}) custom-call(bf16[2048,2048]{1,0:T(8,128)(2,1)} %gather_moe.1.refs_0_, ...), custom_call_target="tpu_custom_call", output_to_operand_aliasing={{0}: (7, {}), {1}: (8, {}), {2}: (9, {})} | custom-call | flops 1000000000 | bytes 4194304 | tf_op jit(solution)/shard_map/expert_chunk/pallas_call | solution.py:409
  317.2 53.1 %expert_chunk.5 = (bf16[2048,4096]{1,0:T(8,128)(2,1)}, bf16[2048,2048]{1,0:T(8,128)(2,1)}, bf16[2048,4096]{1,0:T(8,128)(2,1)}, f32[2048,16]{1,0:T(8,128)}, bf16[4,18,512,128]{3,2,1,0:T(8,128)(2,1)}) custom-call(bf16[2048,2048]{1,0:T(8,128)(2,1)} %gather_moe.1.refs_0_, ...), custom_call_target="tpu_custom_call", output_to_operand_aliasing={{0}: (7, {}), {1}: (8, {}), {2}: (9, {})} | custom-call | flops 1000000000 | bytes 4194304 | tf_op jit(solution)/shard_map/expert_chunk/pallas_call | solution.py:409
  375.5 3.4 all-to-all-start
  378.9 67.8 %moe_back.1 = f32[256,2048]{1,0:T(8,128)} custom-call(bf16[2048,4096]{1,0:T(8,128)(2,1)} %get-tuple-element.86.l_hbm, bf16[2048,4096]{1,0:T(8,128)(2,1)} %get-tuple-element.87.r_hbm), custom_call_target="tpu_custom_call" | custom-call | flops 1000000000 | bytes 4194304 | tf_op jit(solution)/shard_map/moe_back/pallas_call | solution.py:534
  453.6 38.8 %gather_residual.1 = bf16[2048,2048]{1,0:T(8,128)(2,1)} custom-call(bf16[256,2048]{1,0:T(8,128)(2,1)} %fusion.36.x_ref), custom_call_target="tpu_custom_call" | custom-call | bytes 4194304 | tf_op jit(solution)/shard_map/gather_residual/pallas_call | solution.py:632
  492.4 6.1 convolution_convert_fusion.2.do_ref
  498.5 22.4 %attn_bwd.1 = (f32[2048,256]{1,0:T(8,128)S(1)}, f32[2048,256]{1,0:T(8,128)S(1)}, f32[2048,256]{1,0:T(8,128)S(1)}) custom-call(s32[8]{0:T(128)S(1)} %and_select_fusion.lo_ref, bf16[2048,256]{1,0:T(8,128)(2,1)S(1)} %copy-done.6, bf16[2048,256]{1,0:T(8,128)(2,1)S(1)} %copy-done.4, bf16[2048,256]{1,0:T(8,128)(2,1)S(1)} %copy-done.8, ...), custom_call_target="tpu_custom_call" | custom-call | flops 100000000 | bytes 4194304 | tf_op jit(solution)/shard_map/attn_bwd/pallas_call | solution.py:233
  523.6 5.7 reduce-scatter.5.cloned.1.call-done
  536.8 5.0 multiply_reduce_fusion.2
  544.7 52.3 %moe_out.1 = f32[256,2048]{1,0:T(8,128)} custom-call(bf16[2048,2048]{1,0:T(8,128)(2,1)} %get-tuple-element.99.l_hbm, bf16[2048,2048]{1,0:T(8,128)(2,1)} %bitcast.102), custom_call_target="tpu_custom_call" | custom-call | flops 1000000000 | bytes 4194304 | tf_op jit(solution)/shard_map/moe_out/pallas_call | solution.py:534
  597.6 7.2 convolution_convert_fusion.1
  611.1 47.9 %normed_back.1 = f32[256,2048]{1,0:T(8,128)} custom-call(bf16[2048,768]{1,0:T(8,128)(2,1)} %pad_maximum_fusion.2.l_hbm, bf16[2048,768]{1,0:T(8,128)(2,1)} %copy-done.29), custom_call_target="tpu_custom_call" | custom-call | flops 1000000000 | bytes 4194304 | tf_op jit(solution)/shard_map/normed_back/pallas_call | solution.py:534
  661.5 10.4 %convolution_convert_fusion = bf16[2048,768]{0,1:T(8,128)(2,1)S(1)} fusion(bf16[2048,2048]{1,0:T(8,128)(2,1)} %all-gather.4.cloned.1.call-done, f32[2048]{0:T(1024)S(1)} %copy-done.48, f32[2048]{0:T(1024)S(1)} %copy-done.52, bf16[2048,256]{1,0:T(8,128)(2,1)S(1)} %convert_element_type.95, bf16[2048,256]{1,0:T(8,128)(2,1)S(1)} %copy-done.37, ...), kind=kOutput, calls=%fused_computation.6 | convolution fusion | flops 6470238208 | bytes 14696448 | tf_op jit(solution)/shard_map/dot_general | solution.py:32
  674.4 6.1 fusion.12
  680.6 13.4 %reduce-scatter.9.cloned.1.call-done = bf16[1,18,512,128]{3,2,1,0:T(8,128)(2,1)} async-done(((bf16[4,18,512,128]{3,2,1,0:T(8,128)(2,1)}), bf16[1,18,512,128]{3,2,1,0:T(8,128)(2,1)}) %reduce-scatter.9.cloned.1.call-update) | async-done | bytes 2359312 | tf_op jit(solution)/shard_map/reduce_scatter | solution.py:824
  699.6 5.5 collective-permute-done.12
  706.9 4.5 collective-permute-done.13
  714.3 12.3 %collective-permute-done.14 = f32[17,2048]{1,0:T(8,128)S(1)} collective-permute-done((f32[17,2048]{1,0:T(8,128)S(1)}, f32[17,2048]{1,0:T(8,128)S(1)}, u32[]{:S(2)}, u32[]{:S(2)}) %collective-permute-start.14) | collective-permute-done | bytes 139296 | tf_op jit(solution)/shard_map/ppermute | solution.py:649
  731.3 20.8 %collective-permute-done.15 = f32[17,2048]{1,0:T(8,128)S(1)} collective-permute-done((f32[17,2048]{1,0:T(8,128)S(1)}, f32[17,2048]{1,0:T(8,128)S(1)}, u32[]{:S(2)}, u32[]{:S(2)}) %collective-permute-start.15) | collective-permute-done | bytes 139296 | tf_op jit(solution)/shard_map/ppermute | solution.py:649
  753.5 5.7 collective-permute-done.9
  773.8 3.6 maximum_convert_fusion
  (255 shorter events, 114.4 us)
Async XLA Ops:
  7.2 205.9 %copy-start = (bf16[2048,16]{0,1:T(8,128)(2,1)S(1)}, bf16[2048,16]{0,1:T(8,128)(2,1)}, u32[]{:S(2)}) copy-start(bf16[2048,16]{0,1:T(8,128)(2,1)} %param.27) | copy-start | bytes 196612
  7.2 59.8 %all-gather.4.cloned.1.call-start = ((), (), s32[]{:S(2)}) async-start(), calls=%async_computation.5 | async-start | bytes 9437184 | tf_op jit(solution)/shard_map/all_gather | solution.py:690
  7.9 128.2 %all-gather.6.cloned.1.call-start = ((), (), s32[]{:S(2)}) async-start(), calls=%async_computation.6 | async-start | bytes 9437184 | tf_op jit(solution)/shard_map/all_gather | solution.py:737
  21.6 51.3 %copy-start.29 = (bf16[2048,768]{1,0:T(8,128)(2,1)}, bf16[2048,768]{1,0:T(8,128)(2,1)S(1)}, u32[]{:S(2)}) copy-start(bf16[2048,768]{1,0:T(8,128)(2,1)S(1)} %pad_maximum_fusion.1.r_hbm) | copy-start | bytes 9437188
  67.1 158.0 %all-gather.8.cloned.1.call-start = ((), (), s32[]{:S(2)}) async-start(), calls=%async_computation.7 | async-start | bytes 9437184 | tf_op jit(solution)/shard_map/all_gather | solution.py:765
  81.4 1.2 collective-permute-start
  82.7 4.1 collective-permute-start.1
  86.8 4.1 collective-permute-start.2
  98.9 32.8 %copy-start.3 = (bf16[2048,256]{1,0:T(8,128)(2,1)}, bf16[2048,256]{1,0:T(8,128)(2,1)S(1)}, u32[]{:S(2)}) copy-start(bf16[2048,256]{1,0:T(8,128)(2,1)S(1)} %get-tuple-element.196.k_ref) | copy-start | bytes 3145732
  136.0 181.2 %reduce-scatter.7.cloned.1.call-start = ((), (), s32[]{:S(2)}) async-start(), calls=%async_computation.9 | async-start | bytes 3932160 | tf_op jit(solution)/shard_map/reduce_scatter | solution.py:794
  142.5 308.1 %copy-start.21 = (f32[256,2048]{1,0:T(8,128)}, f32[256,2048]{1,0:T(8,128)S(1)}, u32[]{:S(2)}) copy-start(f32[256,2048]{1,0:T(8,128)S(1)} %get-tuple-element.239) | copy-start | bytes 6291460
  248.4 281.0 %reduce-scatter.5.cloned.1.call-start = ((), (), s32[]{:S(2)}) async-start(), calls=%async_computation.8 | async-start | bytes 15728640 | tf_op jit(solution)/shard_map/reduce_scatter | solution.py:794
  375.5 71.2 %all-to-all-start = ((f32[8,256,16]{1,2,0:T(8,128)}), f32[8,256,16]{1,2,0:T(8,128)S(1)}, u32[]{:S(2)}, u32[]{:S(2)}) async-start(f32[8,256,16]{1,2,0:T(8,128)} %copy.134), calls=%async_computation.2 | async-start | bytes 262144 | tf_op jit(solution)/shard_map/all_to_all | solution.py:799
  378.9 315.1 %reduce-scatter.9.cloned.1.call-start = ((), (), s32[]{:S(2)}) async-start(), calls=%async_computation.10 | async-start | bytes 11796480 | tf_op jit(solution)/shard_map/reduce_scatter | solution.py:824
  453.6 38.8 %copy-start.41 = (bf16[256,2048]{1,0:T(8,128)(2,1)S(1)}, bf16[256,2048]{1,0:T(8,128)(2,1)}, u32[]{:S(2)}) copy-start(bf16[256,2048]{1,0:T(8,128)(2,1)} %param.22) | copy-start | bytes 3145732
  529.4 254.3 %reduce-scatter.11.cloned.1.call-start = ((), (), s32[]{:S(2)}) async-start(), calls=%async_computation.11 | async-start | bytes 5242880 | tf_op jit(solution)/shard_map/reduce_scatter | solution.py:854
  541.8 1.2 collective-permute-start.3
  543.1 53.8 %collective-permute-start.4 = (f32[2,2048]{1,0:T(2,128)S(1)}, f32[2,2048]{1,0:T(2,128)S(1)}, u32[]{:S(2)}, u32[]{:S(2)}) collective-permute-start(f32[2,2048]{1,0:T(2,128)S(1)} %fusion.33), channel_id=1, source_target_pairs={{0,2},{1,3},{2,0},{3,1},{4,6},{5,7},{6,4},{7,5},{8,10},{9,11},{10,... | collective-permute-start | bytes 49160 | tf_op jit(solution)/shard_map/ppermute | solution.py:649
  544.7 52.9 %copy-start.18 = (bf16[2048,256]{1,0:T(8,128)(2,1)S(1)}, bf16[2048,256]{1,0:T(8,128)(2,1)}, u32[]{:S(2)}) copy-start(bf16[2048,256]{1,0:T(8,128)(2,1)} %copy-done.17) | copy-start | bytes 3145732
  597.0 7.9 collective-permute-start.5
  611.1 47.9 %copy-start.48 = (f32[2048]{0:T(1024)S(1)}, f32[2048]{0:T(1024)}, u32[]{:S(2)}) copy-start(f32[2048]{0:T(1024)} %param.23) | copy-start | bytes 24580
  695.1 35.0 %copy-start.44 = (bf16[1,6,512,128]{3,2,1,0:T(8,128)(2,1)S(1)}, bf16[1,6,512,128]{3,2,1,0:T(8,128)(2,1)}, u32[]{:S(2)}) copy-start(bf16[1,6,512,128]{3,2,1,0:T(8,128)(2,1)} %reduce-scatter.7.cloned.1.call-done) | copy-start | bytes 2359300
  696.6 1.5 collective-permute-start.11
  698.1 7.0 collective-permute-start.12
  705.1 6.2 collective-permute-start.13
  706.8 5.9 collective-permute-start.6
  711.4 15.3 %collective-permute-start.14 = (f32[17,2048]{1,0:T(8,128)S(1)}, f32[17,2048]{1,0:T(8,128)S(1)}, u32[]{:S(2)}, u32[]{:S(2)}) collective-permute-start(f32[17,2048]{1,0:T(8,128)S(1)} %add.163), channel_id=1, source_target_pairs={{0,8},{8,0},{16,24},{24,16},{1,9},{9,1},{17,25},{25,17},{2,10},{10... | collective-permute-start | bytes 417800 | tf_op jit(solution)/shard_map/ppermute | solution.py:649
  712.7 15.6 %collective-permute-start.7 = (f32[3,2048]{1,0:T(4,128)S(1)}, f32[3,2048]{1,0:T(4,128)S(1)}, u32[]{:S(2)}, u32[]{:S(2)}) collective-permute-start(f32[3,2048]{1,0:T(4,128)S(1)} %fusion.35), channel_id=1, source_target_pairs={{0,2},{1,3},{2,0},{3,1},{4,6},{5,7},{6,4},{7,5},{8,10},{9,11},{10,... | collective-permute-start | bytes 73736 | tf_op jit(solution)/shard_map/ppermute | solution.py:649
  726.7 25.5 %collective-permute-start.15 = (f32[17,2048]{1,0:T(8,128)S(1)}, f32[17,2048]{1,0:T(8,128)S(1)}, u32[]{:S(2)}, u32[]{:S(2)}) collective-permute-start(f32[17,2048]{1,0:T(8,128)S(1)} %add.164), channel_id=1, source_target_pairs={{0,16},{8,24},{16,0},{24,8},{1,17},{9,25},{17,1},{25,9},{2,18},{10... | collective-permute-start | bytes 417800 | tf_op jit(solution)/shard_map/ppermute | solution.py:649
  728.4 23.8 %collective-permute-start.8 = (f32[3,2048]{1,0:T(4,128)S(1)}, f32[3,2048]{1,0:T(4,128)S(1)}, u32[]{:S(2)}, u32[]{:S(2)}) collective-permute-start(f32[3,2048]{1,0:T(4,128)S(1)} %fusion.65), channel_id=1, source_target_pairs={{0,4},{1,5},{2,6},{3,7},{4,0},{5,1},{6,2},{7,3},{8,12},{9,13},{10,... | collective-permute-start | bytes 73736 | tf_op jit(solution)/shard_map/ppermute | solution.py:649
  752.2 7.1 collective-permute-start.9
  759.2 7.2 collective-permute-start.10
  (49 other events, 247.0 us)
Sparse Core Ops, SparseCore 0:
  9.9 57.0 all-gather.3
  68.9 65.9 all-gather.5
  136.8 83.1 all-gather.7
  248.5 60.4 reduce-scatter.6
  317.3 212.0 reduce-scatter.4
  531.6 162.3 reduce-scatter.8
  696.2 87.4 reduce-scatter.10

commit v3 on v2

--- a/solution.py
+++ b/solution.py
@@ -259,9 +259,9 @@
 def expert_body(*refs, first, rows_blk, parts):
     lead = first == 0
     if lead:
-        x_hbm, g_hbm, gates_ref, wg_ref, wu_ref, wd_ref = refs[:6]
-        dgu_ref, ga_ref, wcat, dots_ref, grads_ref, xt_hbm = refs[6:12]
-        x_v, xt_v, g_v, sem_x, sem_t, sem_g = refs[12:]
+        x_hbm, g_hbm, mask_ref, wg_ref, wu_ref, wd_ref, router_ref = refs[:7]
+        dgu_ref, ga_ref, wcat, dots_ref, grads_ref, xt_hbm, gates_ref, probs_ref = refs[7:15]
+        x_v, xt_v, g_v, sem_x, sem_t, sem_g = refs[15:]
     else:
         x_hbm, g_hbm, gates_ref, wg_ref, wu_ref, wd_ref, xt_hbm = refs[:7]
         dgu_ref, ga_ref, wcat, dots_ref, grads_ref = refs[10:15]
@@ -312,6 +312,11 @@
 
         if lead:
             xt_v[:, r] = x_v[r, :].T
+            logits = dot_nn(x_v[r, :], router_ref[...])
+            grown = jnp.exp(logits - jnp.max(logits, axis=1, keepdims=True))
+            probs = grown / jnp.sum(grown, axis=1, keepdims=True)
+            probs_ref[r, :] = probs
+            gates_ref[r, :] = probs * mask_ref[r, :]
         gu = dot_nn(x_v[r, :], wcat[...])
         q = dot_nt(g_v[r, :], wd_ref[...])
         gate_rows = gates_ref[r, :]
@@ -363,7 +368,7 @@
             t_copy.wait()
 
 
-def expert_chunk(x, g, gates, wg, wu, wd, carried, *, first, pairs, parts):
+def expert_chunk(x, g, gates, wg, wu, wd, router, carried, *, first, pairs, parts):
     tokens, width = x.shape
     experts, _, hid = wg.shape
     total = experts // 2
@@ -399,8 +404,11 @@
     args = [x, g, gates, wg, wu, wd]
     alias = {}
     if lead:
-        out_shape.append(jax.ShapeDtypeStruct((width, tokens), BF))
-        out_specs.append(any_spec)
+        args.append(router)
+        in_specs.append(pl.BlockSpec(router.shape, lambda p: (0, 0)))
+        narrow = jax.ShapeDtypeStruct((tokens, experts), F32)
+        out_shape += [jax.ShapeDtypeStruct((width, tokens), BF), narrow, narrow]
+        out_specs += [any_spec] + [pl.BlockSpec((tokens, experts), lambda p: (0, 0))] * 2
     else:
         xt, dgu, ga, wcat = carried
         args += [xt, dgu, ga, wcat]
@@ -427,6 +435,223 @@
         ),
         name="expert_chunk",
     )(*args)
+
+
+GATHER_COPIES = 13
+
+
+def gather_plan(x_hbm, land, me, own, send_sem, recv_sem):
+    half = own // 2
+    pc, px, py = (partner(me, b) for b in (1, 2, 4))
+    diag = partner(px, 4)
+
+    def piece(dev, a, n):
+        return land.at[pl.ds(pl.multiple_of(dev * own + a, half), n)]
+
+    plan = [
+        (me, 0, half, px),
+        (me, half, half, py),
+        (me, half, half, px),
+        (me, 0, half, py),
+        (me, 0, own, pc),
+        (px, 0, half, py),
+        (py, half, half, px),
+        (px, 0, half, pc),
+        (py, half, half, pc),
+        (px, half, half, pc),
+        (py, 0, half, pc),
+        (diag, 0, half, pc),
+        (diag, half, half, pc),
+    ]
+    origin = {0: px, 1: py, 2: px, 3: py, 4: pc, 5: diag, 6: diag}
+
+    def copy(k):
+        dev, a, n, target = plan[k]
+        src = x_hbm.at[pl.ds(a, n)] if k < 5 else piece(dev, a, n)
+        return remote(src, piece(dev, a, n), send_sem.at[k], recv_sem.at[k], target)
+
+    def arrived(k):
+        dev, a, n, target = plan[k]
+        src = origin[k] if k in origin else partner(dev, 1)
+        return remote(piece(src, a, n), piece(src, a, n), send_sem.at[k], recv_sem.at[k], target)
+
+    return copy, arrived, pc, px, py, diag
+
+
+def project_body(
+    x_hbm, wq_hbm, wk_hbm, wv_hbm, gain_ref, qg_ref, kg_ref, pos_ref,
+    normed_hbm, q_ref, k_ref, v_ref, qu_ref, ku_ref, rs_ref, cos_ref, sin_ref,
+    x_v, n_v, w_v, sums, sums_all, send_sem, recv_sem, ss_send, ss_recv, w_sem, x_sem, n_sem, *, size
+):
+    me = lax.axis_index("tensor")
+    own = x_hbm.shape[0]
+    width = x_hbm.shape[1]
+    cols = q_ref.shape[1]
+    heads = cols // HEAD_DIM
+    half_dim = HEAD_DIM // 2
+    weights = [
+        pltpu.make_async_copy(w, w_v.at[:, pl.ds(i * cols, cols)], w_sem.at[i])
+        for i, w in enumerate((wq_hbm, wk_hbm, wv_hbm))
+    ]
+    mine = pl.ds(pl.multiple_of(me * own, own), own)
+    here = pltpu.make_async_copy(x_hbm, x_v.at[mine], x_sem)
+    here.start()
+    for w in weights:
+        w.start()
+    greet([lax.rem(me + t, size) for t in range(1, size)])
+    copy, arrived, pc, px, py, diag = gather_plan(x_hbm, x_v, me, own, send_sem, recv_sem)
+    for k in range(5):
+        copy(k).start()
+
+    lane = lax.broadcasted_iota(jnp.int32, (own, HEAD_DIM), 1)
+    power = (lane % half_dim).astype(F32) * (-2.0 * math.log(10000.0) / HEAD_DIM)
+    frequency = jnp.exp(power)
+
+    def table(i, _):
+        r = pl.ds(pl.multiple_of(i * own, own), own)
+        angle = pos_ref[r, :] * frequency
+        cos_ref[r, :] = jnp.cos(angle)
+        sine = jnp.sin(angle)
+        sin_ref[r, :] = jnp.where(lane < half_dim, -sine, sine)
+        return 0
+
+    lax.fori_loop(0, size, table, 0)
+
+    def stored(dev):
+        r = pl.ds(pl.multiple_of(dev * own, own), own)
+        return pltpu.make_async_copy(n_v.at[r], normed_hbm.at[r], n_sem.at[dev])
+
+    def process(dev):
+        r = pl.ds(pl.multiple_of(dev * own, own), own)
+        wide = x_v[r, :].astype(F32)
+        scale = lax.rsqrt(jnp.mean(wide * wide, axis=1, keepdims=True) + EPS)
+        normed = (wide * scale * gain_ref[...]).astype(BF)
+        n_v[r, :] = normed
+        stored(dev).start()
+        res = dot_nn(normed, w_v[...])
+        q = res[:, :cols]
+        k = res[:, cols : 2 * cols]
+        qu_ref[r, :] = q
+        ku_ref[r, :] = k
+        v_ref[r, :] = res[:, 2 * cols :].astype(BF)
+        pair = jnp.where(
+            lane == 0,
+            jnp.sum(q * q, axis=1, keepdims=True),
+            jnp.sum(k * k, axis=1, keepdims=True),
+        )
+        sums[dev] = pair.T[0:2, :]
+
+    here.wait()
+    for w in weights:
+        w.wait()
+    process(me)
+    arrived(4).wait_recv()
+    process(pc)
+    arrived(0).wait_recv()
+    copy(5).start()
+    copy(7).start()
+    arrived(1).wait_recv()
+    copy(6).start()
+    copy(8).start()
+    arrived(2).wait_recv()
+    copy(9).start()
+    arrived(3).wait_recv()
+    copy(10).start()
+    process(px)
+    process(py)
+    arrived(7).wait_recv()
+    arrived(9).wait_recv()
+    process(partner(px, 1))
+    arrived(8).wait_recv()
+    arrived(10).wait_recv()
+    process(partner(py, 1))
+    arrived(5).wait_recv()
+    copy(11).start()
+    arrived(6).wait_recv()
+    copy(12).start()
+    process(diag)
+    arrived(11).wait_recv()
+    arrived(12).wait_recv()
+    process(partner(diag, 1))
+
+    def exchange(t, src):
+        other = lax.rem(me + t, size)
+        slot = me if src is None else other
+        return remote(sums, sums_all.at[slot], ss_send.at[other], ss_recv.at[slot], other)
+
+    for t in range(1, size):
+        exchange(t, None).start()
+    sums_all[me] = sums[...]
+    for t in range(1, size):
+        exchange(t, 1).wait_recv()
+    total = sums_all[0]
+    for d in range(1, size):
+        total = total + sums_all[d]
+    rows_iota = lax.broadcasted_iota(jnp.int32, (HEAD_DIM, own), 0)
+    for d in range(size):
+        r = slice(d * own, (d + 1) * own)
+        tot = total[d]
+        both = jnp.where(rows_iota == 0, tot[0:1, :], tot[1:2, :])
+        rs = lax.rsqrt(both / width + EPS).T
+        rs_ref[r, :] = rs[:, 0:2]
+        cos, sin = cos_ref[r, :], sin_ref[r, :]
+        for j, (unit_ref, gain, dst) in enumerate(((qu_ref, qg_ref, q_ref), (ku_ref, kg_ref, k_ref))):
+            unit = unit_ref[r, :] * rs[:, j : j + 1]
+            unit_ref[r, :] = unit
+            wide = unit * gain[...]
+            for h in range(heads):
+                c = slice(h * HEAD_DIM, (h + 1) * HEAD_DIM)
+                w = wide[:, c]
+                dst[r, c] = (w * cos + pltpu.roll(w, half_dim, 1) * sin).astype(BF)
+    for t in range(1, size):
+        exchange(t, None).wait_send()
+    for k in range(GATHER_COPIES):
+        copy(k).wait_send()
+    for d in range(size):
+        stored(d).wait()
+
+
+def project(x, wq, wk, wv, gain, qg, kg, pos, size, cid):
+    own, width = x.shape
+    cols = wq.shape[1]
+    tokens = own * size
+    any_spec = pl.BlockSpec(memory_space=pl.ANY)
+    vm = pl.BlockSpec(memory_space=pltpu.VMEM)
+    return pl.pallas_call(
+        functools.partial(project_body, size=size),
+        out_shape=(
+            jax.ShapeDtypeStruct((tokens, width), BF),
+            jax.ShapeDtypeStruct((tokens, cols), BF),
+            jax.ShapeDtypeStruct((tokens, cols), BF),
+            jax.ShapeDtypeStruct((tokens, cols), BF),
+            jax.ShapeDtypeStruct((tokens, cols), F32),
+            jax.ShapeDtypeStruct((tokens, cols), F32),
+            jax.ShapeDtypeStruct((tokens, 2), F32),
+            jax.ShapeDtypeStruct((tokens, HEAD_DIM), F32),
+            jax.ShapeDtypeStruct((tokens, HEAD_DIM), F32),
+        ),
+        in_specs=[any_spec] * 4 + [vm] * 4,
+        out_specs=[any_spec] + [vm] * 8,
+        scratch_shapes=[
+            pltpu.VMEM((tokens, width), BF),
+            pltpu.VMEM((tokens, width), BF),
+            pltpu.VMEM((width, 3 * cols), BF),
+            pltpu.VMEM((size, 2, own), F32),
+            pltpu.VMEM((size, size, 2, own), F32),
+            pltpu.SemaphoreType.DMA((GATHER_COPIES,)),
+            pltpu.SemaphoreType.DMA((GATHER_COPIES,)),
+            pltpu.SemaphoreType.DMA((size,)),
+            pltpu.SemaphoreType.DMA((size,)),
+            pltpu.SemaphoreType.DMA((3,)),
+            pltpu.SemaphoreType.DMA,
+            pltpu.SemaphoreType.DMA((size,)),
+        ],
+        compiler_params=pltpu.CompilerParams(
+            vmem_limit_bytes=56 * MIB, collective_id=cid, has_side_effects=True
+        ),
+        cost_estimate=pl.CostEstimate(flops=10**8, bytes_accessed=4 * MIB, transcendentals=0),
+        name="project",
+    )(x, wq, wk, wv, gain[None, :], qg[None, :], kg[None, :], pos)
 
 
 def matmul_scatter_body(
@@ -561,65 +786,20 @@
 def gather_body(x_ref, out_ref, send_sem, recv_sem, here_sem):
     me = lax.axis_index("tensor")
     own = x_ref.shape[0]
-    half = own // 2
-    pc, px, py = (partner(me, b) for b in (1, 2, 4))
-    diag = partner(px, 4)
-    greet([pc, px, py])
-
-    def piece(dev, a, n):
-        return out_ref.at[pl.ds(pl.multiple_of(dev * own + a, half), n)]
-
-    here = pltpu.make_async_copy(x_ref, piece(me, 0, own), here_sem)
+    greet([partner(me, b) for b in (1, 2, 4)])
+    mine = pl.ds(pl.multiple_of(me * own, own), own)
+    here = pltpu.make_async_copy(x_ref, out_ref.at[mine], here_sem)
     here.start()
-    plan = [
-        (me, 0, half, px),
-        (me, half, half, py),
-        (me, half, half, px),
-        (me, 0, half, py),
-        (me, 0, own, pc),
-        (px, 0, half, py),
-        (py, half, half, px),
-        (px, 0, half, pc),
-        (py, half, half, pc),
-        (px, half, half, pc),
-        (py, 0, half, pc),
-        (diag, 0, half, pc),
-        (diag, half, half, pc),
-    ]
-
-    def copy(k):
-        dev, a, n, target = plan[k]
-        src = x_ref.at[pl.ds(a, n)] if k < 5 else piece(dev, a, n)
-        return remote(src, piece(dev, a, n), send_sem.at[k], recv_sem.at[k], target)
-
-    def arrived(k):
-        dev, a, n, target = plan[k]
-        bit_dev = {0: px, 1: py, 2: px, 3: py, 4: pc, 5: diag, 6: diag}
-        if k in bit_dev:
-            src = bit_dev[k]
-        else:
-            src = partner(dev, 1)
-        return remote(piece(src, a, n), piece(src, a, n), send_sem.at[k], recv_sem.at[k], target)
-
+    copy, arrived = gather_plan(x_ref, out_ref, me, own, send_sem, recv_sem)[:2]
     for k in range(5):
         copy(k).start()
-    arrived(0).wait_recv()
-    copy(5).start()
-    copy(7).start()
-    arrived(1).wait_recv()
-    copy(6).start()
-    copy(8).start()
-    arrived(2).wait_recv()
-    copy(9).start()
-    arrived(3).wait_recv()
-    copy(10).start()
-    arrived(5).wait_recv()
-    copy(11).start()
-    arrived(6).wait_recv()
-    copy(12).start()
+    for k, following in ((0, (5, 7)), (1, (6, 8)), (2, (9,)), (3, (10,)), (5, (11,)), (6, (12,))):
+        arrived(k).wait_recv()
+        for f in following:
+            copy(f).start()
     for k in (4, 7, 8, 9, 10, 11, 12):
         arrived(k).wait_recv()
-    for k in range(13):
+    for k in range(GATHER_COPIES):
         copy(k).wait_send()
     here.wait()
 
@@ -635,8 +815,8 @@
         in_specs=[any_spec],
         out_specs=any_spec,
         scratch_shapes=[
-            pltpu.SemaphoreType.DMA((13,)),
-            pltpu.SemaphoreType.DMA((13,)),
+            pltpu.SemaphoreType.DMA((GATHER_COPIES,)),
+            pltpu.SemaphoreType.DMA((GATHER_COPIES,)),
             pltpu.SemaphoreType.DMA,
         ],
         compiler_params=pltpu.CompilerParams(collective_id=cid, has_side_effects=True),
@@ -687,8 +867,6 @@
     col_start = me * local_cols
     block = 256
 
-    full_input = lax.all_gather(block_input, "tensor", axis=0, tiled=True)
-
     seg = segments.reshape(token_count)
     values16 = jnp.arange(16, dtype=jnp.int32)
     below = jnp.sum((seg[None, :] < values16[:, None]).astype(jnp.int32), axis=1)
@@ -696,15 +874,6 @@
         jnp.where(seg[:, None] == values16[None, :], below[None, :], 0), axis=1
     )
     positions = jnp.arange(token_count, dtype=jnp.int32) - doc_start
-    half = HEAD_DIM // 2
-    frequency = jnp.exp(
-        jnp.arange(half, dtype=F32) * (-2.0 * math.log(10000.0) / HEAD_DIM)
-    )
-    angles = positions.astype(F32)[:, None] * frequency[None, :]
-    cosine, sine = jnp.cos(angles), jnp.sin(angles)
-    cos_all = jnp.concatenate([cosine] * (2 * local_heads), axis=1)
-    sin_all = jnp.concatenate([-sine, sine] * local_heads, axis=1)
-    cos_all, sin_all = lax.optimization_barrier((cos_all, sin_all))
     lo_block = doc_start[::block] // block
     seg_col = seg[:, None]
     seg_rows = seg.reshape(token_count // block, 1, block)
@@ -730,39 +899,49 @@
     mask = (routed_b * (place < capacity).astype(F32)).reshape(token_count, experts)
 
     w_qkv = jnp.concatenate([w_query, w_key, w_value], axis=1)
-    full_input, cos_all, sin_all, mask, w_qkv, lo_block, seg_col, seg_rows = lax.optimization_barrier(
-        (full_input, cos_all, sin_all, mask, w_qkv, lo_block, seg_col, seg_rows)
-    )
-    full_input, w_output_in = lax.optimization_barrier((full_input, w_output))
-    full_wo = lax.all_gather(w_output_in, "tensor", axis=0, tiled=True)
-
-    input_wide = full_input.astype(F32)
-    scale_one = rms_scale(input_wide)
-    normed = (input_wide * scale_one * attn_gain).astype(BF)
-    qkv = dot_nn(normed, w_qkv)
-    query_raw = qkv[:, :local_cols]
-    key_raw = qkv[:, local_cols : 2 * local_cols]
-    value_low = qkv[:, 2 * local_cols :].astype(BF)
-    squares = jnp.stack(
-        [jnp.sum(query_raw * query_raw, axis=1), jnp.sum(key_raw * key_raw, axis=1)]
-    )
-    squares = sum_all(squares, "tensor", n_tensor)
-    scales = lax.rsqrt(squares / model_width + EPS)
-    query_rs = scales[0][:, None]
-    key_rs = scales[1][:, None]
-    query_unit = query_raw * query_rs
-    key_unit = key_raw * key_rs
-    q_n = query_unit * query_gain
-    k_n = key_unit * key_gain
-    queries = (q_n * cos_all + half_swap(q_n) * sin_all).astype(BF)
-    keys_rot = (k_n * cos_all + half_swap(k_n) * sin_all).astype(BF)
+    full_wo = lax.all_gather(w_output, "tensor", axis=0, tiled=True)
+    pos_col = positions.astype(F32)[:, None]
+    if n_tensor == 8:
+        normed, queries, keys_rot, value_low, query_unit, key_unit, scales, cos_one, sin_one = project(
+            block_input, w_query, w_key, w_value, attn_gain, query_gain, key_gain, pos_col, n_tensor, 6
+        )
+        query_rs, key_rs = scales[:, 0:1], scales[:, 1:2]
+        cos_all = jnp.concatenate([cos_one] * local_heads, axis=1)
+        sin_all = jnp.concatenate([sin_one] * local_heads, axis=1)
+    else:
+        half = HEAD_DIM // 2
+        frequency = jnp.exp(
+            jnp.arange(half, dtype=F32) * (-2.0 * math.log(10000.0) / HEAD_DIM)
+        )
+        angles = pos_col * frequency[None, :]
+        cosine, sine = jnp.cos(angles), jnp.sin(angles)
+        cos_all = jnp.concatenate([cosine] * (2 * local_heads), axis=1)
+        sin_all = jnp.concatenate([-sine, sine] * local_heads, axis=1)
+        input_wide = lax.all_gather(block_input, "tensor", axis=0, tiled=True).astype(F32)
+        normed = (input_wide * rms_scale(input_wide) * attn_gain).astype(BF)
+        qkv = dot_nn(normed, w_qkv)
+        query_raw = qkv[:, :local_cols]
+        key_raw = qkv[:, local_cols : 2 * local_cols]
+        value_low = qkv[:, 2 * local_cols :].astype(BF)
+        squares = jnp.stack(
+            [jnp.sum(query_raw * query_raw, axis=1), jnp.sum(key_raw * key_raw, axis=1)]
+        )
+        squares = sum_all(squares, "tensor", n_tensor)
+        scales = lax.rsqrt(squares / model_width + EPS)
+        query_rs, key_rs = scales[0][:, None], scales[1][:, None]
+        query_unit = query_raw * query_rs
+        key_unit = key_raw * key_rs
+        q_n = query_unit * query_gain
+        k_n = key_unit * key_gain
+        queries = (q_n * cos_all + half_swap(q_n) * sin_all).astype(BF)
+        keys_rot = (k_n * cos_all + half_swap(k_n) * sin_all).astype(BF)
+    queries, cot_in = lax.optimization_barrier((queries, cotangent))
+    full_cot = lax.all_gather(cot_in, "tensor", axis=0, tiled=True)
     reach = min(1024 // block, token_count // block)
     attended, attn_low, lse, own_attn = attn_fwd(
         queries, keys_rot, value_low, seg_col, seg_rows, block, reach, n_tensor, 0
     )
 
-    own_attn, cot_in = lax.optimization_barrier((own_attn, cotangent))
-    full_cot = lax.all_gather(cot_in, "tensor", axis=0, tiled=True)
 
     input_own = block_input.astype(F32)
     residual = input_own + dot_nn(own_attn, full_wo)
@@ -770,28 +949,26 @@
     own_moe_in = (residual * scale_two * moe_gain).astype(BF)
     moe_in = gather_all(own_moe_in, n_tensor, 1, "gather_moe")
 
-    router_probs = jax.nn.softmax(dot_nn(moe_in, router), axis=-1)
-    gates = router_probs * mask
     wd_flat = w_down.reshape(experts * hid, model_width)
     pairs_total = experts // 2
-    chunks = (1, 4, 3)
+    chunks = (1, 3, 4)
     dots = None
     reduced = []
     carried = None
     first = 0
     for count in chunks:
         res = expert_chunk(
-            moe_in, full_cot, gates, w_gate, w_up, wd_flat, carried,
+            moe_in, full_cot, mask if first == 0 else gates, w_gate, w_up, wd_flat, router, carried,
             first=first, pairs=count, parts=n_dp,
         )
         dgu, ga, wcat, dot_c, grads = res[:5]
-        xt = res[5] if first == 0 else carried[0]
-        if len(reduced) == 1:
+        if first == 0:
+            xt, gates, router_probs = res[5:]
+        if len(reduced) == 2:
             reduced[0], dgu = lax.optimization_barrier((reduced[0], dgu))
         carried = (xt, dgu, ga, wcat)
         dots = dot_c if dots is None else dots + dot_c
-        if first + count < pairs_total:
-            reduced.append(lax.psum_scatter(grads, "dp", scatter_dimension=0, tiled=False))
+        reduced.append(lax.psum_scatter(grads, "dp", scatter_dimension=0, tiled=False))
         first += count
     moe_back = matmul_scatter(dgu, wcat, n_tensor, 2, True, "moe_back")
 
@@ -820,8 +997,7 @@
     dq_rot, dk_rot, dv = attn_bwd(
         lo_block, queries, keys_rot, value_low, heads_grad, attended, lse, seg_col, seg_rows, block
     )
-    reduced[1], grads, dq_rot = lax.optimization_barrier((reduced[1], grads, dq_rot))
-    reduced.append(lax.psum_scatter(grads, "dp", scatter_dimension=0, tiled=False))
+    reduced[1], dq_rot = lax.optimization_barrier((reduced[1], dq_rot))
     query_norm_grad = dq_rot * cos_all - half_swap(dq_rot) * sin_all
     key_norm_grad = dk_rot * cos_all - half_swap(dk_rot) * sin_all
     query_gain_grad = jnp.sum(query_norm_grad * query_unit, axis=0)

time: 802 us -> 769 us (0.959)
  Pallas kernels: 476 us -> 529 us
  waiting for transfers between devices: 125 us -> 72.5 us
  other arithmetic: 63.6 us -> 42.9 us
  matrix products: 47.2 us -> 34.1 us
    pallas_call x0 -> x1, Pallas kernels: none -> 77.8 us  [project(): pl.pallas_call(functools.partial(project_body, size=size), out_shape=(jax...]
    all_gather x2 -> x1, waiting for transfers between devices: 45.5 us -> 0.01 us  [per_device(): full_wo = lax.all_gather(w_output, 'tensor', axis=0, tiled=True)]
    pallas_call x2, Pallas kernels: 108 us -> 90.5 us  [gather_all(): pl.pallas_call(gather_body, out_shape=jax.ShapeDtypeStruct((own * size, c...]
    dot_general x3 -> x1, matrix products: 19.3 us -> 6.5 us  [dot_nn(): lax.dot_general(a, b, (((1,), (0,)), ((), ())), preferred_element_type=F32)]
    reduce_scatter x3, waiting for transfers between devices: 19.1 us -> 11 us  [per_device(): lax.psum_scatter(grads, 'dp', scatter_dimension=0, tiled=False)]
    ppermute x16 -> x13, waiting for transfers between devices: 58.5 us -> 51.2 us  [swap(): return lax.ppermute(value, axis, [(i, i ^ bit) for i in range(size)])]
    unnamed x118 -> x125, local copies, waits for them, and re-layouts: 20.6 us -> 25.3 us
    ppermute x16 -> x13, starting transfers between devices: 16.5 us -> 14 us  [swap(): return lax.ppermute(value, axis, [(i, i ^ bit) for i in range(size)])]
  transfers between devices with their start and end apart: 24 -> 20, of which waited for: 15 -> 10; matrix products, arithmetic and copies ran while one was open for 17% -> 13% of each run, Pallas kernels for 57% -> 66%
where the time goes in v3:
time: 769 us; the launch traced here: 759 us
  Pallas kernels  529 us (69%)
  waiting for transfers between devices  72.5 us (9%)
  local copies, waits for them, and re-layouts  46.2 us (6%)
  other arithmetic  42.9 us (6%)
  matrix products  34.1 us (4%)
  starting transfers between devices  18.6 us (2%)
  between operations  15.3 us (2%)
    pallas_call x3, Pallas kernels, matmul_scatter(): pl.pallas_call(functools.partial(matmul_scatter_body, size=size, slices=s...  164 us
    pallas_call x3, Pallas kernels, expert_chunk(): pl.pallas_call(functools.partial(expert_body, first=first, rows_blk=rows_...  146 us
    pallas_call x2, Pallas kernels, gather_all(): pl.pallas_call(gather_body, out_shape=jax.ShapeDtypeStruct((own * size, c...  90.5 us
    pallas_call x1, Pallas kernels, project(): pl.pallas_call(functools.partial(project_body, size=size), out_shape=(jax...  77.8 us
    ppermute x13, waiting for transfers between devices, swap(): return lax.ppermute(value, axis, [(i, i ^ bit) for i in range(size)])  51.2 us
    pallas_call x1, Pallas kernels, attn_fwd(): pl.pallas_call(functools.partial(attn_fwd_body, block=block, heads=heads,...  33 us
    unnamed x125, local copies, waits for them, and re-layouts  25.3 us
    pallas_call x1, Pallas kernels, attn_bwd(): pl.pallas_call(functools.partial(attn_bwd_body, block=block, heads=heads)...  18.7 us
  transfers between devices with their start and end apart: 20, of which 10 were waited for; matrix products, arithmetic and copies ran while one was open for 13% of the time, Pallas kernels for 66%

profile of v3, /device:TPU:0, one launch (start us, length us, event | category | flops | bytes accessed | tf_op | source)
XLA Modules:
  0.0 759.0 jit_solution(8179658622459092512)
XLA Ops:
  11.0 77.8 %project.1 = (bf16[2048,2048]{1,0:T(8,128)(2,1)}, bf16[2048,256]{1,0:T(8,128)(2,1)}, bf16[2048,256]{1,0:T(8,128)(2,1)}, bf16[2048,256]{1,0:T(8,128)(2,1)}, f32[2...) custom-call(bf16[256,2048]{1,0:T(8,128)(2,1)} %x_hbm.1, ...), custom_call_target="tpu_custom_call" | custom-call | flops 100000000 | bytes 4194304 | tf_op jit(solution)/shard_map/project/pallas_call | solution.py:620
  93.8 33.0 %attn_fwd.1 = (f32[2048,256]{1,0:T(8,128)S(1)}, bf16[2048,256]{1,0:T(8,128)(2,1)S(1)}, f32[2048,2]{1,0:T(8,128)S(1)}, bf16[256,2048]{1,0:T(8,128)(2,1)S(1)}) custom-call(bf16[2048,256]{1,0:T(8,128)(2,1)S(1)} %copy-done.2, bf16[2048,256]{1,0:T(8,128)(2,1)S(1)} %copy-done.4, bf16[2048,256]{1,0:T(8,128)(2,1)S(1)} %copy-done.6, s32[2048,1]{1,0:T(8,128)S(1)} %copy.139.sq_ref, ...), custom_call_target="tpu_custom_call" | custom-call | flops 100000000 | bytes 4194304 | tf_op jit(solution)/shard_map/attn_fwd/pallas_call | solution.py:151
  131.1 6.5 multiply_reduce_fusion.6
  140.2 50.8 %gather_moe.1.refs_0_ = bf16[2048,2048]{1,0:T(8,128)(2,1)} custom-call(bf16[256,2048]{1,0:T(8,128)(2,1)} %multiply_convert_fusion.2.x_ref), custom_call_target="tpu_custom_call" | custom-call | bytes 4194304 | tf_op jit(solution)/shard_map/gather_moe/pallas_call | solution.py:812
  191.1 26.0 %expert_chunk.3 = (bf16[2048,4096]{1,0:T(8,128)(2,1)}, bf16[2048,2048]{1,0:T(8,128)(2,1)}, bf16[2048,4096]{1,0:T(8,128)(2,1)}, f32[2048,16]{1,0:T(8,128)}, bf16[...) custom-call(bf16[2048,2048]{1,0:T(8,128)(2,1)} %gather_moe.1.refs_0_, ...), custom_call_target="tpu_custom_call" | custom-call | flops 1000000000 | bytes 4194304 | tf_op jit(solution)/shard_map/expert_chunk/pallas_call | solution.py:417
  217.5 52.7 %expert_chunk.4 = (bf16[2048,4096]{1,0:T(8,128)(2,1)}, bf16[2048,2048]{1,0:T(8,128)(2,1)}, bf16[2048,4096]{1,0:T(8,128)(2,1)}, f32[2048,16]{1,0:T(8,128)}, bf16[4,18,512,128]{3,2,1,0:T(8,128)(2,1)}) custom-call(bf16[2048,2048]{1,0:T(8,128)(2,1)} %gather_moe.1.refs_0_, ...), custom_call_target="tpu_custom_call", output_to_operand_aliasing={{0}: (7, {}), {1}: (8, {}), {2}: (9, {})} | custom-call | flops 1000000000 | bytes 4194304 | tf_op jit(solution)/shard_map/expert_chunk/pallas_call | solution.py:417
  270.5 67.2 %expert_chunk.5 = (bf16[2048,4096]{1,0:T(8,128)(2,1)}, bf16[2048,2048]{1,0:T(8,128)(2,1)}, bf16[2048,4096]{1,0:T(8,128)(2,1)}, f32[2048,16]{1,0:T(8,128)}, bf16[4,24,512,128]{3,2,1,0:T(8,128)(2,1)}) custom-call(bf16[2048,2048]{1,0:T(8,128)(2,1)} %gather_moe.1.refs_0_, ...), custom_call_target="tpu_custom_call", output_to_operand_aliasing={{0}: (7, {}), {1}: (8, {}), {2}: (9, {})} | custom-call | flops 1000000000 | bytes 4194304 | tf_op jit(solution)/shard_map/expert_chunk/pallas_call | solution.py:417
  348.3 3.4 all-to-all-start
  352.0 5.2 all-to-all-done
  358.4 65.7 %moe_back.1 = f32[256,2048]{1,0:T(8,128)} custom-call(bf16[2048,4096]{1,0:T(8,128)(2,1)} %get-tuple-element.78.l_hbm, bf16[2048,4096]{1,0:T(8,128)(2,1)} %get-tuple-element.79.r_hbm), custom_call_target="tpu_custom_call" | custom-call | flops 1000000000 | bytes 4194304 | tf_op jit(solution)/shard_map/moe_back/pallas_call | solution.py:759
  424.2 3.9 multiply_reduce_fusion
  428.0 3.3 fusion.20.x_ref
  431.3 39.7 %gather_residual.1 = bf16[2048,2048]{1,0:T(8,128)(2,1)} custom-call(bf16[256,2048]{1,0:T(8,128)(2,1)} %fusion.20.x_ref), custom_call_target="tpu_custom_call" | custom-call | bytes 4194304 | tf_op jit(solution)/shard_map/gather_residual/pallas_call | solution.py:812
  471.1 5.9 convolution_convert_fusion.2.do_ref
  477.1 18.7 %attn_bwd.1 = (f32[2048,256]{1,0:T(8,128)S(1)}, f32[2048,256]{1,0:T(8,128)S(1)}, f32[2048,256]{1,0:T(8,128)S(1)}) custom-call(s32[8]{0:T(128)S(1)} %and_select_fusion.lo_ref, bf16[2048,256]{1,0:T(8,128)(2,1)S(1)} %copy-done.3, bf16[2048,256]{1,0:T(8,128)(2,1)S(1)} %copy-done.5, bf16[2048,256]{1,0:T(8,128)(2,1)S(1)} %copy-done.7, ...), custom_call_target="tpu_custom_call" | custom-call | flops 100000000 | bytes 4194304 | tf_op jit(solution)/shard_map/attn_bwd/pallas_call | solution.py:233
  504.3 6.0 multiply_reduce_fusion.2
  513.1 51.1 %moe_out.1 = f32[256,2048]{1,0:T(8,128)} custom-call(bf16[2048,2048]{1,0:T(8,128)(2,1)} %get-tuple-element.95.l_hbm, bf16[2048,2048]{1,0:T(8,128)(2,1)} %bitcast.100), custom_call_target="tpu_custom_call" | custom-call | flops 1000000000 | bytes 4194304 | tf_op jit(solution)/shard_map/moe_out/pallas_call | solution.py:759
  565.7 6.9 convolution_convert_fusion.1
  578.6 46.7 %normed_back.1 = f32[256,2048]{1,0:T(8,128)} custom-call(bf16[2048,768]{1,0:T(8,128)(2,1)} %pad_maximum_fusion.1.l_hbm, bf16[2048,768]{1,0:T(8,128)(2,1)} %pad_maximum_fusion.2.r_hbm), custom_call_target="tpu_custom_call" | custom-call | flops 1000000000 | bytes 4194304 | tf_op jit(solution)/shard_map/normed_back/pallas_call | solution.py:759
  625.4 2.3 fusion.7
  627.7 9.3 %convolution_convert_fusion = bf16[2048,768]{0,1:T(8,128)(2,1)S(1)} fusion(bf16[2048,2048]{1,0:T(8,128)(2,1)} %get-tuple-element.73, bf16[2048,256]{1,0:T(8,128)(2,1)S(1)} %convert_element_type.81, bf16[2048,256]{1,0:T(8,128)(2,1)S(1)} %get-tuple-element.231, bf16[2048,256]{1,0:T(8,128)(2,1)S(1)} %copy-done.38), kind=kOutput, calls=%fused_computation.1 | convolution fusion | flops 6453460992 | bytes 14680064 | tf_op jit(solution)/shard_map/dot_general | solution.py:32
  639.4 6.0 fusion.6
  645.4 11.0 %reduce-scatter.5.cloned.1.call-done = bf16[1,24,512,128]{3,2,1,0:T(8,128)(2,1)} async-done(((bf16[4,24,512,128]{3,2,1,0:T(8,128)(2,1)}), bf16[1,24,512,128]{3,2,1,0:T(8,128)(2,1)}) %reduce-scatter.5.cloned.1.call-update) | async-done | bytes 3145744 | tf_op jit(solution)/shard_map/reduce_scatter | solution.py:971
  662.1 5.5 collective-permute-done.9
  669.3 4.5 collective-permute-done.10
  676.9 12.2 %collective-permute-done.11 = f32[17,2048]{1,0:T(8,128)S(1)} collective-permute-done((f32[17,2048]{1,0:T(8,128)S(1)}, f32[17,2048]{1,0:T(8,128)S(1)}, u32[]{:S(2)}, u32[]{:S(2)}) %collective-permute-start.11) | collective-permute-done | bytes 139296 | tf_op jit(solution)/shard_map/ppermute | solution.py:829
  694.4 20.9 %collective-permute-done.12 = f32[17,2048]{1,0:T(8,128)} collective-permute-done((f32[17,2048]{1,0:T(8,128)}, f32[17,2048]{1,0:T(8,128)}, u32[]{:S(2)}, u32[]{:S(2)}) %collective-permute-start.12) | collective-permute-done | bytes 139296 | tf_op jit(solution)/shard_map/ppermute | solution.py:829
  717.7 4.4 collective-permute-done.6
  726.1 2.4 collective-permute-done.7
  729.1 3.1 fusion.23
  733.5 3.6 maximum_convert_fusion.2
  741.8 4.3 reduce-scatter.11.cloned.1.call-done
  (236 shorter events, 83.9 us)
Async XLA Ops:
  7.2 123.9 %all-gather.3.cloned.1.call-start = ((), (), s32[]{:S(2)}) async-start(), calls=%async_computation.5 | async-start | bytes 9437184 | tf_op jit(solution)/shard_map/all_gather | solution.py:902
  7.9 183.1 %all-gather.5.cloned.1.call-start = ((), (), s32[]{:S(2)}) async-start(), calls=%async_computation.6 | async-start | bytes 9437184 | tf_op jit(solution)/shard_map/all_gather | solution.py:939
  11.0 78.1 %copy-start.13 = (s32[1,2048]{1,0:T(1,128)S(1)}, s32[1,2048]{1,0:T(1,128)}, u32[]{:S(2)}) copy-start(s32[1,2048]{1,0:T(1,128)} %param.17) | copy-start | bytes 24580
  88.9 269.5 %reduce-scatter.9.cloned.1.call-start = ((), (), s32[]{:S(2)}) async-start(), calls=%async_computation.9 | async-start | bytes 3932160 | tf_op jit(solution)/shard_map/reduce_scatter | solution.py:971
  131.1 7.8 %copy-start.54 = (f32[2048]{0:T(1024)S(1)}, f32[2048]{0:T(1024)}, u32[]{:S(2)}) copy-start(f32[2048]{0:T(1024)} %param.26) | copy-start | bytes 24580
  217.1 283.6 %reduce-scatter.7.cloned.1.call-start = ((), (), s32[]{:S(2)}) async-start(), calls=%async_computation.8 | async-start | bytes 11796480 | tf_op jit(solution)/shard_map/reduce_scatter | solution.py:971
  270.3 386.0 %reduce-scatter.5.cloned.1.call-start = ((), (), s32[]{:S(2)}) async-start(), calls=%async_computation.7 | async-start | bytes 15728640 | tf_op jit(solution)/shard_map/reduce_scatter | solution.py:971
  348.3 8.8 %all-to-all-start = ((f32[8,256,16]{1,2,0:T(8,128)}), f32[8,256,16]{1,2,0:T(8,128)S(1)}, u32[]{:S(2)}, u32[]{:S(2)}) async-start(f32[8,256,16]{1,2,0:T(8,128)} %copy.145), calls=%async_computation.3 | async-start | bytes 262144 | tf_op jit(solution)/shard_map/all_to_all | solution.py:976
  351.7 394.5 %reduce-scatter.11.cloned.1.call-start = ((), (), s32[]{:S(2)}) async-start(), calls=%async_computation.10 | async-start | bytes 5242880 | tf_op jit(solution)/shard_map/reduce_scatter | solution.py:1030
  358.4 65.8 %copy-start.18 = (f32[256,2048]{1,0:T(8,128)S(1)}, f32[256,2048]{1,0:T(8,128)}, u32[]{:S(2)}) copy-start(f32[256,2048]{1,0:T(8,128)} %copy-done.17) | copy-start | bytes 6291460
  431.3 39.7 %copy-start.45 = (bf16[256,2048]{1,0:T(8,128)(2,1)S(1)}, bf16[256,2048]{1,0:T(8,128)(2,1)}, u32[]{:S(2)}) copy-start(bf16[256,2048]{1,0:T(8,128)(2,1)} %param.22) | copy-start | bytes 3145732
  510.3 1.4 collective-permute-start
  511.7 52.5 %collective-permute-start.1 = (f32[2,2048]{1,0:T(2,128)S(1)}, f32[2,2048]{1,0:T(2,128)S(1)}, u32[]{:S(2)}, u32[]{:S(2)}) collective-permute-start(f32[2,2048]{1,0:T(2,128)S(1)} %fusion.18), channel_id=1, source_target_pairs={{0,2},{1,3},{2,0},{3,1},{4,6},{5,7},{6,4},{7,5},{8,10},{9,11},{10,... | collective-permute-start | bytes 49160 | tf_op jit(solution)/shard_map/ppermute | solution.py:829
  513.1 52.7 %copy-start.15 = (bf16[2048,256]{1,0:T(8,128)(2,1)S(1)}, bf16[2048,256]{1,0:T(8,128)(2,1)}, u32[]{:S(2)}) copy-start(bf16[2048,256]{1,0:T(8,128)(2,1)} %copy-done.14) | copy-start | bytes 3145732
  564.2 8.5 %collective-permute-start.2 = (f32[2,2048]{1,0:T(2,128)S(1)}, f32[2,2048]{1,0:T(2,128)S(1)}, u32[]{:S(2)}, u32[]{:S(2)}) collective-permute-start(f32[2,2048]{1,0:T(2,128)S(1)} %fusion.42), channel_id=1, source_target_pairs={{0,4},{1,5},{2,6},{3,7},{4,0},{5,1},{6,2},{7,3},{8,12},{9,13},{10,... | collective-permute-start | bytes 49160 | tf_op jit(solution)/shard_map/ppermute | solution.py:829
  565.7 7.1 copy-start.28
  565.7 7.1 copy-start.29
  578.6 46.7 %copy-start.21 = (bf16[256,2048]{1,0:T(8,128)(2,1)S(1)}, bf16[256,2048]{1,0:T(8,128)(2,1)}, u32[]{:S(2)}) copy-start(bf16[256,2048]{1,0:T(8,128)(2,1)} %x_hbm.1) | copy-start | bytes 3145732
  578.6 46.7 %copy-start.55 = (f32[2048]{0:T(1024)S(1)}, f32[2048]{0:T(1024)}, u32[]{:S(2)}) copy-start(f32[2048]{0:T(1024)} %param.23) | copy-start | bytes 24580
  627.7 9.3 %copy-start.51 = (bf16[2048,256]{0,1:T(8,128)(2,1)S(1)}, bf16[2048,256]{0,1:T(8,128)(2,1)}, u32[]{:S(2)}) copy-start(bf16[2048,256]{0,1:T(8,128)(2,1)} %convolution_convert_fusion.1) | copy-start | bytes 3145732
  657.6 35.7 %copy-start.52 = (bf16[1,6,512,128]{3,2,1,0:T(8,128)(2,1)S(1)}, bf16[1,6,512,128]{3,2,1,0:T(8,128)(2,1)}, u32[]{:S(2)}) copy-start(bf16[1,6,512,128]{3,2,1,0:T(8,128)(2,1)} %reduce-scatter.9.cloned.1.call-done) | copy-start | bytes 2359300
  659.0 1.5 collective-permute-start.8
  660.5 7.0 collective-permute-start.9
  667.6 6.2 collective-permute-start.10
  669.2 6.2 collective-permute-start.3
  673.8 15.3 %collective-permute-start.11 = (f32[17,2048]{1,0:T(8,128)S(1)}, f32[17,2048]{1,0:T(8,128)S(1)}, u32[]{:S(2)}, u32[]{:S(2)}) collective-permute-start(f32[17,2048]{1,0:T(8,128)S(1)} %add.122), channel_id=1, source_target_pairs={{0,8},{8,0},{16,24},{24,16},{1,9},{9,1},{17,25},{25,17},{2,10},{10... | collective-permute-start | bytes 417800 | tf_op jit(solution)/shard_map/ppermute | solution.py:829
  675.5 47.5 %copy-start.44 = (bf16[1,18,512,128]{3,2,1,0:T(8,128)(2,1)S(1)}, bf16[1,18,512,128]{3,2,1,0:T(8,128)(2,1)}, u32[]{:S(2)}) copy-start(bf16[1,18,512,128]{3,2,1,0:T(8,128)(2,1)} %reduce-scatter.7.cloned.1.call-done) | copy-start | bytes 7077892
  675.5 15.9 %collective-permute-start.4 = (f32[3,2048]{1,0:T(4,128)S(1)}, f32[3,2048]{1,0:T(4,128)S(1)}, u32[]{:S(2)}, u32[]{:S(2)}) collective-permute-start(f32[3,2048]{1,0:T(4,128)S(1)} %fusion.19), channel_id=1, source_target_pairs={{0,2},{1,3},{2,0},{3,1},{4,6},{5,7},{6,4},{7,5},{8,10},{9,11},{10,... | collective-permute-start | bytes 73736 | tf_op jit(solution)/shard_map/ppermute | solution.py:829
  689.8 25.5 %collective-permute-start.12 = (f32[17,2048]{1,0:T(8,128)}, f32[17,2048]{1,0:T(8,128)}, u32[]{:S(2)}, u32[]{:S(2)}) collective-permute-start(f32[17,2048]{1,0:T(8,128)} %add.123), channel_id=1, source_target_pairs={{0,16},{8,24},{16,0},{24,8},{1,17},{9,25},{17,1},{25,9},{2,18},{10... | collective-permute-start | bytes 417800 | tf_op jit(solution)/shard_map/ppermute | solution.py:829
  691.4 24.9 %collective-permute-start.5 = (f32[3,2048]{1,0:T(4,128)S(1)}, f32[3,2048]{1,0:T(4,128)S(1)}, u32[]{:S(2)}, u32[]{:S(2)}) collective-permute-start(f32[3,2048]{1,0:T(4,128)S(1)} %fusion.41), channel_id=1, source_target_pairs={{0,4},{1,5},{2,6},{3,7},{4,0},{5,1},{6,2},{7,3},{8,12},{9,13},{10,... | collective-permute-start | bytes 73736 | tf_op jit(solution)/shard_map/ppermute | solution.py:829
  716.3 5.7 collective-permute-start.6
  722.1 6.4 collective-permute-start.7
  (47 other events, 135.6 us)
Sparse Core Ops, SparseCore 0:
  9.9 78.8 all-gather.2
  90.7 73.9 all-gather.4
  217.2 60.6 reduce-scatter.8
  280.1 161.2 reduce-scatter.6
  443.6 212.6 reduce-scatter.4
  658.5 87.6 reduce-scatter.10

commit v4 on v3

--- a/solution.py
+++ b/solution.py
@@ -478,11 +478,25 @@
     return copy, arrived, pc, px, py, diag
 
 
-def project_body(
-    x_hbm, wq_hbm, wk_hbm, wv_hbm, gain_ref, qg_ref, kg_ref, pos_ref,
-    normed_hbm, q_ref, k_ref, v_ref, qu_ref, ku_ref, rs_ref, cos_ref, sin_ref,
-    x_v, n_v, w_v, sums, sums_all, send_sem, recv_sem, ss_send, ss_recv, w_sem, x_sem, n_sem, *, size
+def front_body(
+    x_hbm, wo_hbm, g_hbm, wq_hbm, wk_hbm, wv_hbm, gain_ref, qg_ref, kg_ref, mg_ref, pos_ref, sq_ref, sk_ref,
+    normed_hbm, *rest, size, block, reach
 ):
+    outs, rest = rest[:13], rest[13:]
+    g_all, rest = rest[0], rest[1:]
+    local, rest = rest[:13], rest[13:]
+    (
+        q_ref, k_ref, v_ref, qu_ref, ku_ref, rs_ref, cos_ref, sin_ref, o_ref, low_ref, lse_ref, res_ref, moe_ref,
+    ) = local
+    (
+        x_v, n_v, w_v, wo_all, own_ref, sums, sums_all,
+        send_sem, recv_sem, wo_send, wo_recv, g_send, g_recv, ss_send, ss_recv, a_send, a_recv,
+        w_sem, x_sem, wo_sem, g_sem, a_sem, n_sem, o_sem,
+    ) = rest
+
+    def written(i):
+        return pltpu.make_async_copy(local[i], outs[i], o_sem.at[i])
+
     me = lax.axis_index("tensor")
     own = x_hbm.shape[0]
     width = x_hbm.shape[1]
@@ -500,8 +514,14 @@
         w.start()
     greet([lax.rem(me + t, size) for t in range(1, size)])
     copy, arrived, pc, px, py, diag = gather_plan(x_hbm, x_v, me, own, send_sem, recv_sem)
+    wo_copy, wo_arrived = gather_plan(wo_hbm, wo_all, me, own, wo_send, wo_recv)[:2]
     for k in range(5):
         copy(k).start()
+    g_copy, g_arrived = gather_plan(g_hbm, g_all, me, own, g_send, g_recv)[:2]
+    wo_here = pltpu.make_async_copy(wo_hbm, wo_all.at[mine], wo_sem)
+    wo_here.start()
+    g_here = pltpu.make_async_copy(g_hbm, g_all.at[mine], g_sem)
+    g_here.start()
 
     lane = lax.broadcasted_iota(jnp.int32, (own, HEAD_DIM), 1)
     power = (lane % half_dim).astype(F32) * (-2.0 * math.log(10000.0) / HEAD_DIM)
@@ -516,6 +536,8 @@
         return 0
 
     lax.fori_loop(0, size, table, 0)
+    for i in (6, 7):
+        written(i).start()
 
     def stored(dev):
         r = pl.ds(pl.multiple_of(dev * own, own), own)
@@ -544,6 +566,324 @@
     here.wait()
     for w in weights:
         w.wait()
+    process(me)
+    arrived(4).wait_recv()
+    process(pc)
+    arrived(0).wait_recv()
+    copy(5).start()
+    copy(7).start()
+    arrived(1).wait_recv()
+    copy(6).start()
+    copy(8).start()
+    arrived(2).wait_recv()
+    copy(9).start()
+    arrived(3).wait_recv()
+    copy(10).start()
+    for k in range(5):
+        wo_copy(k).start()
+    process(px)
+    process(py)
+    arrived(7).wait_recv()
+    arrived(9).wait_recv()
+    process(partner(px, 1))
+    arrived(8).wait_recv()
+    arrived(10).wait_recv()
+    process(partner(py, 1))
+    arrived(5).wait_recv()
+    copy(11).start()
+    arrived(6).wait_recv()
+    copy(12).start()
+    process(diag)
+    arrived(11).wait_recv()
+    arrived(12).wait_recv()
+    process(partner(diag, 1))
+    hand_on(wo_arrived, wo_copy, ((0, (5, 7)), (1, (6, 8))))
+
+    def exchange(t, src):
+        other = lax.rem(me + t, size)
+        slot = me if src is None else other
+        return remote(sums, sums_all.at[slot], ss_send.at[other], ss_recv.at[slot], other)
+
+    for t in range(1, size):
+        exchange(t, None).start()
+    sums_all[me] = sums[...]
+    hand_on(wo_arrived, wo_copy, ((2, (9,)), (3, (10,))))
+    for k in range(5):
+        g_copy(k).start()
+    for t in range(1, size):
+        exchange(t, 1).wait_recv()
+    total = sums_all[0]
+    for d in range(1, size):
+        total = total + sums_all[d]
+    rows_iota = lax.broadcasted_iota(jnp.int32, (HEAD_DIM, own), 0)
+    for d in range(size):
+        r = slice(d * own, (d + 1) * own)
+        tot = total[d]
+        both = jnp.where(rows_iota == 0, tot[0:1, :], tot[1:2, :])
+        rs = lax.rsqrt(both / width + EPS).T
+        rs_ref[r, :] = rs[:, 0:2]
+        cos, sin = cos_ref[r, :], sin_ref[r, :]
+        for j, (unit_ref, gain, dst) in enumerate(((qu_ref, qg_ref, q_ref), (ku_ref, kg_ref, k_ref))):
+            unit = unit_ref[r, :] * rs[:, j : j + 1]
+            unit_ref[r, :] = unit
+            wide = unit * gain[...]
+            for h in range(heads):
+                c = slice(h * HEAD_DIM, (h + 1) * HEAD_DIM)
+                w = wide[:, c]
+                dst[r, c] = (w * cos + pltpu.roll(w, half_dim, 1) * sin).astype(BF)
+
+    for i in range(6):
+        written(i).start()
+    score_scale = 1.0 / math.sqrt(HEAD_DIM)
+    row0 = lax.broadcasted_iota(jnp.int32, (block, block), 0)
+    col0 = lax.broadcasted_iota(jnp.int32, (block, block), 1)
+    hc = [slice(h * HEAD_DIM, (h + 1) * HEAD_DIM) for h in range(heads)]
+
+    def land(src):
+        return own_ref.at[:, pl.ds(pl.multiple_of(src * cols, HEAD_DIM), cols)]
+
+    def rows_of(dev):
+        return low_ref.at[pl.ds(pl.multiple_of(dev * own, own), own)]
+
+    def send(t):
+        return remote(rows_of(t), land(me), a_send.at[t], a_recv.at[me], t)
+
+    def query_block(qb, _):
+        rq = pl.ds(pl.multiple_of(qb * block, block), block)
+        seg_q = sq_ref[rq, :]
+        qs = [q_ref[rq, c] for c in hc]
+
+        def step(kb, carry):
+            rows = pl.ds(pl.multiple_of(kb * block, block), block)
+            allowed = (seg_q == sk_ref[kb]) & (kb * block + col0 <= qb * block + row0)
+            out = []
+            for h in range(heads):
+                m, l, acc = carry[h]
+                s = jnp.where(allowed, dot_nt(qs[h], k_ref[rows, hc[h]]) * score_scale, NEG)
+                m_new = jnp.maximum(m, jnp.max(s, axis=1, keepdims=True))
+                p = jnp.exp(s - m_new)
+                alpha = jnp.exp(m - m_new)
+                l = alpha * l + jnp.sum(p, axis=1, keepdims=True)
+                acc = alpha * acc + dot_nn(p.astype(BF), v_ref[rows, hc[h]])
+                out.append((m_new, l, acc))
+            return tuple(out)
+
+        init = tuple(
+            (
+                jnp.full((block, 1), NEG, F32),
+                jnp.zeros((block, 1), F32),
+                jnp.zeros((block, HEAD_DIM), F32),
+            )
+            for _ in range(heads)
+        )
+        final = lax.fori_loop(jnp.maximum(qb - reach, 0), qb + 1, step, init)
+        for h in range(heads):
+            m, l, acc = final[h]
+            out = acc / l
+            o_ref[rq, hc[h]] = out
+            low_ref[rq, hc[h]] = out.astype(BF)
+            lse_ref[rq, h : h + 1] = m + jnp.log(l)
+
+        @pl.when(qb != me)
+        def _():
+            send(qb).start()
+
+        @pl.when(qb == me)
+        def _():
+            pltpu.make_async_copy(rows_of(me), land(me), a_sem).start()
+
+        @pl.when(qb == 3)
+        def _():
+            hand_on(wo_arrived, wo_copy, ((5, (11,)), (6, (12,))))
+
+        @pl.when(qb == 5)
+        def _():
+            hand_on(g_arrived, g_copy, ((0, (5, 7)), (1, (6, 8))))
+
+        return 0
+
+    lax.fori_loop(0, size, query_block, 0)
+    for i in (8, 9, 10):
+        written(i).start()
+    pltpu.make_async_copy(rows_of(me), land(me), a_sem).wait()
+    for t in range(1, size):
+        other = lax.rem(me + t, size)
+        remote(rows_of(other), land(other), a_send.at[other], a_recv.at[other], other).wait_recv()
+    for k in (4, 7, 8, 9, 10, 11, 12):
+        wo_arrived(k).wait_recv()
+    wo_here.wait()
+    sl = width // 4
+    total = jnp.zeros((own, 1), F32)
+    for i in range(4):
+        c = slice(i * sl, (i + 1) * sl)
+        part = x_v[mine, c].astype(F32) + dot_nn(own_ref[...], wo_all[:, c])
+        res_ref[:, c] = part
+        total = total + jnp.sum(part * part, axis=1, keepdims=True)
+    scale = lax.rsqrt(total / width + EPS)
+    for i in range(4):
+        c = slice(i * sl, (i + 1) * sl)
+        moe_ref[:, c] = (res_ref[:, c] * scale * mg_ref[:, c]).astype(BF)
+    for i in (11, 12):
+        written(i).start()
+    hand_on(g_arrived, g_copy, ((2, (9,)), (3, (10,)), (5, (11,)), (6, (12,))))
+    for t in range(1, size):
+        exchange(t, None).wait_send()
+        send(lax.rem(me + t, size)).wait_send()
+    for d in range(size):
+        stored(d).wait()
+    for k in (4, 7, 8, 9, 10, 11, 12):
+        g_arrived(k).wait_recv()
+    for k in range(GATHER_COPIES):
+        copy(k).wait_send()
+        wo_copy(k).wait_send()
+        g_copy(k).wait_send()
+    g_here.wait()
+    for i in range(13):
+        written(i).wait()
+
+
+def hand_on(arrived, copy, steps):
+    for k, following in steps:
+        arrived(k).wait_recv()
+        for f in following:
+            copy(f).start()
+
+
+def front(x, wo, g, wq, wk, wv, gain, qg, kg, mg, pos, seg_col, seg_rows, size, block, reach, cid):
+    own, width = x.shape
+    cols = wq.shape[1]
+    tokens = own * size
+    heads = cols // HEAD_DIM
+    any_spec = pl.BlockSpec(memory_space=pl.ANY)
+    vm = pl.BlockSpec(memory_space=pltpu.VMEM)
+    arr = jax.ShapeDtypeStruct
+    dma = pltpu.SemaphoreType.DMA
+    kept = (
+            arr((tokens, cols), BF),
+            arr((tokens, cols), BF),
+            arr((tokens, cols), BF),
+            arr((tokens, cols), F32),
+            arr((tokens, cols), F32),
+            arr((tokens, 2), F32),
+            arr((tokens, HEAD_DIM), F32),
+            arr((tokens, HEAD_DIM), F32),
+            arr((tokens, cols), F32),
+            arr((tokens, cols), BF),
+            arr((tokens, heads), F32),
+            arr((own, width), F32),
+            arr((own, width), BF),
+    )
+    return pl.pallas_call(
+        functools.partial(front_body, size=size, block=block, reach=reach),
+        out_shape=(
+            arr((tokens, width), BF),
+            *kept,
+            arr((tokens, width), BF),
+        ),
+        in_specs=[any_spec] * 6 + [vm] * 7,
+        out_specs=[any_spec] * 15,
+        scratch_shapes=[pltpu.VMEM(k.shape, k.dtype) for k in kept]
+        + [
+            pltpu.VMEM((tokens, width), BF),
+            pltpu.VMEM((tokens, width), BF),
+            pltpu.VMEM((width, 3 * cols), BF),
+            pltpu.VMEM((width, width), BF),
+            pltpu.VMEM((own, width), BF),
+            pltpu.VMEM((size, 2, own), F32),
+            pltpu.VMEM((size, size, 2, own), F32),
+        ]
+        + [dma((GATHER_COPIES,))] * 6
+        + [dma((size,))] * 4
+        + [
+            dma((3,)),
+            dma,
+            dma,
+            dma,
+            dma,
+            dma((size,)),
+            dma((13,)),
+        ],
+        compiler_params=pltpu.CompilerParams(
+            vmem_limit_bytes=58 * MIB, collective_id=cid, has_side_effects=True
+        ),
+        cost_estimate=pl.CostEstimate(flops=10**8, bytes_accessed=4 * MIB, transcendentals=0),
+        name="front",
+    )(x, wo, g, wq, wk, wv, gain[None, :], qg[None, :], kg[None, :], mg[None, :], pos, seg_col, seg_rows)
+
+
+def middle_body(
+    own_hbm, g_hbm, mask_ref, router_ref, wg_ref, wu_ref, wd_ref,
+    moe_hbm, dgu_hbm, ga_hbm, wcat_hbm, dots_ref, grads_ref, xt_hbm, gates_ref, probs_ref,
+    x_v, xt_v, g_v, wcat, dgu_v, ga_v, send_sem, recv_sem, own_sem, g_sem, m_sem, out_sem, *, size, parts
+):
+    me = lax.axis_index("tensor")
+    tokens, width = x_v.shape
+    own = tokens // size
+    hid = wg_ref.shape[2]
+    experts = gates_ref.shape[1]
+    ds = width // parts
+
+    def g_copy(d):
+        r = pl.ds(d * own, own)
+        return pltpu.make_async_copy(g_hbm.at[r], g_v.at[r], g_sem.at[d])
+
+    mine = pl.ds(pl.multiple_of(me * own, own), own)
+    own_copy = pltpu.make_async_copy(own_hbm, x_v.at[mine], own_sem)
+    own_copy.start()
+    greet([partner(me, b) for b in (1, 2, 4)])
+    copy, arrived, pc, px, py, diag = gather_plan(own_hbm, x_v, me, own, send_sem, recv_sem)
+    for k in range(5):
+        copy(k).start()
+    for d in range(size):
+        g_copy(d).start()
+
+    wcat[:, 0:hid] = wg_ref[0]
+    wcat[:, hid : 2 * hid] = wg_ref[1]
+    wcat[:, 2 * hid : 3 * hid] = wu_ref[0]
+    wcat[:, 3 * hid : 4 * hid] = wu_ref[1]
+    wcat_out = pltpu.make_async_copy(wcat, wcat_hbm.at[:, pl.ds(0, 4 * hid)], out_sem.at[0])
+    wcat_out.start()
+    own_copy.wait()
+    for d in range(size):
+        g_copy(d).wait()
+    lane = lax.broadcasted_iota(jnp.int32, (own, experts), 1)
+
+    def moe_out(dev):
+        r = pl.ds(pl.multiple_of(dev * own, own), own)
+        return pltpu.make_async_copy(x_v.at[r], moe_hbm.at[r], m_sem.at[dev])
+
+    def process(dev):
+        r = pl.ds(pl.multiple_of(dev * own, own), own)
+        moe_out(dev).start()
+        xt_v[:, r] = x_v[r, :].T
+        logits = dot_nn(x_v[r, :], router_ref[...])
+        grown = jnp.exp(logits - jnp.max(logits, axis=1, keepdims=True))
+        probs = grown / jnp.sum(grown, axis=1, keepdims=True)
+        probs_ref[r, :] = probs
+        gate_rows = probs * mask_ref[r, :]
+        gates_ref[r, :] = gate_rows
+        gu = dot_nn(x_v[r, :], wcat[...])
+        q = dot_nt(g_v[r, :], wd_ref[...])
+        dots = jnp.zeros((own, experts), F32)
+        for j in range(2):
+            pre = gu[:, j * hid : (j + 1) * hid]
+            up = gu[:, (2 + j) * hid : (3 + j) * hid]
+            back = q[:, j * hid : (j + 1) * hid]
+            here = lane == j
+            gate = jnp.sum(jnp.where(here, gate_rows, 0.0), axis=1, keepdims=True)
+            sig = jax.nn.sigmoid(pre)
+            silu = pre * sig
+            act = silu * up
+            dot = jnp.sum(act * back, axis=1, keepdims=True)
+            dots = dots + jnp.where(here, dot, 0.0)
+            scaled = gate * back
+            d_up = scaled * silu
+            d_gate = scaled * up * (sig + silu * (1.0 - sig))
+            dgu_v[r, j * hid : (j + 1) * hid] = d_gate.astype(BF)
+            dgu_v[r, (2 + j) * hid : (3 + j) * hid] = d_up.astype(BF)
+            ga_v[r, j * hid : (j + 1) * hid] = (gate * act).astype(BF)
+        dots_ref[r, :] = dots
+
     process(me)
     arrived(4).wait_recv()
     process(pc)
@@ -574,84 +914,98 @@
     arrived(12).wait_recv()
     process(partner(diag, 1))
 
-    def exchange(t, src):
-        other = lax.rem(me + t, size)
-        slot = me if src is None else other
-        return remote(sums, sums_all.at[slot], ss_send.at[other], ss_recv.at[slot], other)
-
-    for t in range(1, size):
-        exchange(t, None).start()
-    sums_all[me] = sums[...]
-    for t in range(1, size):
-        exchange(t, 1).wait_recv()
-    total = sums_all[0]
-    for d in range(1, size):
-        total = total + sums_all[d]
-    rows_iota = lax.broadcasted_iota(jnp.int32, (HEAD_DIM, own), 0)
+    outs = [
+        pltpu.make_async_copy(dgu_v, dgu_hbm.at[:, pl.ds(0, 4 * hid)], out_sem.at[1]),
+        pltpu.make_async_copy(ga_v, ga_hbm.at[:, pl.ds(0, 2 * hid)], out_sem.at[2]),
+        pltpu.make_async_copy(xt_v, xt_hbm, out_sem.at[3]),
+    ]
+    for o in outs:
+        o.start()
+    for s in range(parts):
+        gd = dot_tn(ga_v[...], g_v[:, s * ds : (s + 1) * ds]).astype(BF)
+        gw = dot_nn(xt_v[s * ds : (s + 1) * ds, :], dgu_v[...]).astype(BF)
+        for j in range(2):
+            grads_ref[s, 3 * j] = gw[:, j * hid : (j + 1) * hid]
+            grads_ref[s, 3 * j + 1] = gw[:, (2 + j) * hid : (3 + j) * hid]
+            for c in range(ds // hid):
+                grads_ref[s, 3 * j + 2, c * hid : (c + 1) * hid, :] = gd[
+                    j * hid : (j + 1) * hid, c * hid : (c + 1) * hid
+                ]
+    wcat_out.wait()
+    for o in outs:
+        o.wait()
     for d in range(size):
-        r = slice(d * own, (d + 1) * own)
-        tot = total[d]
-        both = jnp.where(rows_iota == 0, tot[0:1, :], tot[1:2, :])
-        rs = lax.rsqrt(both / width + EPS).T
-        rs_ref[r, :] = rs[:, 0:2]
-        cos, sin = cos_ref[r, :], sin_ref[r, :]
-        for j, (unit_ref, gain, dst) in enumerate(((qu_ref, qg_ref, q_ref), (ku_ref, kg_ref, k_ref))):
-            unit = unit_ref[r, :] * rs[:, j : j + 1]
-            unit_ref[r, :] = unit
-            wide = unit * gain[...]
-            for h in range(heads):
-                c = slice(h * HEAD_DIM, (h + 1) * HEAD_DIM)
-                w = wide[:, c]
-                dst[r, c] = (w * cos + pltpu.roll(w, half_dim, 1) * sin).astype(BF)
-    for t in range(1, size):
-        exchange(t, None).wait_send()
+        moe_out(d).wait()
     for k in range(GATHER_COPIES):
         copy(k).wait_send()
-    for d in range(size):
-        stored(d).wait()
-
-
-def project(x, wq, wk, wv, gain, qg, kg, pos, size, cid):
-    own, width = x.shape
-    cols = wq.shape[1]
+
+
+def middle(own_rows, g, mask, router, wg, wu, wd, size, parts, cid):
+    own, width = own_rows.shape
     tokens = own * size
+    experts, _, hid = wg.shape
+    total = experts // 2
+    ds = width // parts
     any_spec = pl.BlockSpec(memory_space=pl.ANY)
     vm = pl.BlockSpec(memory_space=pltpu.VMEM)
+    first = lambda shape: pl.BlockSpec(shape, lambda i: (0,) * len(shape))
+    arr = jax.ShapeDtypeStruct
+    dma = pltpu.SemaphoreType.DMA
+    narrow = arr((tokens, experts), F32)
     return pl.pallas_call(
-        functools.partial(project_body, size=size),
+        functools.partial(middle_body, size=size, parts=parts),
         out_shape=(
-            jax.ShapeDtypeStruct((tokens, width), BF),
-            jax.ShapeDtypeStruct((tokens, cols), BF),
-            jax.ShapeDtypeStruct((tokens, cols), BF),
-            jax.ShapeDtypeStruct((tokens, cols), BF),
-            jax.ShapeDtypeStruct((tokens, cols), F32),
-            jax.ShapeDtypeStruct((tokens, cols), F32),
-            jax.ShapeDtypeStruct((tokens, 2), F32),
-            jax.ShapeDtypeStruct((tokens, HEAD_DIM), F32),
-            jax.ShapeDtypeStruct((tokens, HEAD_DIM), F32),
+            arr((tokens, width), BF),
+            arr((tokens, total * 4 * hid), BF),
+            arr((tokens, total * 2 * hid), BF),
+            arr((width, total * 4 * hid), BF),
+            narrow,
+            arr((parts, 6, ds, hid), BF),
+            arr((width, tokens), BF),
+            narrow,
+            narrow,
         ),
-        in_specs=[any_spec] * 4 + [vm] * 4,
-        out_specs=[any_spec] + [vm] * 8,
+        grid=(1,),
+        in_specs=[
+            any_spec,
+            any_spec,
+            first((tokens, experts)),
+            first(router.shape),
+            first((2, width, hid)),
+            first((2, width, hid)),
+            first((2 * hid, width)),
+        ],
+        out_specs=[
+            any_spec,
+            any_spec,
+            any_spec,
+            any_spec,
+            first((tokens, experts)),
+            first((parts, 6, ds, hid)),
+            any_spec,
+            first((tokens, experts)),
+            first((tokens, experts)),
+        ],
         scratch_shapes=[
             pltpu.VMEM((tokens, width), BF),
+            pltpu.VMEM((width, tokens), BF),
             pltpu.VMEM((tokens, width), BF),
-            pltpu.VMEM((width, 3 * cols), BF),
-            pltpu.VMEM((size, 2, own), F32),
-            pltpu.VMEM((size, size, 2, own), F32),
-            pltpu.SemaphoreType.DMA((GATHER_COPIES,)),
-            pltpu.SemaphoreType.DMA((GATHER_COPIES,)),
-            pltpu.SemaphoreType.DMA((size,)),
-            pltpu.SemaphoreType.DMA((size,)),
-            pltpu.SemaphoreType.DMA((3,)),
-            pltpu.SemaphoreType.DMA,
-            pltpu.SemaphoreType.DMA((size,)),
+            pltpu.VMEM((width, 4 * hid), BF),
+            pltpu.VMEM((tokens, 4 * hid), BF),
+            pltpu.VMEM((tokens, 2 * hid), BF),
+            dma((GATHER_COPIES,)),
+            dma((GATHER_COPIES,)),
+            dma,
+            dma((size,)),
+            dma((size,)),
+            dma((4,)),
         ],
         compiler_params=pltpu.CompilerParams(
-            vmem_limit_bytes=56 * MIB, collective_id=cid, has_side_effects=True
+            vmem_limit_bytes=62 * MIB, collective_id=cid, has_side_effects=True
         ),
-        cost_estimate=pl.CostEstimate(flops=10**8, bytes_accessed=4 * MIB, transcendentals=0),
-        name="project",
-    )(x, wq, wk, wv, gain[None, :], qg[None, :], kg[None, :], pos)
+        cost_estimate=pl.CostEstimate(flops=10**9, bytes_accessed=4 * MIB, transcendentals=0),
+        name="middle",
+    )(own_rows, g, mask, router, wg, wu, wd)
 
 
 def matmul_scatter_body(
@@ -837,8 +1191,23 @@
     return value
 
 
-def bits_of(size):
-    return [1 << b for b in range(size.bit_length() - 1)]
+def sum_everywhere(value, n_tensor, n_dp):
+    me = lax.axis_index("tensor")
+    bits = [1 << b for b in range(n_tensor.bit_length() - 1)]
+    for bit in bits[::-1]:
+        half = value.shape[1] // 2
+        low, high = value[:, :half], value[:, half:]
+        upper = (me // bit) % 2 == 1
+        send = jnp.where(upper, low, high)
+        value = jnp.where(upper, high, low) + swap(send, "tensor", n_tensor, bit)
+    value = sum_all(value, "dp", n_dp)
+    for bit in bits:
+        got = swap(value, "tensor", n_tensor, bit)
+        upper = (me // bit) % 2 == 1
+        value = jnp.concatenate(
+            [jnp.where(upper, got, value), jnp.where(upper, value, got)], axis=1
+        )
+    return value
 
 
 def half_swap(values):
@@ -899,15 +1268,26 @@
     mask = (routed_b * (place < capacity).astype(F32)).reshape(token_count, experts)
 
     w_qkv = jnp.concatenate([w_query, w_key, w_value], axis=1)
-    full_wo = lax.all_gather(w_output, "tensor", axis=0, tiled=True)
     pos_col = positions.astype(F32)[:, None]
+    input_own = block_input.astype(F32)
+    wd_flat = w_down.reshape(experts * hid, model_width)
+    reach = min(1024 // block, token_count // block)
     if n_tensor == 8:
-        normed, queries, keys_rot, value_low, query_unit, key_unit, scales, cos_one, sin_one = project(
-            block_input, w_query, w_key, w_value, attn_gain, query_gain, key_gain, pos_col, n_tensor, 6
+        (
+            normed, queries, keys_rot, value_low, query_unit, key_unit, scales, cos_one, sin_one,
+            attended, attn_low, lse, residual, own_moe_in, full_cot,
+        ) = front(
+            block_input, w_output, cotangent, w_query, w_key, w_value, attn_gain, query_gain, key_gain, moe_gain,
+            pos_col, seg_col, seg_rows,
+            n_tensor, block, reach, 6,
         )
         query_rs, key_rs = scales[:, 0:1], scales[:, 1:2]
         cos_all = jnp.concatenate([cos_one] * local_heads, axis=1)
         sin_all = jnp.concatenate([sin_one] * local_heads, axis=1)
+        lead = middle(
+            own_moe_in, full_cot, mask, router, w_gate, w_up, wd_flat, n_tensor, n_dp, 1
+        )
+        moe_in, lead = lead[0], lead[1:]
     else:
         half = HEAD_DIM // 2
         frequency = jnp.exp(
@@ -917,6 +1297,8 @@
         cosine, sine = jnp.cos(angles), jnp.sin(angles)
         cos_all = jnp.concatenate([cosine] * (2 * local_heads), axis=1)
         sin_all = jnp.concatenate([-sine, sine] * local_heads, axis=1)
+        full_cot = lax.all_gather(cotangent, "tensor", axis=0, tiled=True)
+        full_wo = lax.all_gather(w_output, "tensor", axis=0, tiled=True)
         input_wide = lax.all_gather(block_input, "tensor", axis=0, tiled=True).astype(F32)
         normed = (input_wide * rms_scale(input_wide) * attn_gain).astype(BF)
         qkv = dot_nn(normed, w_qkv)
@@ -935,30 +1317,25 @@
         k_n = key_unit * key_gain
         queries = (q_n * cos_all + half_swap(q_n) * sin_all).astype(BF)
         keys_rot = (k_n * cos_all + half_swap(k_n) * sin_all).astype(BF)
-    queries, cot_in = lax.optimization_barrier((queries, cotangent))
-    full_cot = lax.all_gather(cot_in, "tensor", axis=0, tiled=True)
-    reach = min(1024 // block, token_count // block)
-    attended, attn_low, lse, own_attn = attn_fwd(
-        queries, keys_rot, value_low, seg_col, seg_rows, block, reach, n_tensor, 0
-    )
-
-
-    input_own = block_input.astype(F32)
-    residual = input_own + dot_nn(own_attn, full_wo)
+        attended, attn_low, lse, own_attn = attn_fwd(
+            queries, keys_rot, value_low, seg_col, seg_rows, block, reach, n_tensor, 0
+        )
+        residual = input_own + dot_nn(own_attn, full_wo)
+        own_moe_in = (residual * rms_scale(residual) * moe_gain).astype(BF)
+        moe_in = lax.all_gather(own_moe_in, "tensor", axis=0, tiled=True)
+        lead = expert_chunk(
+            moe_in, full_cot, mask, w_gate, w_up, wd_flat, router, None, first=0, pairs=1, parts=n_dp
+        )
     scale_two = rms_scale(residual)
-    own_moe_in = (residual * scale_two * moe_gain).astype(BF)
-    moe_in = gather_all(own_moe_in, n_tensor, 1, "gather_moe")
-
-    wd_flat = w_down.reshape(experts * hid, model_width)
-    pairs_total = experts // 2
+
     chunks = (1, 3, 4)
     dots = None
     reduced = []
     carried = None
     first = 0
     for count in chunks:
-        res = expert_chunk(
-            moe_in, full_cot, mask if first == 0 else gates, w_gate, w_up, wd_flat, router, carried,
+        res = lead if first == 0 else expert_chunk(
+            moe_in, full_cot, gates, w_gate, w_up, wd_flat, router, carried,
             first=first, pairs=count, parts=n_dp,
         )
         dgu, ga, wcat, dot_c, grads = res[:5]
@@ -1013,6 +1390,7 @@
     qkv_grad = jnp.concatenate([query_grad_low, key_grad_low, dv.astype(BF)], axis=1)
     qkv_w_grad = dot_tn(normed, qkv_grad).astype(BF)
     normed_grad = matmul_scatter(qkv_grad, w_qkv, n_tensor, 4, True, "normed_back")
+    ga, qkv_w_grad = lax.optimization_barrier((ga, qkv_w_grad))
     moe_out = matmul_scatter(ga, wd_flat, n_tensor, 5, False, "moe_out")
     block_output = (residual + moe_out).astype(BF)
     scale_own = rms_scale(input_own)
@@ -1027,22 +1405,23 @@
     reduced[2], proj_grad, block_output, grad_input = lax.optimization_barrier(
         (reduced[2], proj_grad, block_output, grad_input)
     )
-    qkv_red = lax.psum_scatter(proj_grad, "dp", scatter_dimension=0, tiled=True).astype(F32)
-    wo_red = qkv_red[:, 3 * local_cols :].T
-    early = jnp.concatenate([router_grad, moe_gain_grad[None, :]], axis=0)
-    early = sum_all(sum_all(early, "tensor", n_tensor), "dp", n_dp)
-    gains = jnp.stack(
+    qkv_red = lax.psum_scatter(proj_grad, "dp", scatter_dimension=0, tiled=True)
+    wo_red = qkv_red[:, 3 * local_cols :].T.astype(F32)
+    gains = jnp.concatenate(
         [
-            attn_gain_grad,
+            router_grad,
+            moe_gain_grad[None, :],
+            attn_gain_grad[None, :],
             lax.dynamic_update_slice_in_dim(
-                jnp.zeros((model_width,), F32), query_gain_grad, col_start, 0
+                jnp.zeros((1, model_width), F32), query_gain_grad[None, :], col_start, 1
             ),
             lax.dynamic_update_slice_in_dim(
-                jnp.zeros((model_width,), F32), key_gain_grad, col_start, 0
+                jnp.zeros((1, model_width), F32), key_gain_grad[None, :], col_start, 1
             ),
-        ]
-    )
-    gains = sum_all(sum_all(gains, "tensor", n_tensor), "dp", n_dp)
+        ],
+        axis=0,
+    )
+    gains = sum_everywhere(gains, n_tensor, n_dp)
 
     ds = model_width // n_dp
     gate_out, up_out, down_out = [], [], []
@@ -1058,15 +1437,15 @@
     return (
         block_output,
         grad_input,
-        qkv_red[:, :local_cols],
-        qkv_red[:, local_cols : 2 * local_cols],
-        qkv_red[:, 2 * local_cols : 3 * local_cols],
+        qkv_red[:, :local_cols].astype(F32),
+        qkv_red[:, local_cols : 2 * local_cols].astype(F32),
+        qkv_red[:, 2 * local_cols : 3 * local_cols].astype(F32),
         wo_red,
-        gains[0],
-        gains[1],
-        gains[2],
-        early[experts],
-        early[:experts].T,
+        gains[experts + 1],
+        gains[experts + 2],
+        gains[experts + 3],
+        gains[experts],
+        gains[:experts].T,
         grad_gate,
         grad_up,
         grad_down,

time: 769 us -> 739 us (0.961)
  waiting for transfers between devices: 72.5 us -> 61.2 us
  local copies, waits for them, and re-layouts: 46.2 us -> 35.3 us
  matrix products: 34.1 us -> 24.6 us
    pallas_call x2, Pallas kernels: 111 us -> 182 us  [the longest x1 125 us: front(): pl.pallas_call(functools.partial(front_body, size=size, block=block, reac...]
    pallas_call x2 -> x1, Pallas kernels: 90.5 us -> 38.9 us  [gather_all(): pl.pallas_call(gather_body, out_shape=jax.ShapeDtypeStruct((own * size, c...]
    ppermute x13 -> x11, waiting for transfers between devices: 51.2 us -> 17.2 us  [swap(): return lax.ppermute(value, axis, [(i, i ^ bit) for i in range(size)])]
    reduce_scatter x1, waiting for transfers between devices: 4.32 us -> 33.3 us  [per_device(): qkv_red = lax.psum_scatter(proj_grad, 'dp', scatter_dimension=0, tiled=True)]
    pallas_call x3 -> x2, Pallas kernels: 146 us -> 120 us  [expert_chunk(): pl.pallas_call(functools.partial(expert_body, first=first, rows_blk=rows_...]
    unnamed x125 -> x97, local copies, waits for them, and re-layouts: 25.3 us -> 14.6 us
  transfers between devices with their start and end apart: 20 -> 16, of which waited for: 10 -> 11; matrix products, arithmetic and copies ran while one was open for 13% -> 11% of each run, Pallas kernels for 66% -> 48%
where the time goes in v4:
time: 739 us; the launch traced here: 728 us
  Pallas kernels  530 us (72%)
  waiting for transfers between devices  61.2 us (8%)
  other arithmetic  45.3 us (6%)
  local copies, waits for them, and re-layouts  35.3 us (5%)
  matrix products  24.6 us (3%)
  starting transfers between devices  17.6 us (2%)
  between operations  14.9 us (2%)
    pallas_call x3, Pallas kernels, matmul_scatter(): pl.pallas_call(functools.partial(matmul_scatter_body, size=size, slices=s...  166 us
    pallas_call x1, Pallas kernels, front(): pl.pallas_call(functools.partial(front_body, size=size, block=block, reac...  125 us
    pallas_call x2, Pallas kernels, expert_chunk(): pl.pallas_call(functools.partial(expert_body, first=first, rows_blk=rows_...  120 us
    pallas_call x1, Pallas kernels, middle(): pl.pallas_call(functools.partial(middle_body, size=size, parts=parts), ou...  57 us
    pallas_call x1, Pallas kernels, gather_all(): pl.pallas_call(gather_body, out_shape=jax.ShapeDtypeStruct((own * size, c...  38.9 us
    reduce_scatter x1, waiting for transfers between devices, per_device(): qkv_red = lax.psum_scatter(proj_grad, 'dp', scatter_dimension=0, tiled=True)  33.3 us
    pallas_call x1, Pallas kernels, attn_bwd(): pl.pallas_call(functools.partial(attn_bwd_body, block=block, heads=heads)...  22.3 us
    ppermute x11, waiting for transfers between devices, swap(): return lax.ppermute(value, axis, [(i, i ^ bit) for i in range(size)])  17.2 us
  transfers between devices with their start and end apart: 16, of which 11 were waited for; matrix products, arithmetic and copies ran while one was open for 11% of the time, Pallas kernels for 48%

profile of v4, /device:TPU:0, one launch (start us, length us, event | category | flops | bytes accessed | tf_op | source)
XLA Modules:
  0.0 728.4 jit_solution(3442288849681877755)
XLA Ops:
  14.7 125.1 %front.1 = (bf16[2048,2048]{1,0:T(8,128)(2,1)}, bf16[2048,256]{1,0:T(8,128)(2,1)}, bf16[2048,256]{1,0:T(8,128)(2,1)}, bf16[2048,256]{1,0:T(8,128)(2,1)}, f32[204...) custom-call(bf16[256,2048]{1,0:T(8,128)(2,1)} %x_hbm.1, ...), custom_call_target="tpu_custom_call" | custom-call | flops 100000000 | bytes 4194304 | tf_op jit(solution)/shard_map/front/pallas_call | solution.py:776
  139.7 57.0 %middle.1 = (bf16[2048,2048]{1,0:T(8,128)(2,1)}, bf16[2048,4096]{1,0:T(8,128)(2,1)}, bf16[2048,2048]{1,0:T(8,128)(2,1)}, bf16[2048,4096]{1,0:T(8,128)(2,1)}, f32...) custom-call(bf16[256,2048]{1,0:T(8,128)(2,1)} %get-tuple-element.61., ...), custom_call_target="tpu_custom_call" | custom-call | flops 1000000000 | bytes 4194304 | tf_op jit(solution)/shard_map/middle/pallas_call | solution.py:955
  196.8 53.0 %expert_chunk.2 = (bf16[2048,4096]{1,0:T(8,128)(2,1)}, bf16[2048,2048]{1,0:T(8,128)(2,1)}, bf16[2048,4096]{1,0:T(8,128)(2,1)}, f32[2048,16]{1,0:T(8,128)}, bf16[4,18,512,128]{3,2,1,0:T(8,128)(2,1)}) custom-call(bf16[2048,2048]{1,0:T(8,128)(2,1)} %get-tuple-element.63.refs_0_, ...), custom_call_target="tpu_custom_call", output_to_operand_aliasing={{0}: (7, {}), {1}: (8, {}), {2}: (9, {})} | custom-call | flops 1000000000 | bytes 4194304 | tf_op jit(solution)/shard_map/expert_chunk/pallas_call | solution.py:417
  249.8 67.3 %expert_chunk.3 = (bf16[2048,4096]{1,0:T(8,128)(2,1)}, bf16[2048,2048]{1,0:T(8,128)(2,1)}, bf16[2048,4096]{1,0:T(8,128)(2,1)}, f32[2048,16]{1,0:T(8,128)}, bf16[4,24,512,128]{3,2,1,0:T(8,128)(2,1)}) custom-call(bf16[2048,2048]{1,0:T(8,128)(2,1)} %get-tuple-element.63.refs_0_, ...), custom_call_target="tpu_custom_call", output_to_operand_aliasing={{0}: (7, {}), {1}: (8, {}), {2}: (9, {})} | custom-call | flops 1000000000 | bytes 4194304 | tf_op jit(solution)/shard_map/expert_chunk/pallas_call | solution.py:417
  318.4 2.8 add_add_fusion
  323.5 3.6 all-to-all-start
  335.3 67.6 %moe_back.1 = f32[256,2048]{1,0:T(8,128)} custom-call(bf16[2048,4096]{1,0:T(8,128)(2,1)} %get-tuple-element.83.l_hbm, bf16[2048,4096]{1,0:T(8,128)(2,1)} %get-tuple-element.84.r_hbm), custom_call_target="tpu_custom_call" | custom-call | flops 1000000000 | bytes 4194304 | tf_op jit(solution)/shard_map/moe_back/pallas_call | solution.py:1113
  402.9 2.6 multiply_reduce_fusion.2
  408.5 38.9 %gather_residual.1 = bf16[2048,2048]{1,0:T(8,128)(2,1)} custom-call(bf16[256,2048]{1,0:T(8,128)(2,1)} %fusion.19.x_ref), custom_call_target="tpu_custom_call" | custom-call | bytes 4194304 | tf_op jit(solution)/shard_map/gather_residual/pallas_call | solution.py:1166
  447.5 5.9 convolution_convert_fusion.2.do_ref
  453.5 22.3 %attn_bwd.1 = (f32[2048,256]{1,0:T(8,128)S(1)}, f32[2048,256]{1,0:T(8,128)S(1)}, f32[2048,256]{1,0:T(8,128)S(1)}) custom-call(s32[8]{0:T(128)S(1)} %and_select_fusion.lo_ref, bf16[2048,256]{1,0:T(8,128)(2,1)S(1)} %copy-done.5, bf16[2048,256]{1,0:T(8,128)(2,1)S(1)} %copy-done.6, bf16[2048,256]{1,0:T(8,128)(2,1)S(1)} %copy-done.7, ...), custom_call_target="tpu_custom_call" | custom-call | flops 100000000 | bytes 4194304 | tf_op jit(solution)/shard_map/attn_bwd/pallas_call | solution.py:233
  478.5 2.6 fusion.25
  484.7 5.2 multiply_reduce_fusion.1
  496.5 3.7 convolution_convert_fusion.1
  502.0 10.8 %convolution_convert_fusion = bf16[2048,768]{1,0:T(8,128)(2,1)} fusion(bf16[2048,2048]{1,0:T(8,128)(2,1)} %get-tuple-element.74, bf16[2048,256]{1,0:T(8,128)(2,1)S(1)} %convert_element_type.88, bf16[2048,256]{1,0:T(8,128)(2,1)S(1)} %get-tuple-element.243, bf16[2048,256]{1,0:T(8,128)(2,1)S(1)} %get-tuple-element.244), kind=kOutput, calls=%fused_computation.1 | convolution fusion | flops 6453460992 | bytes 14680064 | tf_op jit(solution)/shard_map/dot_general | solution.py:32
  512.8 51.3 %moe_out.1 = f32[256,2048]{1,0:T(8,128)} custom-call(bf16[2048,2048]{1,0:T(8,128)(2,1)} %get-tuple-element.101.l_hbm, bf16[2048,2048]{1,0:T(8,128)(2,1)} %bitcast.99), custom_call_target="tpu_custom_call" | custom-call | flops 1000000000 | bytes 4194304 | tf_op jit(solution)/shard_map/moe_out/pallas_call | solution.py:1113
  564.2 2.8 pad_maximum_fusion.1.l_hbm
  567.0 47.1 %normed_back.1 = f32[256,2048]{1,0:T(8,128)} custom-call(bf16[2048,768]{1,0:T(8,128)(2,1)} %pad_maximum_fusion.1.l_hbm, bf16[2048,768]{1,0:T(8,128)(2,1)} %pad_maximum_fusion.2.r_hbm), custom_call_target="tpu_custom_call" | custom-call | flops 1000000000 | bytes 4194304 | tf_op jit(solution)/shard_map/normed_back/pallas_call | solution.py:1113
  614.1 2.4 fusion.7
  616.6 3.9 pad_maximum_fusion
  620.5 6.0 fusion.6
  626.5 10.6 %reduce-scatter.5.cloned.1.call-done = bf16[1,24,512,128]{3,2,1,0:T(8,128)(2,1)} async-done(((bf16[4,24,512,128]{3,2,1,0:T(8,128)(2,1)}), bf16[1,24,512,128]{3,2,1,0:T(8,128)(2,1)}) %reduce-scatter.5.cloned.1.call-update) | async-done | bytes 3145744 | tf_op jit(solution)/shard_map/reduce_scatter | solution.py:1348
  641.4 3.1 collective-permute-done.3
  646.1 2.6 collective-permute-done.4
  651.5 3.0 collective-permute-done.6
  654.4 3.3 collective-permute-start.7
  657.8 3.0 collective-permute-done.7
  672.2 3.1 fusion.22
  676.6 3.6 maximum_convert_fusion.2
  680.2 2.3 maximum_convert_fusion.1
  684.9 33.3 %reduce-scatter.11.cloned.1.call-done = bf16[512,1024]{1,0:T(8,128)(2,1)} async-done(((bf16[2048,1024]{1,0:T(8,128)(2,1)}), bf16[512,1024]{1,0:T(8,128)(2,1)}) %reduce-scatter.11.cloned.1.call-update) | async-done | bytes 1048592 | tf_op jit(solution)/shard_map/reduce_scatter | solution.py:1408
  718.2 2.4 convert_bitcast_fusion
  (195 shorter events, 61.2 us)
Async XLA Ops:
  7.2 328.1 %reduce-scatter.9.cloned.1.call-start = ((), (), s32[]{:S(2)}) async-start(), calls=%async_computation.7 | async-start | bytes 3932160 | tf_op jit(solution)/shard_map/reduce_scatter | solution.py:1348
  196.7 284.3 %reduce-scatter.7.cloned.1.call-start = ((), (), s32[]{:S(2)}) async-start(), calls=%async_computation.6 | async-start | bytes 11796480 | tf_op jit(solution)/shard_map/reduce_scatter | solution.py:1348
  249.8 387.3 %reduce-scatter.5.cloned.1.call-start = ((), (), s32[]{:S(2)}) async-start(), calls=%async_computation.5 | async-start | bytes 15728640 | tf_op jit(solution)/shard_map/reduce_scatter | solution.py:1348
  318.4 8.8 %copy-start.11 = (f32[256,2048]{1,0:T(8,128)S(1)}, f32[256,2048]{1,0:T(8,128)}, u32[]{:S(2)}) copy-start(f32[256,2048]{1,0:T(8,128)} %get-tuple-element.80) | copy-start | bytes 6291460
  321.2 6.3 copy-start.23
  323.5 10.5 %all-to-all-start = ((f32[8,256,16]{1,2,0:T(8,128)}), f32[8,256,16]{1,2,0:T(8,128)S(1)}, u32[]{:S(2)}, u32[]{:S(2)}) async-start(f32[8,256,16]{1,2,0:T(8,128)} %copy.140), calls=%async_computation.3 | async-start | bytes 262144 | tf_op jit(solution)/shard_map/all_to_all | solution.py:1353
  327.1 391.1 %reduce-scatter.11.cloned.1.call-start = ((), (), s32[]{:S(2)}) async-start(), calls=%async_computation.8 | async-start | bytes 5242880 | tf_op jit(solution)/shard_map/reduce_scatter | solution.py:1408
  335.3 67.7 %copy-start.38 = (f32[2048]{0:T(1024)S(1)}, f32[2048]{0:T(1024)}, u32[]{:S(2)}) copy-start(f32[2048]{0:T(1024)} %param.26) | copy-start | bytes 24580
  408.5 38.9 %copy-start.36 = (bf16[256,2048]{1,0:T(8,128)(2,1)S(1)}, bf16[256,2048]{1,0:T(8,128)(2,1)}, u32[]{:S(2)}) copy-start(bf16[256,2048]{1,0:T(8,128)(2,1)} %wo_hbm.1) | copy-start | bytes 3145732
  447.5 6.0 copy-start.2
  447.5 6.0 copy-start.5
  447.5 6.0 copy-start.6
  447.5 6.0 copy-start.7
  447.5 6.0 copy-start.8
  481.8 14.7 %slice-start = ((s8[8388608]{0:T(1024)(128)(4,1)}), s8[4194304]{0:T(1024)(128)(4,1)S(1)}, s32[]{:S(2)}) async-start(s8[8388608]{0:T(1024)(128)(4,1)} %bitcast.100), calls=%async_computation.9 | async-start | bytes 8388608
  484.7 7.5 %copy-start.21 = (f32[2048,2]{1,0:T(8,128)S(1)}, f32[2048,2]{1,0:T(8,128)}, u32[]{:S(2)}) copy-start(f32[2048,2]{1,0:T(8,128)} %get-tuple-element.75) | copy-start | bytes 49156
  484.7 11.9 %slice-start.1 = ((s8[8388608]{0:T(1024)(128)(4,1)}), s8[4194304]{0:T(1024)(128)(4,1)S(1)}, s32[]{:S(2)}) async-start(s8[8388608]{0:T(1024)(128)(4,1)} %bitcast.100), calls=%async_computation.10 | async-start | bytes 8388608
  489.9 6.6 copy-start.43
  490.0 1.3 collective-permute-start
  491.3 3.8 collective-permute-start.1
  495.1 5.2 collective-permute-start.2
  502.0 10.8 %copy-start.24 = (bf16[2048,256]{1,0:T(8,128)(2,1)}, bf16[2048,256]{1,0:T(8,128)(2,1)S(1)}, u32[]{:S(2)}) copy-start(bf16[2048,256]{1,0:T(8,128)(2,1)S(1)} %get-tuple-element.244) | copy-start | bytes 3145732
  567.0 47.1 %copy-start.39 = (f32[2048]{0:T(1024)S(1)}, f32[2048]{0:T(1024)}, u32[]{:S(2)}) copy-start(f32[2048]{0:T(1024)} %param.23) | copy-start | bytes 24580
  639.8 4.7 collective-permute-start.3
  641.4 26.3 %copy-start.32 = (bf16[1,18,512,128]{3,2,1,0:T(8,128)(2,1)S(1)}, bf16[1,18,512,128]{3,2,1,0:T(8,128)(2,1)}, u32[]{:S(2)}) copy-start(bf16[1,18,512,128]{3,2,1,0:T(8,128)(2,1)} %reduce-scatter.7.cloned.1.call-done) | copy-start | bytes 7077892
  644.6 4.2 collective-permute-start.4
  648.7 1.3 collective-permute-start.5
  650.0 4.4 collective-permute-start.6
  654.4 6.3 collective-permute-start.7
  660.8 1.2 collective-permute-start.8
  662.0 4.2 collective-permute-start.9
  666.2 4.7 collective-permute-start.10
  (30 other events, 81.7 us)
Sparse Core Ops, SparseCore 0:
  196.9 61.4 reduce-scatter.8
  260.7 161.2 reduce-scatter.6
  424.4 212.6 reduce-scatter.4
  639.3 78.8 reduce-scatter.10

commit v5 on v4

--- a/solution.py
+++ b/solution.py
@@ -479,17 +479,18 @@
 
 
 def front_body(
-    x_hbm, wo_hbm, g_hbm, wq_hbm, wk_hbm, wv_hbm, gain_ref, qg_ref, kg_ref, mg_ref, pos_ref, sq_ref, sk_ref,
-    normed_hbm, *rest, size, block, reach
+    x_hbm, wo_hbm, g_hbm, wq_hbm, wk_hbm, wv_hbm, gain_ref, qg_ref, kg_ref, mg_ref, routes_ref, sk_ref,
+    normed_hbm, *rest, size, block, reach, capacity
 ):
-    outs, rest = rest[:13], rest[13:]
+    outs, rest = rest[:14], rest[14:]
     g_all, rest = rest[0], rest[1:]
-    local, rest = rest[:13], rest[13:]
+    local, rest = rest[:14], rest[14:]
     (
         q_ref, k_ref, v_ref, qu_ref, ku_ref, rs_ref, cos_ref, sin_ref, o_ref, low_ref, lse_ref, res_ref, moe_ref,
+        mask_ref,
     ) = local
     (
-        x_v, n_v, w_v, wo_all, own_ref, sums, sums_all,
+        x_v, n_v, w_v, wo_all, own_ref, sums, sums_all, place_v,
         send_sem, recv_sem, wo_send, wo_recv, g_send, g_recv, ss_send, ss_recv, a_send, a_recv,
         w_sem, x_sem, wo_sem, g_sem, a_sem, n_sem, o_sem,
     ) = rest
@@ -527,16 +528,50 @@
     power = (lane % half_dim).astype(F32) * (-2.0 * math.log(10000.0) / HEAD_DIM)
     frequency = jnp.exp(power)
 
+    seg = jnp.concatenate([sk_ref[i] for i in range(size)], axis=0)
+    first_token = jnp.zeros(seg.shape, F32)
+    for value in range(1, 16):
+        count = jnp.sum(jnp.where(seg < value, 1.0, 0.0))
+        first_token = jnp.where(seg == value, count, first_token)
+    index = lax.broadcasted_iota(jnp.int32, seg.shape, 0) * block + lax.broadcasted_iota(
+        jnp.int32, seg.shape, 1
+    )
+    place = index.astype(F32) - first_token
+    for i in range(size):
+        place_v[i] = place[i : i + 1]
+
+    def column(row):
+        return jnp.broadcast_to(row, (HEAD_DIM, block)).T
+
     def table(i, _):
         r = pl.ds(pl.multiple_of(i * own, own), own)
-        angle = pos_ref[r, :] * frequency
+        angle = column(place_v[i]) * frequency
         cos_ref[r, :] = jnp.cos(angle)
         sine = jnp.sin(angle)
         sin_ref[r, :] = jnp.where(lane < half_dim, -sine, sine)
         return 0
 
     lax.fori_loop(0, size, table, 0)
-    for i in (6, 7):
+
+    experts = mask_ref.shape[1]
+    expert = lax.broadcasted_iota(jnp.int32, (experts, block), 0)
+    earlier = (
+        lax.broadcasted_iota(jnp.int32, (block, block), 0)
+        < lax.broadcasted_iota(jnp.int32, (block, block), 1)
+    )
+    earlier = jnp.where(earlier, 1.0, 0.0).astype(BF)
+    before = jnp.zeros((experts, 1), F32)
+    fill = jnp.zeros((HEAD_DIM - experts, block), F32)
+    for i in range(size):
+        chosen = routes_ref[:, i * block : (i + 1) * block]
+        routed = jnp.zeros((experts, block), F32)
+        for k in range(chosen.shape[0]):
+            routed = routed + jnp.where(chosen[k : k + 1] == expert, 1.0, 0.0)
+        taken = dot_nn(routed.astype(BF), earlier) + before
+        before = before + jnp.sum(routed, axis=1, keepdims=True)
+        kept = jnp.where(taken < capacity, routed, 0.0)
+        mask_ref[i * block : (i + 1) * block, :] = jnp.concatenate([kept, fill], axis=0).T[:, :experts]
+    for i in (6, 7, 13):
         written(i).start()
 
     def stored(dev):
@@ -650,12 +685,12 @@
 
     def query_block(qb, _):
         rq = pl.ds(pl.multiple_of(qb * block, block), block)
-        seg_q = sq_ref[rq, :]
+        seg_q = column(sk_ref[qb].astype(F32))[:, 0:1]
         qs = [q_ref[rq, c] for c in hc]
 
         def step(kb, carry):
             rows = pl.ds(pl.multiple_of(kb * block, block), block)
-            allowed = (seg_q == sk_ref[kb]) & (kb * block + col0 <= qb * block + row0)
+            allowed = (seg_q == sk_ref[kb].astype(F32)) & (kb * block + col0 <= qb * block + row0)
             out = []
             for h in range(heads):
                 m, l, acc = carry[h]
@@ -738,7 +773,7 @@
         wo_copy(k).wait_send()
         g_copy(k).wait_send()
     g_here.wait()
-    for i in range(13):
+    for i in range(14):
         written(i).wait()
 
 
@@ -749,7 +784,7 @@
             copy(f).start()
 
 
-def front(x, wo, g, wq, wk, wv, gain, qg, kg, mg, pos, seg_col, seg_rows, size, block, reach, cid):
+def front(x, wo, g, wq, wk, wv, gain, qg, kg, mg, routes_t, seg_rows, experts, size, block, reach, capacity, cid):
     own, width = x.shape
     cols = wq.shape[1]
     tokens = own * size
@@ -772,16 +807,17 @@
             arr((tokens, heads), F32),
             arr((own, width), F32),
             arr((own, width), BF),
+            arr((tokens, experts), F32),
     )
     return pl.pallas_call(
-        functools.partial(front_body, size=size, block=block, reach=reach),
+        functools.partial(front_body, size=size, block=block, reach=reach, capacity=capacity),
         out_shape=(
             arr((tokens, width), BF),
             *kept,
             arr((tokens, width), BF),
         ),
-        in_specs=[any_spec] * 6 + [vm] * 7,
-        out_specs=[any_spec] * 15,
+        in_specs=[any_spec] * 6 + [vm] * 6,
+        out_specs=[any_spec] * 16,
         scratch_shapes=[pltpu.VMEM(k.shape, k.dtype) for k in kept]
         + [
             pltpu.VMEM((tokens, width), BF),
@@ -791,6 +827,7 @@
             pltpu.VMEM((own, width), BF),
             pltpu.VMEM((size, 2, own), F32),
             pltpu.VMEM((size, size, 2, own), F32),
+            pltpu.VMEM((size, 1, block), F32),
         ]
         + [dma((GATHER_COPIES,))] * 6
         + [dma((size,))] * 4
@@ -801,14 +838,14 @@
             dma,
             dma,
             dma((size,)),
-            dma((13,)),
+            dma((14,)),
         ],
         compiler_params=pltpu.CompilerParams(
             vmem_limit_bytes=58 * MIB, collective_id=cid, has_side_effects=True
         ),
         cost_estimate=pl.CostEstimate(flops=10**8, bytes_accessed=4 * MIB, transcendentals=0),
         name="front",
-    )(x, wo, g, wq, wk, wv, gain[None, :], qg[None, :], kg[None, :], mg[None, :], pos, seg_col, seg_rows)
+    )(x, wo, g, wq, wk, wv, gain[None, :], qg[None, :], kg[None, :], mg[None, :], routes_t, seg_rows)
 
 
 def middle_body(
@@ -856,7 +893,7 @@
         r = pl.ds(pl.multiple_of(dev * own, own), own)
         moe_out(dev).start()
         xt_v[:, r] = x_v[r, :].T
-        logits = dot_nn(x_v[r, :], router_ref[...])
+        logits = dot_nt(x_v[r, :], router_ref[...])
         grown = jnp.exp(logits - jnp.max(logits, axis=1, keepdims=True))
         probs = grown / jnp.sum(grown, axis=1, keepdims=True)
         probs_ref[r, :] = probs
@@ -1219,6 +1256,46 @@
     return jnp.concatenate(pieces, axis=1)
 
 
+def document_blocks(segments, block):
+    seg = segments.reshape(-1)
+    tokens = seg.shape[0]
+    values16 = jnp.arange(16, dtype=jnp.int32)
+    below = jnp.sum((seg[None, :] < values16[:, None]).astype(jnp.int32), axis=1)
+    doc_start = jnp.sum(
+        jnp.where(seg[:, None] == values16[None, :], below[None, :], 0), axis=1
+    )
+    positions = jnp.arange(tokens, dtype=jnp.int32) - doc_start
+    return (
+        seg[:, None],
+        seg.reshape(tokens // block, 1, block),
+        doc_start[::block] // block,
+        positions.astype(F32)[:, None],
+    )
+
+
+def routing_mask(routes, experts, capacity, block):
+    tokens = routes.shape[0]
+    expert_ids = jnp.arange(experts, dtype=jnp.int32)
+    routed = jnp.sum(
+        (routes[:, :, None] == expert_ids[None, None, :]).astype(F32), axis=1
+    )
+    tri = (
+        jnp.arange(block, dtype=jnp.int32)[:, None] > jnp.arange(block, dtype=jnp.int32)[None, :]
+    ).astype(BF)
+    nb = tokens // block
+    routed_b = routed.reshape(nb, block, experts)
+    within = jnp.einsum("ij,bje->bie", tri, routed_b.astype(BF), preferred_element_type=F32)
+    sums = jnp.sum(routed_b, axis=1)
+    before = jnp.sum(
+        jnp.where(
+            (jnp.arange(nb)[:, None] > jnp.arange(nb)[None, :])[:, :, None], sums[None, :, :], 0.0
+        ),
+        axis=1,
+    )
+    place = within + before[:, None, :]
+    return (routed_b * (place < capacity).astype(F32)).reshape(tokens, experts)
+
+
 def per_device(
     block_input, segments, routes, w_query, w_key, w_value, w_output, attn_gain, query_gain, key_gain,
     moe_gain, router, w_gate, w_up, w_down, cotangent, *, n_dp, n_tensor
@@ -1236,59 +1313,31 @@
     col_start = me * local_cols
     block = 256
 
-    seg = segments.reshape(token_count)
-    values16 = jnp.arange(16, dtype=jnp.int32)
-    below = jnp.sum((seg[None, :] < values16[:, None]).astype(jnp.int32), axis=1)
-    doc_start = jnp.sum(
-        jnp.where(seg[:, None] == values16[None, :], below[None, :], 0), axis=1
-    )
-    positions = jnp.arange(token_count, dtype=jnp.int32) - doc_start
-    lo_block = doc_start[::block] // block
-    seg_col = seg[:, None]
-    seg_rows = seg.reshape(token_count // block, 1, block)
-
-    expert_ids = jnp.arange(experts, dtype=jnp.int32)
-    routed = jnp.sum(
-        (routes[:, :, None] == expert_ids[None, None, :]).astype(F32), axis=1
-    )
-    tri = (
-        jnp.arange(block, dtype=jnp.int32)[:, None] > jnp.arange(block, dtype=jnp.int32)[None, :]
-    ).astype(BF)
-    nb = token_count // block
-    routed_b = routed.reshape(nb, block, experts)
-    within = jnp.einsum("ij,bje->bie", tri, routed_b.astype(BF), preferred_element_type=F32)
-    sums = jnp.sum(routed_b, axis=1)
-    before = jnp.sum(
-        jnp.where(
-            (jnp.arange(nb)[:, None] > jnp.arange(nb)[None, :])[:, :, None], sums[None, :, :], 0.0
-        ),
-        axis=1,
-    )
-    place = within + before[:, None, :]
-    mask = (routed_b * (place < capacity).astype(F32)).reshape(token_count, experts)
-
     w_qkv = jnp.concatenate([w_query, w_key, w_value], axis=1)
-    pos_col = positions.astype(F32)[:, None]
     input_own = block_input.astype(F32)
     wd_flat = w_down.reshape(experts * hid, model_width)
     reach = min(1024 // block, token_count // block)
     if n_tensor == 8:
         (
             normed, queries, keys_rot, value_low, query_unit, key_unit, scales, cos_one, sin_one,
-            attended, attn_low, lse, residual, own_moe_in, full_cot,
+            attended, attn_low, lse, residual, own_moe_in, mask, full_cot,
         ) = front(
             block_input, w_output, cotangent, w_query, w_key, w_value, attn_gain, query_gain, key_gain, moe_gain,
-            pos_col, seg_col, seg_rows,
-            n_tensor, block, reach, 6,
+            routes.T, segments.reshape(token_count // block, 1, block),
+            experts, n_tensor, block, reach, capacity, 6,
         )
+        segments, own_moe_in = lax.optimization_barrier((segments, own_moe_in))
+        seg_col, seg_rows, lo_block = document_blocks(segments, block)[:3]
         query_rs, key_rs = scales[:, 0:1], scales[:, 1:2]
         cos_all = jnp.concatenate([cos_one] * local_heads, axis=1)
         sin_all = jnp.concatenate([sin_one] * local_heads, axis=1)
         lead = middle(
-            own_moe_in, full_cot, mask, router, w_gate, w_up, wd_flat, n_tensor, n_dp, 1
+            own_moe_in, full_cot, mask, router.T, w_gate, w_up, wd_flat, n_tensor, n_dp, 1
         )
         moe_in, lead = lead[0], lead[1:]
     else:
+        seg_col, seg_rows, lo_block, pos_col = document_blocks(segments, block)
+        mask = routing_mask(routes, experts, capacity, block)
         half = HEAD_DIM // 2
         frequency = jnp.exp(
             jnp.arange(half, dtype=F32) * (-2.0 * math.log(10000.0) / HEAD_DIM)

time: 739 us -> 730 us (0.988)
    unnamed x97 -> x91, local copies, waits for them, and re-layouts: 14.6 us -> 15 us
where the time goes in v5:
time: 730 us; the launch traced here: 720 us
  Pallas kernels  528 us (72%)
  waiting for transfers between devices  63.2 us (9%)
  other arithmetic  40.4 us (6%)
  local copies, waits for them, and re-layouts  31.4 us (4%)
  matrix products  24 us (3%)
  starting transfers between devices  17.8 us (2%)
  between operations  14.9 us (2%)
    pallas_call x3, Pallas kernels, matmul_scatter(): pl.pallas_call(functools.partial(matmul_scatter_body, size=size, slices=s...  166 us
    pallas_call x1, Pallas kernels, front(): pl.pallas_call(functools.partial(front_body, size=size, block=block, reac...  124 us
    pallas_call x2, Pallas kernels, expert_chunk(): pl.pallas_call(functools.partial(expert_body, first=first, rows_blk=rows_...  120 us
    pallas_call x1, Pallas kernels, middle(): pl.pallas_call(functools.partial(middle_body, size=size, parts=parts), ou...  56.7 us
    pallas_call x1, Pallas kernels, gather_all(): pl.pallas_call(gather_body, out_shape=jax.ShapeDtypeStruct((own * size, c...  39 us
    reduce_scatter x1, waiting for transfers between devices, per_device(): qkv_red = lax.psum_scatter(proj_grad, 'dp', scatter_dimension=0, tiled=True)  33.3 us
    pallas_call x1, Pallas kernels, attn_bwd(): pl.pallas_call(functools.partial(attn_bwd_body, block=block, heads=heads)...  22.2 us
    ppermute x11, waiting for transfers between devices, swap(): return lax.ppermute(value, axis, [(i, i ^ bit) for i in range(size)])  17 us
  transfers between devices with their start and end apart: 16, of which 11 were waited for; matrix products, arithmetic and copies ran while one was open for 11% of the time, Pallas kernels for 48%

profile of v5, /device:TPU:0, one launch (start us, length us, event | category | flops | bytes accessed | tf_op | source)
XLA Modules:
  0.0 720.1 jit_solution(16491410637100865466)
XLA Ops:
  7.2 124.4 %front.1 = (bf16[2048,2048]{1,0:T(8,128)(2,1)}, bf16[2048,256]{1,0:T(8,128)(2,1)}, bf16[2048,256]{1,0:T(8,128)(2,1)}, bf16[2048,256]{1,0:T(8,128)(2,1)}, f32[204...) custom-call(bf16[256,2048]{1,0:T(8,128)(2,1)} %x_hbm.1, ...), custom_call_target="tpu_custom_call" | custom-call | flops 100000000 | bytes 4194304 | tf_op jit(solution)/shard_map/front/pallas_call | solution.py:812
  131.6 56.7 %middle.1 = (bf16[2048,2048]{1,0:T(8,128)(2,1)}, bf16[2048,4096]{1,0:T(8,128)(2,1)}, bf16[2048,2048]{1,0:T(8,128)(2,1)}, bf16[2048,4096]{1,0:T(8,128)(2,1)}, f32...) custom-call(bf16[256,2048]{1,0:T(8,128)(2,1)} %get-tuple-element.65., ...), custom_call_target="tpu_custom_call" | custom-call | flops 1000000000 | bytes 4194304 | tf_op jit(solution)/shard_map/middle/pallas_call | solution.py:992
  188.4 52.7 %expert_chunk.2 = (bf16[2048,4096]{1,0:T(8,128)(2,1)}, bf16[2048,2048]{1,0:T(8,128)(2,1)}, bf16[2048,4096]{1,0:T(8,128)(2,1)}, f32[2048,16]{1,0:T(8,128)}, bf16[4,18,512,128]{3,2,1,0:T(8,128)(2,1)}) custom-call(bf16[2048,2048]{1,0:T(8,128)(2,1)} %get-tuple-element.68.refs_0_, ...), custom_call_target="tpu_custom_call", output_to_operand_aliasing={{0}: (7, {}), {1}: (8, {}), {2}: (9, {})} | custom-call | flops 1000000000 | bytes 4194304 | tf_op jit(solution)/shard_map/expert_chunk/pallas_call | solution.py:417
  241.2 67.4 %expert_chunk.3 = (bf16[2048,4096]{1,0:T(8,128)(2,1)}, bf16[2048,2048]{1,0:T(8,128)(2,1)}, bf16[2048,4096]{1,0:T(8,128)(2,1)}, f32[2048,16]{1,0:T(8,128)}, bf16[4,24,512,128]{3,2,1,0:T(8,128)(2,1)}) custom-call(bf16[2048,2048]{1,0:T(8,128)(2,1)} %get-tuple-element.68.refs_0_, ...), custom_call_target="tpu_custom_call", output_to_operand_aliasing={{0}: (7, {}), {1}: (8, {}), {2}: (9, {})} | custom-call | flops 1000000000 | bytes 4194304 | tf_op jit(solution)/shard_map/expert_chunk/pallas_call | solution.py:417
  312.6 3.6 all-to-all-start
  322.6 2.2 pad_maximum_fusion.2.r_hbm
  326.3 67.1 %moe_back.1 = f32[256,2048]{1,0:T(8,128)} custom-call(bf16[2048,4096]{1,0:T(8,128)(2,1)} %get-tuple-element.89.l_hbm, bf16[2048,4096]{1,0:T(8,128)(2,1)} %get-tuple-element.90.r_hbm), custom_call_target="tpu_custom_call" | custom-call | flops 1000000000 | bytes 4194304 | tf_op jit(solution)/shard_map/moe_back/pallas_call | solution.py:1150
  393.5 2.8 multiply_reduce_fusion.2
  399.3 39.0 %gather_residual.1 = bf16[2048,2048]{1,0:T(8,128)(2,1)} custom-call(bf16[256,2048]{1,0:T(8,128)(2,1)} %fusion.13.x_ref), custom_call_target="tpu_custom_call" | custom-call | bytes 4194304 | tf_op jit(solution)/shard_map/gather_residual/pallas_call | solution.py:1203
  438.3 5.9 convolution_convert_fusion.2.do_ref
  444.3 22.2 %attn_bwd.1 = (f32[2048,256]{1,0:T(8,128)S(1)}, f32[2048,256]{1,0:T(8,128)S(1)}, f32[2048,256]{1,0:T(8,128)S(1)}) custom-call(s32[8]{0:T(128)S(1)} %and_select_fusion.lo_ref, bf16[2048,256]{1,0:T(8,128)(2,1)S(1)} %copy-done.4, bf16[2048,256]{1,0:T(8,128)(2,1)S(1)} %copy-done.5, bf16[2048,256]{1,0:T(8,128)(2,1)S(1)} %copy-done.6, ...), custom_call_target="tpu_custom_call" | custom-call | flops 100000000 | bytes 4194304 | tf_op jit(solution)/shard_map/attn_bwd/pallas_call | solution.py:233
  469.2 2.3 fusion.19
  475.1 5.3 multiply_reduce_fusion.1
  486.9 3.6 convolution_convert_fusion.1
  492.3 10.4 %convolution_convert_fusion = bf16[2048,768]{1,0:T(8,128)(2,1)} fusion(bf16[2048,2048]{1,0:T(8,128)(2,1)} %get-tuple-element.79, bf16[2048,256]{1,0:T(8,128)(2,1)S(1)} %convert_element_type.67, bf16[2048,256]{1,0:T(8,128)(2,1)S(1)} %get-tuple-element.235, bf16[2048,256]{1,0:T(8,128)(2,1)S(1)} %get-tuple-element.236), kind=kOutput, calls=%fused_computation.1 | convolution fusion | flops 6453460992 | bytes 14680064 | tf_op jit(solution)/shard_map/dot_general | solution.py:32
  502.7 52.0 %moe_out.1 = f32[256,2048]{1,0:T(8,128)} custom-call(bf16[2048,2048]{1,0:T(8,128)(2,1)} %get-tuple-element.107.l_hbm, bf16[2048,2048]{1,0:T(8,128)(2,1)} %bitcast.85), custom_call_target="tpu_custom_call" | custom-call | flops 1000000000 | bytes 4194304 | tf_op jit(solution)/shard_map/moe_out/pallas_call | solution.py:1150
  556.5 46.8 %normed_back.1 = f32[256,2048]{1,0:T(8,128)} custom-call(bf16[2048,768]{1,0:T(8,128)(2,1)} %pad_maximum_fusion.1.l_hbm, bf16[2048,768]{1,0:T(8,128)(2,1)} %pad_maximum_fusion.2.r_hbm), custom_call_target="tpu_custom_call" | custom-call | flops 1000000000 | bytes 4194304 | tf_op jit(solution)/shard_map/normed_back/pallas_call | solution.py:1150
  603.4 2.4 fusion.7
  605.9 3.9 pad_maximum_fusion
  609.8 6.1 fusion.6
  615.9 12.8 %reduce-scatter.5.cloned.1.call-done = bf16[1,24,512,128]{3,2,1,0:T(8,128)(2,1)} async-done(((bf16[4,24,512,128]{3,2,1,0:T(8,128)(2,1)}), bf16[1,24,512,128]{3,2,1,0:T(8,128)(2,1)}) %reduce-scatter.5.cloned.1.call-update) | async-done | bytes 3145744 | tf_op jit(solution)/shard_map/reduce_scatter | solution.py:1397
  633.0 3.1 collective-permute-done.3
  637.7 2.6 collective-permute-done.4
  643.1 2.9 collective-permute-done.6
  646.1 3.4 collective-permute-start.7
  649.4 3.0 collective-permute-done.7
  663.8 3.1 fusion.16
  668.2 3.6 maximum_convert_fusion.2
  671.9 2.3 maximum_convert_fusion.1
  674.2 2.3 maximum_convert_fusion
  676.5 33.3 %reduce-scatter.11.cloned.1.call-done = bf16[512,1024]{1,0:T(8,128)(2,1)} async-done(((bf16[2048,1024]{1,0:T(8,128)(2,1)}), bf16[512,1024]{1,0:T(8,128)(2,1)}) %reduce-scatter.11.cloned.1.call-update) | async-done | bytes 1048592 | tf_op jit(solution)/shard_map/reduce_scatter | solution.py:1457
  709.8 2.4 convert_bitcast_fusion
  (178 shorter events, 53.5 us)
Async XLA Ops:
  7.2 319.1 %reduce-scatter.9.cloned.1.call-start = ((), (), s32[]{:S(2)}) async-start(), calls=%async_computation.7 | async-start | bytes 3932160 | tf_op jit(solution)/shard_map/reduce_scatter | solution.py:1397
  188.4 283.2 %reduce-scatter.7.cloned.1.call-start = ((), (), s32[]{:S(2)}) async-start(), calls=%async_computation.6 | async-start | bytes 11796480 | tf_op jit(solution)/shard_map/reduce_scatter | solution.py:1397
  241.2 387.6 %reduce-scatter.5.cloned.1.call-start = ((), (), s32[]{:S(2)}) async-start(), calls=%async_computation.5 | async-start | bytes 15728640 | tf_op jit(solution)/shard_map/reduce_scatter | solution.py:1397
  310.2 6.1 copy-start.8
  311.6 5.4 copy-start.9
  312.6 12.5 %all-to-all-start = ((f32[8,256,16]{1,2,0:T(8,128)}), f32[8,256,16]{1,2,0:T(8,128)S(1)}, u32[]{:S(2)}, u32[]{:S(2)}) async-start(f32[8,256,16]{1,2,0:T(8,128)} %copy.86), calls=%async_computation.3 | async-start | bytes 262144 | tf_op jit(solution)/shard_map/all_to_all | solution.py:1402
  316.2 393.6 %reduce-scatter.11.cloned.1.call-start = ((), (), s32[]{:S(2)}) async-start(), calls=%async_computation.8 | async-start | bytes 5242880 | tf_op jit(solution)/shard_map/reduce_scatter | solution.py:1457
  326.3 67.2 %copy-start.36 = (bf16[2048,16]{0,1:T(8,128)(2,1)S(1)}, bf16[2048,16]{0,1:T(8,128)(2,1)}, u32[]{:S(2)}) copy-start(bf16[2048,16]{0,1:T(8,128)(2,1)} %param.27) | copy-start | bytes 196612
  326.3 67.2 %copy-start.37 = (f32[2048]{0:T(1024)S(1)}, f32[2048]{0:T(1024)}, u32[]{:S(2)}) copy-start(f32[2048]{0:T(1024)} %param.26) | copy-start | bytes 24580
  399.3 39.0 %copy-start.33 = (bf16[256,2048]{1,0:T(8,128)(2,1)S(1)}, bf16[256,2048]{1,0:T(8,128)(2,1)}, u32[]{:S(2)}) copy-start(bf16[256,2048]{1,0:T(8,128)(2,1)} %wo_hbm.1) | copy-start | bytes 3145732
  438.3 6.0 copy-start.4
  438.3 6.0 copy-start.5
  438.3 6.0 copy-start.6
  438.3 6.0 copy-start.7
  472.2 14.7 %slice-start = ((s8[8388608]{0:T(1024)(128)(4,1)}), s8[4194304]{0:T(1024)(128)(4,1)S(1)}, s32[]{:S(2)}) async-start(s8[8388608]{0:T(1024)(128)(4,1)} %bitcast.86), calls=%async_computation.9 | async-start | bytes 8388608
  475.0 7.6 %copy-start.20 = (f32[2048,2]{1,0:T(8,128)S(1)}, f32[2048,2]{1,0:T(8,128)}, u32[]{:S(2)}) copy-start(f32[2048,2]{1,0:T(8,128)} %get-tuple-element.80) | copy-start | bytes 49156
  475.0 11.8 %slice-start.1 = ((s8[8388608]{0:T(1024)(128)(4,1)}), s8[4194304]{0:T(1024)(128)(4,1)S(1)}, s32[]{:S(2)}) async-start(s8[8388608]{0:T(1024)(128)(4,1)} %bitcast.86), calls=%async_computation.10 | async-start | bytes 8388608
  480.4 6.5 copy-start.41
  480.4 1.2 collective-permute-start
  481.7 3.8 collective-permute-start.1
  485.5 5.2 collective-permute-start.2
  556.5 46.9 %copy-start.13 = (bf16[256,2048]{1,0:T(8,128)(2,1)S(1)}, bf16[256,2048]{1,0:T(8,128)(2,1)}, u32[]{:S(2)}) copy-start(bf16[256,2048]{1,0:T(8,128)(2,1)} %x_hbm.1) | copy-start | bytes 3145732
  556.5 46.9 %copy-start.38 = (f32[2048]{0:T(1024)S(1)}, f32[2048]{0:T(1024)}, u32[]{:S(2)}) copy-start(f32[2048]{0:T(1024)} %param.23) | copy-start | bytes 24580
  631.4 4.7 collective-permute-start.3
  633.0 26.3 %copy-start.30 = (bf16[1,18,512,128]{3,2,1,0:T(8,128)(2,1)S(1)}, bf16[1,18,512,128]{3,2,1,0:T(8,128)(2,1)}, u32[]{:S(2)}) copy-start(bf16[1,18,512,128]{3,2,1,0:T(8,128)(2,1)} %reduce-scatter.7.cloned.1.call-done) | copy-start | bytes 7077892
  636.2 4.2 collective-permute-start.4
  640.3 1.3 collective-permute-start.5
  641.6 4.4 collective-permute-start.6
  646.1 6.3 collective-permute-start.7
  652.4 1.2 collective-permute-start.8
  653.6 4.2 collective-permute-start.9
  657.8 4.7 collective-permute-start.10
  (28 other events, 69.6 us)
Sparse Core Ops, SparseCore 0:
  188.5 61.4 reduce-scatter.8
  252.3 161.2 reduce-scatter.6
  416.0 212.6 reduce-scatter.4
  630.9 78.8 reduce-scatter.10

commit v6 on v5

--- a/solution.py
+++ b/solution.py
@@ -850,8 +850,8 @@
 
 def middle_body(
     own_hbm, g_hbm, mask_ref, router_ref, wg_ref, wu_ref, wd_ref,
-    moe_hbm, dgu_hbm, ga_hbm, wcat_hbm, dots_ref, grads_ref, xt_hbm, gates_ref, probs_ref,
-    x_v, xt_v, g_v, wcat, dgu_v, ga_v, send_sem, recv_sem, own_sem, g_sem, m_sem, out_sem, *, size, parts
+    moe_hbm, dgu_hbm, ga_hbm, wcat_hbm, dots_hbm, grads_hbm, xt_hbm, gates_hbm, probs_hbm,
+    x_v, xt_v, g_v, wcat, dgu_v, ga_v, dots_ref, grads_ref, gates_ref, probs_ref, part_sem, send_sem, recv_sem, own_sem, g_sem, m_sem, out_sem, *, size, parts
 ):
     me = lax.axis_index("tensor")
     tokens, width = x_v.shape
@@ -955,6 +955,9 @@
         pltpu.make_async_copy(dgu_v, dgu_hbm.at[:, pl.ds(0, 4 * hid)], out_sem.at[1]),
         pltpu.make_async_copy(ga_v, ga_hbm.at[:, pl.ds(0, 2 * hid)], out_sem.at[2]),
         pltpu.make_async_copy(xt_v, xt_hbm, out_sem.at[3]),
+        pltpu.make_async_copy(dots_ref, dots_hbm, out_sem.at[4]),
+        pltpu.make_async_copy(gates_ref, gates_hbm, out_sem.at[5]),
+        pltpu.make_async_copy(probs_ref, probs_hbm, out_sem.at[6]),
     ]
     for o in outs:
         o.start()
@@ -968,6 +971,9 @@
                 grads_ref[s, 3 * j + 2, c * hid : (c + 1) * hid, :] = gd[
                     j * hid : (j + 1) * hid, c * hid : (c + 1) * hid
                 ]
+        part_out = pltpu.make_async_copy(grads_ref.at[s], grads_hbm.at[s], part_sem.at[s])
+        part_out.start()
+        outs.append(part_out)
     wcat_out.wait()
     for o in outs:
         o.wait()
@@ -1012,17 +1018,7 @@
             first((2, width, hid)),
             first((2 * hid, width)),
         ],
-        out_specs=[
-            any_spec,
-            any_spec,
-            any_spec,
-            any_spec,
-            first((tokens, experts)),
-            first((parts, 6, ds, hid)),
-            any_spec,
-            first((tokens, experts)),
-            first((tokens, experts)),
-        ],
+        out_specs=[any_spec] * 9,
         scratch_shapes=[
             pltpu.VMEM((tokens, width), BF),
             pltpu.VMEM((width, tokens), BF),
@@ -1030,12 +1026,17 @@
             pltpu.VMEM((width, 4 * hid), BF),
             pltpu.VMEM((tokens, 4 * hid), BF),
             pltpu.VMEM((tokens, 2 * hid), BF),
+            pltpu.VMEM((tokens, experts), F32),
+            pltpu.VMEM((parts, 6, ds, hid), BF),
+            pltpu.VMEM((tokens, experts), F32),
+            pltpu.VMEM((tokens, experts), F32),
+            dma((parts,)),
             dma((GATHER_COPIES,)),
             dma((GATHER_COPIES,)),
             dma,
             dma((size,)),
             dma((size,)),
-            dma((4,)),
+            dma((7,)),
         ],
         compiler_params=pltpu.CompilerParams(
             vmem_limit_bytes=62 * MIB, collective_id=cid, has_side_effects=True

time: 730 us -> 728 us (level)
  no operation moved by 1% of the time
where the time goes in v6:
time: 728 us; the launch traced here: 718 us
  Pallas kernels  527 us (72%)
  waiting for transfers between devices  63.3 us (9%)
  other arithmetic  40.4 us (6%)
  local copies, waits for them, and re-layouts  31.4 us (4%)
  matrix products  24 us (3%)
  starting transfers between devices  17.8 us (2%)
  between operations  14.9 us (2%)
    pallas_call x3, Pallas kernels, matmul_scatter(): pl.pallas_call(functools.partial(matmul_scatter_body, size=size, slices=s...  166 us
    pallas_call x1, Pallas kernels, front(): pl.pallas_call(functools.partial(front_body, size=size, block=block, reac...  124 us
    pallas_call x2, Pallas kernels, expert_chunk(): pl.pallas_call(functools.partial(expert_body, first=first, rows_blk=rows_...  120 us
    pallas_call x1, Pallas kernels, middle(): pl.pallas_call(functools.partial(middle_body, size=size, parts=parts), ou...  55.1 us
    pallas_call x1, Pallas kernels, gather_all(): pl.pallas_call(gather_body, out_shape=jax.ShapeDtypeStruct((own * size, c...  39 us
    reduce_scatter x1, waiting for transfers between devices, per_device(): qkv_red = lax.psum_scatter(proj_grad, 'dp', scatter_dimension=0, tiled=True)  33.3 us
    pallas_call x1, Pallas kernels, attn_bwd(): pl.pallas_call(functools.partial(attn_bwd_body, block=block, heads=heads)...  22.2 us
    ppermute x11, waiting for transfers between devices, swap(): return lax.ppermute(value, axis, [(i, i ^ bit) for i in range(size)])  17.1 us
  transfers between devices with their start and end apart: 16, of which 11 were waited for; matrix products, arithmetic and copies ran while one was open for 11% of the time, Pallas kernels for 48%

profile of v6, /device:TPU:0, one launch (start us, length us, event | category | flops | bytes accessed | tf_op | source)
XLA Modules:
  0.0 718.5 jit_solution(10828390437691700286)
XLA Ops:
  7.2 124.4 %front.1 = (bf16[2048,2048]{1,0:T(8,128)(2,1)}, bf16[2048,256]{1,0:T(8,128)(2,1)}, bf16[2048,256]{1,0:T(8,128)(2,1)}, bf16[2048,256]{1,0:T(8,128)(2,1)}, f32[204...) custom-call(bf16[256,2048]{1,0:T(8,128)(2,1)} %x_hbm.1, ...), custom_call_target="tpu_custom_call" | custom-call | flops 100000000 | bytes 4194304 | tf_op jit(solution)/shard_map/front/pallas_call | solution.py:812
  131.6 55.1 %middle.1 = (bf16[2048,2048]{1,0:T(8,128)(2,1)}, bf16[2048,4096]{1,0:T(8,128)(2,1)}, bf16[2048,2048]{1,0:T(8,128)(2,1)}, bf16[2048,4096]{1,0:T(8,128)(2,1)}, f32...) custom-call(bf16[256,2048]{1,0:T(8,128)(2,1)} %get-tuple-element.65., ...), custom_call_target="tpu_custom_call" | custom-call | flops 1000000000 | bytes 4194304 | tf_op jit(solution)/shard_map/middle/pallas_call | solution.py:998
  186.8 52.7 %expert_chunk.2 = (bf16[2048,4096]{1,0:T(8,128)(2,1)}, bf16[2048,2048]{1,0:T(8,128)(2,1)}, bf16[2048,4096]{1,0:T(8,128)(2,1)}, f32[2048,16]{1,0:T(8,128)}, bf16[4,18,512,128]{3,2,1,0:T(8,128)(2,1)}) custom-call(bf16[2048,2048]{1,0:T(8,128)(2,1)} %get-tuple-element.68.refs_0_, ...), custom_call_target="tpu_custom_call", output_to_operand_aliasing={{0}: (7, {}), {1}: (8, {}), {2}: (9, {})} | custom-call | flops 1000000000 | bytes 4194304 | tf_op jit(solution)/shard_map/expert_chunk/pallas_call | solution.py:417
  239.6 67.4 %expert_chunk.3 = (bf16[2048,4096]{1,0:T(8,128)(2,1)}, bf16[2048,2048]{1,0:T(8,128)(2,1)}, bf16[2048,4096]{1,0:T(8,128)(2,1)}, f32[2048,16]{1,0:T(8,128)}, bf16[4,24,512,128]{3,2,1,0:T(8,128)(2,1)}) custom-call(bf16[2048,2048]{1,0:T(8,128)(2,1)} %get-tuple-element.68.refs_0_, ...), custom_call_target="tpu_custom_call", output_to_operand_aliasing={{0}: (7, {}), {1}: (8, {}), {2}: (9, {})} | custom-call | flops 1000000000 | bytes 4194304 | tf_op jit(solution)/shard_map/expert_chunk/pallas_call | solution.py:417
  310.9 3.6 all-to-all-start
  321.0 2.2 pad_maximum_fusion.2.r_hbm
  324.7 67.2 %moe_back.1 = f32[256,2048]{1,0:T(8,128)} custom-call(bf16[2048,4096]{1,0:T(8,128)(2,1)} %get-tuple-element.89.l_hbm, bf16[2048,4096]{1,0:T(8,128)(2,1)} %get-tuple-element.90.r_hbm), custom_call_target="tpu_custom_call" | custom-call | flops 1000000000 | bytes 4194304 | tf_op jit(solution)/shard_map/moe_back/pallas_call | solution.py:1151
  391.9 2.8 multiply_reduce_fusion.2
  397.7 39.0 %gather_residual.1 = bf16[2048,2048]{1,0:T(8,128)(2,1)} custom-call(bf16[256,2048]{1,0:T(8,128)(2,1)} %fusion.13.x_ref), custom_call_target="tpu_custom_call" | custom-call | bytes 4194304 | tf_op jit(solution)/shard_map/gather_residual/pallas_call | solution.py:1204
  436.7 5.9 convolution_convert_fusion.2.do_ref
  442.7 22.2 %attn_bwd.1 = (f32[2048,256]{1,0:T(8,128)S(1)}, f32[2048,256]{1,0:T(8,128)S(1)}, f32[2048,256]{1,0:T(8,128)S(1)}) custom-call(s32[8]{0:T(128)S(1)} %and_select_fusion.lo_ref, bf16[2048,256]{1,0:T(8,128)(2,1)S(1)} %copy-done.4, bf16[2048,256]{1,0:T(8,128)(2,1)S(1)} %copy-done.5, bf16[2048,256]{1,0:T(8,128)(2,1)S(1)} %copy-done.6, ...), custom_call_target="tpu_custom_call" | custom-call | flops 100000000 | bytes 4194304 | tf_op jit(solution)/shard_map/attn_bwd/pallas_call | solution.py:233
  467.6 2.3 fusion.19
  473.4 5.3 multiply_reduce_fusion.1
  485.3 3.6 convolution_convert_fusion.1
  490.7 10.4 %convolution_convert_fusion = bf16[2048,768]{1,0:T(8,128)(2,1)} fusion(bf16[2048,2048]{1,0:T(8,128)(2,1)} %get-tuple-element.79, bf16[2048,256]{1,0:T(8,128)(2,1)S(1)} %convert_element_type.67, bf16[2048,256]{1,0:T(8,128)(2,1)S(1)} %get-tuple-element.235, bf16[2048,256]{1,0:T(8,128)(2,1)S(1)} %get-tuple-element.236), kind=kOutput, calls=%fused_computation.1 | convolution fusion | flops 6453460992 | bytes 14680064 | tf_op jit(solution)/shard_map/dot_general | solution.py:32
  501.1 51.9 %moe_out.1 = f32[256,2048]{1,0:T(8,128)} custom-call(bf16[2048,2048]{1,0:T(8,128)(2,1)} %get-tuple-element.107.l_hbm, bf16[2048,2048]{1,0:T(8,128)(2,1)} %bitcast.85), custom_call_target="tpu_custom_call" | custom-call | flops 1000000000 | bytes 4194304 | tf_op jit(solution)/shard_map/moe_out/pallas_call | solution.py:1151
  554.8 46.8 %normed_back.1 = f32[256,2048]{1,0:T(8,128)} custom-call(bf16[2048,768]{1,0:T(8,128)(2,1)} %pad_maximum_fusion.1.l_hbm, bf16[2048,768]{1,0:T(8,128)(2,1)} %pad_maximum_fusion.2.r_hbm), custom_call_target="tpu_custom_call" | custom-call | flops 1000000000 | bytes 4194304 | tf_op jit(solution)/shard_map/normed_back/pallas_call | solution.py:1151
  601.7 2.4 fusion.7
  604.2 3.9 pad_maximum_fusion
  608.2 6.1 fusion.6
  614.3 12.8 %reduce-scatter.5.cloned.1.call-done = bf16[1,24,512,128]{3,2,1,0:T(8,128)(2,1)} async-done(((bf16[4,24,512,128]{3,2,1,0:T(8,128)(2,1)}), bf16[1,24,512,128]{3,2,1,0:T(8,128)(2,1)}) %reduce-scatter.5.cloned.1.call-update) | async-done | bytes 3145744 | tf_op jit(solution)/shard_map/reduce_scatter | solution.py:1398
  631.3 3.1 collective-permute-done.3
  636.1 2.6 collective-permute-done.4
  641.4 3.0 collective-permute-done.6
  644.4 3.4 collective-permute-start.7
  647.8 3.0 collective-permute-done.7
  662.2 3.1 fusion.16
  666.6 3.6 maximum_convert_fusion.2
  670.2 2.3 maximum_convert_fusion.1
  672.5 2.3 maximum_convert_fusion
  674.9 33.3 %reduce-scatter.11.cloned.1.call-done = bf16[512,1024]{1,0:T(8,128)(2,1)} async-done(((bf16[2048,1024]{1,0:T(8,128)(2,1)}), bf16[512,1024]{1,0:T(8,128)(2,1)}) %reduce-scatter.11.cloned.1.call-update) | async-done | bytes 1048592 | tf_op jit(solution)/shard_map/reduce_scatter | solution.py:1458
  708.1 2.4 convert_bitcast_fusion
  (178 shorter events, 53.5 us)
Async XLA Ops:
  7.2 317.5 %reduce-scatter.9.cloned.1.call-start = ((), (), s32[]{:S(2)}) async-start(), calls=%async_computation.7 | async-start | bytes 3932160 | tf_op jit(solution)/shard_map/reduce_scatter | solution.py:1398
  186.7 283.2 %reduce-scatter.7.cloned.1.call-start = ((), (), s32[]{:S(2)}) async-start(), calls=%async_computation.6 | async-start | bytes 11796480 | tf_op jit(solution)/shard_map/reduce_scatter | solution.py:1398
  239.5 387.6 %reduce-scatter.5.cloned.1.call-start = ((), (), s32[]{:S(2)}) async-start(), calls=%async_computation.5 | async-start | bytes 15728640 | tf_op jit(solution)/shard_map/reduce_scatter | solution.py:1398
  308.5 6.1 copy-start.8
  310.0 5.4 copy-start.9
  310.9 12.5 %all-to-all-start = ((f32[8,256,16]{1,2,0:T(8,128)}), f32[8,256,16]{1,2,0:T(8,128)S(1)}, u32[]{:S(2)}, u32[]{:S(2)}) async-start(f32[8,256,16]{1,2,0:T(8,128)} %copy.86), calls=%async_computation.3 | async-start | bytes 262144 | tf_op jit(solution)/shard_map/all_to_all | solution.py:1403
  314.6 393.6 %reduce-scatter.11.cloned.1.call-start = ((), (), s32[]{:S(2)}) async-start(), calls=%async_computation.8 | async-start | bytes 5242880 | tf_op jit(solution)/shard_map/reduce_scatter | solution.py:1458
  324.7 67.2 %copy-start.36 = (bf16[2048,16]{0,1:T(8,128)(2,1)S(1)}, bf16[2048,16]{0,1:T(8,128)(2,1)}, u32[]{:S(2)}) copy-start(bf16[2048,16]{0,1:T(8,128)(2,1)} %param.27) | copy-start | bytes 196612
  324.7 67.2 %copy-start.37 = (f32[2048]{0:T(1024)S(1)}, f32[2048]{0:T(1024)}, u32[]{:S(2)}) copy-start(f32[2048]{0:T(1024)} %param.26) | copy-start | bytes 24580
  397.7 39.0 %copy-start.33 = (bf16[256,2048]{1,0:T(8,128)(2,1)S(1)}, bf16[256,2048]{1,0:T(8,128)(2,1)}, u32[]{:S(2)}) copy-start(bf16[256,2048]{1,0:T(8,128)(2,1)} %wo_hbm.1) | copy-start | bytes 3145732
  436.7 6.0 copy-start.4
  436.7 6.0 copy-start.5
  436.7 6.0 copy-start.6
  436.7 6.0 copy-start.7
  470.6 14.7 %slice-start = ((s8[8388608]{0:T(1024)(128)(4,1)}), s8[4194304]{0:T(1024)(128)(4,1)S(1)}, s32[]{:S(2)}) async-start(s8[8388608]{0:T(1024)(128)(4,1)} %bitcast.86), calls=%async_computation.9 | async-start | bytes 8388608
  473.4 7.6 %copy-start.20 = (f32[2048,2]{1,0:T(8,128)S(1)}, f32[2048,2]{1,0:T(8,128)}, u32[]{:S(2)}) copy-start(f32[2048,2]{1,0:T(8,128)} %get-tuple-element.80) | copy-start | bytes 49156
  473.4 11.9 %slice-start.1 = ((s8[8388608]{0:T(1024)(128)(4,1)}), s8[4194304]{0:T(1024)(128)(4,1)S(1)}, s32[]{:S(2)}) async-start(s8[8388608]{0:T(1024)(128)(4,1)} %bitcast.86), calls=%async_computation.10 | async-start | bytes 8388608
  478.7 6.6 copy-start.41
  478.8 1.2 collective-permute-start
  480.0 3.8 collective-permute-start.1
  483.9 5.2 collective-permute-start.2
  554.8 46.9 %copy-start.13 = (bf16[256,2048]{1,0:T(8,128)(2,1)S(1)}, bf16[256,2048]{1,0:T(8,128)(2,1)}, u32[]{:S(2)}) copy-start(bf16[256,2048]{1,0:T(8,128)(2,1)} %x_hbm.1) | copy-start | bytes 3145732
  554.8 46.9 %copy-start.38 = (f32[2048]{0:T(1024)S(1)}, f32[2048]{0:T(1024)}, u32[]{:S(2)}) copy-start(f32[2048]{0:T(1024)} %param.23) | copy-start | bytes 24580
  629.8 4.7 collective-permute-start.3
  631.3 26.3 %copy-start.30 = (bf16[1,18,512,128]{3,2,1,0:T(8,128)(2,1)S(1)}, bf16[1,18,512,128]{3,2,1,0:T(8,128)(2,1)}, u32[]{:S(2)}) copy-start(bf16[1,18,512,128]{3,2,1,0:T(8,128)(2,1)} %reduce-scatter.7.cloned.1.call-done) | copy-start | bytes 7077892
  634.5 4.2 collective-permute-start.4
  638.7 1.3 collective-permute-start.5
  640.0 4.4 collective-permute-start.6
  644.4 6.3 collective-permute-start.7
  650.8 1.2 collective-permute-start.8
  652.0 4.2 collective-permute-start.9
  656.2 4.7 collective-permute-start.10
  (28 other events, 69.6 us)
Sparse Core Ops, SparseCore 0:
  186.8 61.4 reduce-scatter.8
  250.7 161.2 reduce-scatter.6
  414.4 212.6 reduce-scatter.4
  629.2 78.8 reduce-scatter.10
